TPU v7x, 32 devices: a whole 2x2x4 slice. The times are simulated.
32 devices in a mesh: row: 8 (over z, y), col: 4 (over x, core).
Axes of the slice: x: 2, y: 2, z: 4, core: 2. Of those that a mesh axis runs over, the one named last changes fastest.
Arguments:
- basis_values: bfloat16 [4, 4096, 4096], P(None, 'row', 'col'), may hold values from -6 to 6
- density: float32 [4096, 2560], P('row'), may hold values from -1 to 1, as said below
- screen: int32 [32, 32], P('row', 'col'), may hold values 0 or 1
- atom_of_block: int32 [32], P('col'), may hold values from 0 to 63
- atom_factor: float32 [64], replicated, may hold values from 0.5 to 2
- quad_weight: float32 [4096], P('col'), may hold values from 0.5 to 2
- core_density: float32 [4096], P('col'), may hold values from 0.3 to 1
Outputs:
- xc_matrix: float32 [4096, 1536], P(('row', 'col'))
Inputs may be any that keep to these rules, and one draw needn't show every extreme that they name: The density matrix is symmetric. Column block k of a row (k from 0 to 4, 512 columns each) holds the row's entries with the basis block k - 2 places further along the closed chain of 8 blocks; all other entries are zero.
All inputs are finite; a program needn't handle non-finite values. No bound on the sum of `screen` on one device may be relied on, other than what follows from the above.
Results may differ from a plain program's by a relative error of at most 0.0014.
Values may be sent and summed in bfloat16 or wider, within the bound.
No kernel may reach another device: no remote copies, remote signals or barrier semaphores. Data moves between devices by JAX's collectives and lax.ppermute only.
A program may use at most 64 MiB of HBM per device.

v0:
```python
import functools
import math

import jax
import jax.numpy as jnp
from jax import lax
from jax.experimental import pallas as pl
from jax.experimental.pallas import tpu as pltpu
from jax.sharding import PartitionSpec as P


BAND = 5
REACH = BAND // 2

KAPPA_VALUE = 0.804
MU_VALUE = 0.22
SLATER_COEF = 0.7386


WHOLE = pl.BlockSpec(memory_space=pltpu.VMEM)
SCALARS = pl.BlockSpec(memory_space=pltpu.SMEM)
ANYWHERE = pl.BlockSpec(memory_space=pl.ANY)
PARAMS = pltpu.CompilerParams(vmem_limit_bytes=20 << 20)
F32 = jnp.float32
BF16 = jnp.bfloat16


def from_ahead(block, distance):
    size = lax.axis_size("row")
    return lax.ppermute(block, "row", [((i + distance) % size, i) for i in range(size)])


def from_side(block, distance):
    size = lax.axis_size("row")
    route = [((i + (distance if i % 2 == 0 else -distance)) % size, i) for i in range(size)]
    return lax.ppermute(block, "row", route)


def swap(block, axis, bit):
    return lax.ppermute(block, axis, [(i, i ^ bit) for i in range(lax.axis_size(axis))])


def energy_density(density_in, squared_in, core):
    regular = jnp.sqrt(density_in * density_in + core * core)
    reduced = squared_in * regular ** (-8.0 / 3.0)
    enhance = 1.0 + KAPPA_VALUE - KAPPA_VALUE / (1.0 + MU_VALUE * reduced / KAPPA_VALUE)
    return -SLATER_COEF * regular ** (4.0 / 3.0) * enhance


def potentials(density_in, squared_in, core):

    def total_energy(first_arg, second_arg):
        return jnp.sum(energy_density(first_arg, second_arg, core))

    return jax.grad(total_energy, argnums=(0, 1))(density_in, squared_in)


def call(kernel, outs, in_specs, flops, bytes_accessed, out_specs=None, scratch=()):
    return pl.pallas_call(
        kernel,
        out_shape=outs,
        in_specs=in_specs,
        out_specs=jax.tree.map(lambda _: WHOLE, outs) if out_specs is None else out_specs,
        scratch_shapes=list(scratch),
        compiler_params=PARAMS,
        cost_estimate=pl.CostEstimate(
            flops=int(flops), bytes_accessed=int(bytes_accessed), transcendentals=0
        ),
    )


def dot(left, right):
    return jnp.dot(left, right, preferred_element_type=F32)


def dot_rows(left, right):
    return lax.dot_general(left, right, (((1,), (1,)), ((), ())), preferred_element_type=F32)


def position():
    col = lax.axis_index("col")
    return lax.axis_index("row") % 2, col % 2, (col // 2) % 2


def mask_kernel(sb, gb, screen_ref, basis_ref, own_ref, *rest):
    chunk_refs, (tile_ref, sems) = rest[:-2], rest[-2:]
    row_count, _ = own_ref.shape
    copies = []
    for row in range(row_count // sb):
        window = pl.ds(row * sb, sb)
        copy = pltpu.make_async_copy(basis_ref.at[0, window], tile_ref.at[window], sems.at[row])
        copy.start()
        copies.append(copy)
    for row, copy in enumerate(copies):
        rows = slice(row * sb, (row + 1) * sb)
        copy.wait()
        col = 0
        for chunk in chunk_refs:
            for start in range(0, chunk.shape[1], gb):
                keep = screen_ref[row, col // gb].astype(F32)
                tile = (tile_ref[rows, col : col + gb].astype(F32) * keep).astype(BF16)
                own_ref[rows, col : col + gb] = tile
                chunk[rows, start : start + gb] = tile
                col += gb


def split_kernel(density_ref, high_ref, low_ref):
    size = density_ref.shape[0]
    for column in range(BAND):
        strip = density_ref[:, column * size : (column + 1) * size]
        high = strip.astype(BF16)
        high_ref[column] = high
        low_ref[column] = (strip - high.astype(F32)).astype(BF16)


def both(high_ref, low_ref, column, block):
    return dot(high_ref[column], block) + dot(low_ref[column], block)


def early_kernel(high_ref, low_ref, own, beside, *rest):
    near, totals = rest[: len(rest) // 2], rest[len(rest) // 2 :]
    sign = 1 - 2 * position()[0]
    start = 0
    for block, total in zip(near, totals):
        cols = slice(start, start + block.shape[1])
        total[...] = (
            both(high_ref, low_ref, REACH, own[:, cols])
            + both(high_ref, low_ref, REACH + sign, beside[:, cols])
            + both(high_ref, low_ref, REACH + 2 * sign, block[...])
        )
        start += block.shape[1]


def sums_kernel(sb, gb, first, screen_ref, high_ref, low_ref, partial_ref, far, across, basis_ref,
                sums_ref, total_ref):
    sign = 1 - 2 * position()[0]
    total_ref[...] = (
        partial_ref[...]
        + both(high_ref, low_ref, REACH - 2 * sign, far[...])
        + both(high_ref, low_ref, REACH - sign, across[...])
    )
    components, row_count, width = basis_ref.shape[0], far.shape[0], far.shape[1]
    for part in range(width // gb):
        cols = slice(part * gb, (part + 1) * gb)
        source = slice((first + part) * gb, (first + part + 1) * gb)
        found = [jnp.zeros((1, gb), F32) for _ in range(components)]
        for row in range(row_count // sb):
            rows = slice(row * sb, (row + 1) * sb)
            keep = screen_ref[row, first + part].astype(F32)
            applied = total_ref[rows, cols]
            for c in range(components):
                product = basis_ref[c, rows, source].astype(F32) * applied
                found[c] += keep * jnp.sum(product, axis=0, keepdims=True)
        for c in range(components):
            sums_ref[c : c + 1, cols] = found[c]


def half_kernel(sb, gb, screen_ref, basis_ref, parts_ref, half_ref):
    components, row_count, points = basis_ref.shape
    for part in range(points // gb):
        cols = slice(part * gb, (part + 1) * gb)
        for row in range(row_count // sb):
            rows = slice(row * sb, (row + 1) * sb)
            keep = screen_ref[row, part].astype(F32)
            total = (parts_ref[0:1, cols] * keep) * basis_ref[0, rows, cols].astype(F32)
            for c in range(1, components):
                total += (parts_ref[c : c + 1, cols] * keep) * basis_ref[c, rows, cols].astype(F32)
            half_ref[rows, cols] = total.astype(BF16)


def rows_of(ref, cols, side, share, count):
    blocks = []
    for step in range(count):
        window = pl.ds(pl.multiple_of((2 * step + side) * share, share), share)
        blocks.append(ref[window, cols])
    return jnp.concatenate(blocks, axis=0) if count > 1 else blocks[0]


def pieces(blocks):
    start = 0
    for block in blocks:
        width = block.shape[1]
        yield slice(start, start + width), block
        start += width


def mirrored_product(half_ref, one, two, side, share, count):
    total = 0
    for blocks in zip(pieces(two), pieces(one) if len(one) > 1 else pieces(two)):
        (cols, second), (_, first) = blocks
        if len(one) > 1:
            first_rows = rows_of(first, slice(None), side, share, count)
        else:
            first_rows = rows_of(one[0], cols, side, share, count)
        left = jnp.concatenate(
            [first_rows, rows_of(second, slice(None), side, share, count)], axis=0
        )
        total += dot_rows(left, half_ref[:, cols])
    return total.reshape(REACH, count, share, half_ref.shape[0])


def central_product(half_ref, own, side, share, count):
    cols = slice(None)
    total = dot_rows(rows_of(own, cols, side, share, count), half_ref[...])
    total += dot_rows(rows_of(half_ref, cols, side, share, count), own[...])
    return total.reshape(count, share, half_ref.shape[0])


def direct_product(half_ref, blocks, side, share, count):
    total = 0
    for cols, block in pieces(blocks):
        total += dot_rows(rows_of(half_ref, cols, side, share, count), block[...])
    return total.reshape(count, share, half_ref.shape[0])


def neighbours(refs, chunks):
    beside, near = refs[:1], refs[1 : 1 + chunks]
    far, across = refs[1 + chunks : 1 + 2 * chunks], refs[1 + 2 * chunks : 1 + 3 * chunks]
    return (beside, near), (across, far)


def on_side(refs, chunks, ahead, run):
    first, second = neighbours(refs, chunks)
    odd = position()[0]

    @pl.when(odd == (0 if ahead else 1))
    def _():
        run(*first)

    @pl.when(odd == (1 if ahead else 0))
    def _():
        run(*second)


def deposit(total, side, keep_ref, send_ref):
    for step in range(total.shape[-3] // 2):
        low, high = total[..., 2 * step, :, :], total[..., 2 * step + 1, :, :]
        keep_ref[..., step, :, :] = jnp.where(side == 0, low, high)
        send_ref[..., step, :, :] = jnp.where(side == 0, high, low).astype(send_ref.dtype)


def mirrored_other_kernel(share, count, chunks, half_ref, *refs):
    refs, out = refs[:-1], refs[-1]
    side = 1 - position()[1]

    def run(one, two):
        out[...] = mirrored_product(half_ref, one, two, side, share, count)

    on_side(refs, chunks, False, run)


def mirrored_own_kernel(share, count, chunks, half_ref, found_ref, *refs):
    refs, keep_ref, send_ref = refs[:-2], refs[-2], refs[-1]
    _, core, side = position()

    def run(one, two):
        total = mirrored_product(half_ref, one, two, core, share, count)
        deposit(total + found_ref[...], side, keep_ref, send_ref)

    on_side(refs, chunks, False, run)


def direct_other_kernel(share, count, chunks, half_ref, own, earlier_ref, *refs):
    refs, out = refs[:-1], refs[-1]
    side = 1 - position()[1]
    out[0] = central_product(half_ref, own, side, share, count)

    def run(one, two):
        out[1] = direct_product(half_ref, one, side, share, count)
        out[2] = direct_product(half_ref, two, side, share, count)

    on_side(refs, chunks, True, run)


def direct_own_kernel(share, count, chunks, half_ref, own, earlier_ref, found_ref, *refs):
    refs, keep_ref, send_ref = refs[:-2], refs[-2], refs[-1]
    _, core, side = position()
    size = half_ref.shape[0]
    spare = send_ref.shape[-1] - 3 * size

    def place(k, total):
        for step in range(count // 2):
            low, high = total[2 * step], total[2 * step + 1]
            keep_ref[k, step] = jnp.where(side == 0, low, high)
            send = jnp.where(side == 0, high, low)
            rounded = send.astype(BF16)
            send_ref[step, :, k * size : (k + 1) * size] = rounded
            if k == 0:
                for block in range(size // spare):
                    quarter = (2 * step + 1 - side) * 2 + core

                    @pl.when((quarter * share) // spare == block)
                    def _():
                        cols = slice(block * spare, (block + 1) * spare)
                        rest = send[:, cols] - rounded[:, cols].astype(F32)
                        send_ref[step, :, 3 * size :] = rest.astype(BF16)

    place(0, central_product(half_ref, own, core, share, count) + found_ref[0])

    def run(one, two):
        place(1, direct_product(half_ref, one, core, share, count) + found_ref[1])
        place(2, direct_product(half_ref, two, core, share, count) + found_ref[2])

    on_side(refs, chunks, True, run)


def joined_kernel(share, keep_ref, found_ref, out_ref):
    _, core, side = position()
    size = keep_ref.shape[-1]
    spare = found_ref.shape[-1] - 3 * size
    for step in range(found_ref.shape[0]):
        for k in range(3):
            part = found_ref[step, :, k * size : (k + 1) * size].astype(F32)
            out_ref[step, :, k * size : (k + 1) * size] = keep_ref[k, step] + part
        quarter = (2 * step + side) * 2 + core
        for block in range(size // spare):

            @pl.when((quarter * share) // spare == block)
            def _():
                cols = slice(block * spare, (block + 1) * spare)
                out_ref[step, :, cols] += found_ref[step, :, 3 * size :].astype(F32)


def final_kernel(share, keep_ref, found_ref, *refs):
    mirrored, out_ref = refs[:-1], refs[-1]
    joined_kernel(share, keep_ref, found_ref, out_ref)
    size = keep_ref.shape[-1]
    for k, block in enumerate(mirrored):
        cols = slice((k + 1) * size, (k + 2) * size)
        out_ref[0, :, cols] += block[...].astype(F32)


def shape(dims, kind=F32):
    return jax.ShapeDtypeStruct(dims, kind)


def body(basis_values, density, screen, atom_of_block, atom_factor, quad_weight, core_density):
    rows, cols = lax.axis_size("row"), lax.axis_size("col")
    col = lax.axis_index("col")
    components, row_count, points = basis_values.shape
    sb, gb = row_count // screen.shape[0], points // screen.shape[1]
    last = max(1, screen.shape[1] // 4) * gb
    widths = (points - last, last)
    chunks = len(widths)
    share, count = row_count // cols, cols // 2
    square = 2 * row_count * row_count

    own, *mine = call(
        functools.partial(mask_kernel, sb, gb),
        [shape((row_count, width), BF16) for width in (points, *widths)],
        [SCALARS, pl.BlockSpec(memory_space=pltpu.HBM)], row_count * points, 6 * row_count * points,
        scratch=[
            pltpu.VMEM((row_count, points), BF16),
            pltpu.SemaphoreType.DMA((screen.shape[0],)),
        ],
    )(screen, basis_values)
    near, far, across = [], [], []
    for chunk, block in enumerate(mine):
        near.append(from_side(block, 2))
        far.append(from_side(block, -2))
        across.append(swap(near[chunk], "row", 1))
    beside = swap(own, "row", 1)

    high, low = call(
        split_kernel, [shape((BAND, row_count, row_count), BF16)] * 2, [WHOLE],
        density.size * 4, density.size * 8,
    )(density)
    partial = call(
        early_kernel, [shape((row_count, width)) for width in widths], [WHOLE] * (4 + chunks),
        6 * square * points, 10 * square,
    )(high, low, own, beside, *near)
    sums, first = [], 0
    for chunk, width in enumerate(widths):
        sums.append(
            call(
                functools.partial(sums_kernel, sb, gb, first), shape((components, width)),
                [SCALARS] + [WHOLE] * 6, 4 * square * width, 6 * square,
                scratch=[pltpu.VMEM((row_count, width), F32)],
            )(screen, high, low, partial[chunk], far[chunk], across[chunk], basis_values)
        )
        first += width // gb
    summed = jnp.concatenate(sums, axis=1)
    bit = 1
    while bit < rows:
        summed = summed + swap(summed, "row", bit)
        bit *= 2

    point_density = summed[0]
    gradient = 2.0 * summed[1:]
    squared = jnp.sum(gradient * gradient, axis=0)
    atoms = atom_factor.shape[0]
    chooser = (atom_of_block[:, None] == jnp.arange(atoms, dtype=jnp.int32)[None, :]).astype(F32)
    block_factor = jnp.dot(chooser, atom_factor, precision=lax.Precision.HIGHEST)
    group_size = points // atom_of_block.shape[0]
    weights = (quad_weight.reshape(-1, group_size) * block_factor[:, None]).reshape(
        points
    ) / math.sqrt(points * cols)
    density_pot, gradient_pot = potentials(point_density, squared, core_density)
    scalar_part = 0.5 * weights * density_pot
    vector_part = 2.0 * weights * gradient_pot * gradient
    parts = jnp.concatenate([scalar_part[None], vector_part], axis=0)
    half = call(
        functools.partial(half_kernel, sb, gb), shape((row_count, points), BF16),
        [SCALARS, WHOLE, WHOLE], 8 * basis_values.size, 2 * basis_values.size,
    )(screen, basis_values, parts)

    beyond = (beside, *near, *far, *across)
    product = 2 * row_count * points * share * count
    mirrored_other = call(
        functools.partial(mirrored_other_kernel, share, count, chunks),
        shape((REACH, count, share, row_count)), [WHOLE] * (1 + len(beyond)),
        product * 2, 4 * row_count * points,
    )(half, *beyond)
    mirrored_found = swap(mirrored_other, "col", 1)
    direct_other = call(
        functools.partial(direct_other_kernel, share, count, chunks),
        shape((REACH + 1, count, share, row_count)),
        [WHOLE] * 2 + [ANYWHERE] + [WHOLE] * len(beyond),
        product * 4, 6 * row_count * points,
    )(half, own, mirrored_other, *beyond)
    direct_found = swap(direct_other, "col", 1)
    kept = count // 2
    mirrored_keep, mirrored_send = call(
        functools.partial(mirrored_own_kernel, share, count, chunks),
        [
            shape((REACH, kept, share, row_count)),
            shape((REACH, kept, share, row_count), BF16),
        ],
        [WHOLE] * (2 + len(beyond)), product * 2, 6 * row_count * points,
    )(half, mirrored_found, *beyond)
    spare = max(share, 128)
    direct_keep, direct_send = call(
        functools.partial(direct_own_kernel, share, count, chunks),
        [
            shape((REACH + 1, kept, share, row_count)),
            shape((kept, share, 3 * row_count + spare), BF16),
        ],
        [WHOLE] * 2 + [ANYWHERE] + [WHOLE] * (1 + len(beyond)), product * 4, 8 * row_count * points,
    )(half, own, mirrored_keep, direct_found, *beyond)

    def scatter(total, axis):
        bit = 4
        while bit < cols:
            paired = total.reshape(*total.shape[:axis], -1, 2, *total.shape[axis + 1 :])
            mine = (col // bit) % 2
            keep = lax.dynamic_index_in_dim(paired, mine, axis + 1, keepdims=False)
            send = lax.dynamic_index_in_dim(paired, 1 - mine, axis + 1, keepdims=False)
            total = keep + swap(send, "col", bit)
            bit *= 2
        return total

    found = swap(mirrored_send, "col", 2)
    mirrored = mirrored_keep + found.astype(F32)
    mirrored = scatter(mirrored, 1).astype(BF16)
    mirrored = [from_ahead(mirrored[k, 0], k + 1) for k in range(REACH)]
    found = swap(direct_send, "col", 2)
    if kept > 1:
        total = call(
            functools.partial(joined_kernel, share), shape((kept, share, 3 * row_count)),
            [WHOLE] * 2, direct_keep.size, 8 * direct_keep.size,
        )(direct_keep, found)
        total = scatter(total, 0)[0]
        zero = jnp.zeros((share, row_count), BF16)
        return total + jnp.concatenate([zero, *mirrored], axis=1).astype(F32)
    return call(
        functools.partial(final_kernel, share), shape((1, share, 3 * row_count)),
        [WHOLE] * (2 + REACH), direct_keep.size, 10 * direct_keep.size,
    )(direct_keep, found, *mirrored)[0]


def solution(mesh):
    in_specs = (
        P(None, "row", "col"),
        P("row", None),
        P("row", "col"),
        P("col"),
        P(),
        P("col"),
        P("col"),
    )
    out_specs = P(("row", "col"), None)

    return jax.shard_map(body, mesh=mesh, in_specs=in_specs, out_specs=out_specs, check_vma=False)
```

profile of v0, /device:TPU:0, one launch (start us, length us, event | category | flops | bytes accessed | tf_op | source)
XLA Modules:
  0.0 105.6 jit_solution(18361904118080517647)
XLA Ops:
  0.0 2.2 %copy-done.1 = bf16[4,512,1024]{2,1,0:T(8,128)(2,1)S(1)} copy-done((bf16[4,512,1024]{2,1,0:T(8,128)(2,1)S(1)}, bf16[4,512,1024]{2,1,0:T(8,128)(2,1)}, u32[]{:S(2)}) %copy-start.1) | copy-done | bytes 4194328
  4.0 5.1 %collective-permute-start.1 = (bf16[512,768]{1,0:T(8,128)(2,1)S(1)}, bf16[512,768]{1,0:T(8,128)(2,1)S(1)}, u32[]{:S(2)}, u32[]{:S(2)}) collective-permute-start(bf16[512,768]{1,0:T(8,128)(2,1)S(1)} %get-tuple-element.19), channel_id=1, source_target_pairs={{8,0},{28,4},{16,8},{4,12},{24,16},{12,20},{0,24},{20,28},{9,1},{2... | collective-permute-start | bytes 2359304 | tf_op jit(solution)/shard_map/ppermute | solution.py:36
  9.1 1.1 %collective-permute-start.3 = (bf16[512,768]{1,0:T(8,128)(2,1)S(1)}, bf16[512,768]{1,0:T(8,128)(2,1)S(1)}, u32[]{:S(2)}, u32[]{:S(2)}) collective-permute-start(bf16[512,768]{1,0:T(8,128)(2,1)S(1)} %get-tuple-element.19), channel_id=1, source_target_pairs={{24,0},{12,4},{0,8},{20,12},{8,16},{28,20},{16,24},{4,28},{25,1},{... | collective-permute-start | bytes 2359304 | tf_op jit(solution)/shard_map/ppermute | solution.py:36
  10.2 16.9 %collective-permute-done.1.rest_0_.refs_1_ = bf16[512,768]{1,0:T(8,128)(2,1)S(1)} collective-permute-done((bf16[512,768]{1,0:T(8,128)(2,1)S(1)}, bf16[512,768]{1,0:T(8,128)(2,1)S(1)}, u32[]{:S(2)}, u32[]{:S(2)}) %collective-permute-start.1) | collective-permute-done | bytes 786464 | tf_op jit(solution)/shard_map/ppermute | solution.py:36
  27.1 2.2 %collective-permute-start.4 = (bf16[512,768]{1,0:T(8,128)(2,1)S(1)}, bf16[512,768]{1,0:T(8,128)(2,1)S(1)}, u32[]{:S(2)}, u32[]{:S(2)}) collective-permute-start(bf16[512,768]{1,0:T(8,128)(2,1)S(1)} %collective-permute-done.1.rest_0_.refs_1_), channel_id=1, source_target_pairs={{0,4},{4,0},{8,12},{12,8},{16,20},{20,16},{24,28},{28,24},{1,5},{5... | collective-permute-start | bytes 2359304 | tf_op jit(solution)/shard_map/ppermute | solution.py:40
  29.3 16.7 %collective-permute-start.2 = (bf16[512,256]{1,0:T(8,128)(2,1)S(1)}, bf16[512,256]{1,0:T(8,128)(2,1)S(1)}, u32[]{:S(2)}, u32[]{:S(2)}) collective-permute-start(bf16[512,256]{1,0:T(8,128)(2,1)S(1)} %get-tuple-element.20), channel_id=1, source_target_pairs={{8,0},{28,4},{16,8},{4,12},{24,16},{12,20},{0,24},{20,28},{9,1},{2... | collective-permute-start | bytes 786440 | tf_op jit(solution)/shard_map/ppermute | solution.py:36
  46.0 2.5 %copy-done.3 = f32[512,2560]{1,0:T(8,128)S(1)} copy-done((f32[512,2560]{1,0:T(8,128)S(1)}, f32[512,2560]{1,0:T(8,128)}, u32[]{:S(2)}) %copy-start.3) | copy-done | bytes 5242904
  49.2 2.9 %collective-permute-done.2.rest_1_.refs_2_ = bf16[512,256]{1,0:T(8,128)(2,1)S(1)} collective-permute-done((bf16[512,256]{1,0:T(8,128)(2,1)S(1)}, bf16[512,256]{1,0:T(8,128)(2,1)S(1)}, u32[]{:S(2)}, u32[]{:S(2)}) %collective-permute-start.2) | collective-permute-done | bytes 262176 | tf_op jit(solution)/shard_map/ppermute | solution.py:36
  53.2 3.4 %shard_map.75 = (f32[512,768]{1,0:T(8,128)S(1)}, f32[512,256]{1,0:T(8,128)S(1)}) custom-call(bf16[5,512,512]{2,1,0:T(8,128)(2,1)S(1)} %get-tuple-element.16.high_ref, bf16[5,512,512]{2,1,0:T(8,128)(2,1)S(1)} %get-tuple-element.17.low_ref, bf16[512,1024]{1,0:T(8,128)(2,1)S(1)} %get-tuple-element.18.own, ...), custom_call_target="tpu_custom_call" | custom-call | flops 3221225472 | bytes 5242880 | tf_op jit(solution)/shard_map/pallas_call | solution.py:368
  56.6 3.8 %collective-permute-done.6.across.refs_6_ = bf16[512,256]{1,0:T(8,128)(2,1)S(1)} collective-permute-done((bf16[512,256]{1,0:T(8,128)(2,1)S(1)}, bf16[512,256]{1,0:T(8,128)(2,1)S(1)}, u32[]{:S(2)}, u32[]{:S(2)}) %collective-permute-start.6) | collective-permute-done | bytes 262176 | tf_op jit(solution)/shard_map/ppermute | solution.py:40
  60.4 1.4 %shard_map.77 = f32[4,256]{1,0:T(4,128)S(1)} custom-call(s32[4,8]{1,0:T(4,128)S(1)} %copy-done.5, bf16[5,512,512]{2,1,0:T(8,128)(2,1)S(1)} %get-tuple-element.16.high_ref, bf16[5,512,512]{2,1,0:T(8,128)(2,1)S(1)} %get-tuple-element.17.low_ref, f32[512,256]{1,0:T(8,128)S(1)} %get-tuple-element.22.partial_ref, ...), custom_call_target="tpu_custom_call" | custom-call | flops 536870912 | bytes 3145728 | tf_op jit(solution)/shard_map/pallas_call | solution.py:375
  61.9 2.9 %shard_map.76 = f32[4,768]{1,0:T(4,128)S(1)} custom-call(s32[4,8]{1,0:T(4,128)S(1)} %copy-done.5, bf16[5,512,512]{2,1,0:T(8,128)(2,1)S(1)} %get-tuple-element.16.high_ref, bf16[5,512,512]{2,1,0:T(8,128)(2,1)S(1)} %get-tuple-element.17.low_ref, f32[512,768]{1,0:T(8,128)S(1)} %get-tuple-element.21.partial_ref, ...), custom_call_target="tpu_custom_call" | custom-call | flops 1610612736 | bytes 3145728 | tf_op jit(solution)/shard_map/pallas_call | solution.py:375
  65.1 3.5 %collective-permute-done.7 = f32[4,1024]{1,0:T(4,128)S(1)} collective-permute-done((f32[4,1024]{1,0:T(4,128)S(1)}, f32[4,1024]{1,0:T(4,128)S(1)}, u32[]{:S(2)}, u32[]{:S(2)}) %collective-permute-start.7) | collective-permute-done | bytes 16416 | tf_op jit(solution)/shard_map/ppermute | solution.py:40
  68.7 3.7 %collective-permute-done.8 = f32[4,1024]{1,0:T(4,128)S(1)} collective-permute-done((f32[4,1024]{1,0:T(4,128)S(1)}, f32[4,1024]{1,0:T(4,128)S(1)}, u32[]{:S(2)}, u32[]{:S(2)}) %collective-permute-start.8) | collective-permute-done | bytes 16416 | tf_op jit(solution)/shard_map/ppermute | solution.py:40
  73.1 3.9 %collective-permute-done.9 = f32[4,1024]{1,0:T(4,128)S(1)} collective-permute-done((f32[4,1024]{1,0:T(4,128)S(1)}, f32[4,1024]{1,0:T(4,128)S(1)}, u32[]{:S(2)}, u32[]{:S(2)}) %collective-permute-start.9) | collective-permute-done | bytes 16416 | tf_op jit(solution)/shard_map/ppermute | solution.py:40
  77.2 1.6 %shard_map.78.half_ref = bf16[512,1024]{1,0:T(8,128)(2,1)S(1)} custom-call(s32[4,8]{1,0:T(4,128)S(1)} %copy-done.5, bf16[4,512,1024]{2,1,0:T(8,128)(2,1)S(1)} %copy-done.2, f32[4,1024]{1,0:T(4,128)S(1)} %pad_maximum_fusion.1.parts_ref), custom_call_target="tpu_custom_call" | custom-call | flops 16777216 | bytes 4194304 | tf_op jit(solution)/shard_map/pallas_call | solution.py:402
  79.6 1.5 %shard_map.81 = f32[3,2,128,512]{3,2,1,0:T(8,128)S(1)} custom-call(bf16[512,1024]{1,0:T(8,128)(2,1)S(1)} %shard_map.78.half_ref, bf16[512,1024]{1,0:T(8,128)(2,1)S(1)} %get-tuple-element.18.own, f32[2,2,128,512]{3,2,1,0:T(8,128)S(1)} %shard_map.79.earlier_ref, bf16[512,1024]{1,0:T(8,128)(2,1)S(1)} %collective-permute-done.beside.refs_0_, ...), custom_call_target="tpu_custom_call" | custom-call | flops 1073741824 | bytes 3145728 | tf_op jit(solution)/shard_map/pallas_call | solution.py:415
  81.6 4.4 %collective-permute-done.10.found_ref = f32[2,2,128,512]{3,2,1,0:T(8,128)S(1)} collective-permute-done((f32[2,2,128,512]{3,2,1,0:T(8,128)S(1)}, f32[2,2,128,512]{3,2,1,0:T(8,128)S(1)}, u32[]{:S(2)}, u32[]{:S(2)}) %collective-permute-start.10) | collective-permute-done | bytes 1048608 | tf_op jit(solution)/shard_map/ppermute | solution.py:40
  86.8 1.6 %collective-permute-start.13 = (bf16[2,1,128,512]{3,2,1,0:T(8,128)(2,1)S(1)}, bf16[2,1,128,512]{3,2,1,0:T(8,128)(2,1)S(1)}, u32[]{:S(2)}, u32[]{:S(2)}) collective-permute-start(bf16[2,1,128,512]{3,2,1,0:T(8,128)(2,1)S(1)} %get-tuple-element.26), channel_id=1, source_target_pairs={{0,2},{1,3},{2,0},{3,1},{4,6},{5,7},{6,4},{7,5},{8,10},{9,11},{10,... | collective-permute-start | bytes 786440 | tf_op jit(solution)/shard_map/ppermute | solution.py:40
  88.3 1.6 %shard_map.82 = (f32[3,1,128,512]{3,2,1,0:T(8,128)S(1)}, bf16[1,128,1664]{2,1,0:T(8,128)(2,1)S(1)}) custom-call(bf16[512,1024]{1,0:T(8,128)(2,1)S(1)} %shard_map.78.half_ref, bf16[512,1024]{1,0:T(8,128)(2,1)S(1)} %get-tuple-element.18.own, f32[2,1,128,512]{3,2,1,0:T(8,128)S(1)} %get-tuple-element.23.earlier_ref, ...), custom_call_target="tpu_custom_call" | custom-call | flops 1073741824 | bytes 4194304 | tf_op jit(solution)/shard_map/pallas_call | solution.py:432
  90.5 5.5 %collective-permute-done.13 = bf16[2,1,128,512]{3,2,1,0:T(8,128)(2,1)S(1)} collective-permute-done((bf16[2,1,128,512]{3,2,1,0:T(8,128)(2,1)S(1)}, bf16[2,1,128,512]{3,2,1,0:T(8,128)(2,1)S(1)}, u32[]{:S(2)}, u32[]{:S(2)}) %collective-permute-start.13) | collective-permute-done | bytes 262176 | tf_op jit(solution)/shard_map/ppermute | solution.py:40
  96.1 3.5 %collective-permute-start.14 = (bf16[128,512]{1,0:T(8,128)(2,1)S(1)}, bf16[128,512]{1,0:T(8,128)(2,1)S(1)}, u32[]{:S(2)}, u32[]{:S(2)}) collective-permute-start(bf16[128,512]{1,0:T(8,128)(2,1)S(1)} %get-tuple-element.28), channel_id=1, source_target_pairs={{4,0},{8,4},{12,8},{16,12},{20,16},{24,20},{28,24},{0,28},{5,1},{9... | collective-permute-start | bytes 393224 | tf_op jit(solution)/shard_map/ppermute | solution.py:30
  99.6 2.8 %collective-permute-done.14.refs_0_ = bf16[128,512]{1,0:T(8,128)(2,1)S(1)} collective-permute-done((bf16[128,512]{1,0:T(8,128)(2,1)S(1)}, bf16[128,512]{1,0:T(8,128)(2,1)S(1)}, u32[]{:S(2)}, u32[]{:S(2)}) %collective-permute-start.14) | collective-permute-done | bytes 131104 | tf_op jit(solution)/shard_map/ppermute | solution.py:30
  102.4 2.2 %collective-permute-done.15.refs_1_ = bf16[128,512]{1,0:T(8,128)(2,1)S(1)} collective-permute-done((bf16[128,512]{1,0:T(8,128)(2,1)S(1)}, bf16[128,512]{1,0:T(8,128)(2,1)S(1)}, u32[]{:S(2)}, u32[]{:S(2)}) %collective-permute-start.15) | collective-permute-done | bytes 131104 | tf_op jit(solution)/shard_map/ppermute | solution.py:30
  (49 shorter events, 8.6 us)
Async XLA Ops:
  0.0 72.9 %copy-start = (f32[64]{0:T(128)S(1)}, f32[64]{0:T(128)}, u32[]{:S(2)}) copy-start(f32[64]{0:T(128)} %param.11) | copy-start | bytes 772
  0.0 2.2 %copy-start.1 = (bf16[4,512,1024]{2,1,0:T(8,128)(2,1)S(1)}, bf16[4,512,1024]{2,1,0:T(8,128)(2,1)}, u32[]{:S(2)}) copy-start(bf16[4,512,1024]{2,1,0:T(8,128)(2,1)} %basis_ref.7) | copy-start | bytes 12582916
  4.0 23.1 %collective-permute-start.1 = (bf16[512,768]{1,0:T(8,128)(2,1)S(1)}, bf16[512,768]{1,0:T(8,128)(2,1)S(1)}, u32[]{:S(2)}, u32[]{:S(2)}) collective-permute-start(bf16[512,768]{1,0:T(8,128)(2,1)S(1)} %get-tuple-element.19), channel_id=1, source_target_pairs={{8,0},{28,4},{16,8},{4,12},{24,16},{12,20},{0,24},{20,28},{9,1},{2... | collective-permute-start | bytes 2359304 | tf_op jit(solution)/shard_map/ppermute | solution.py:36
  9.1 44.1 %collective-permute-start = (bf16[512,1024]{1,0:T(8,128)(2,1)S(1)}, bf16[512,1024]{1,0:T(8,128)(2,1)S(1)}, u32[]{:S(2)}, u32[]{:S(2)}) collective-permute-start(bf16[512,1024]{1,0:T(8,128)(2,1)S(1)} %get-tuple-element.18.own), channel_id=1, source_target_pairs={{0,4},{4,0},{8,12},{12,8},{16,20},{20,16},{24,28},{28,24},{1,5},{5... | collective-permute-start | bytes 3145736 | tf_op jit(solution)/shard_map/ppermute | solution.py:40
  9.1 52.7 %collective-permute-start.3 = (bf16[512,768]{1,0:T(8,128)(2,1)S(1)}, bf16[512,768]{1,0:T(8,128)(2,1)S(1)}, u32[]{:S(2)}, u32[]{:S(2)}) collective-permute-start(bf16[512,768]{1,0:T(8,128)(2,1)S(1)} %get-tuple-element.19), channel_id=1, source_target_pairs={{24,0},{12,4},{0,8},{20,12},{8,16},{28,20},{16,24},{4,28},{25,1},{... | collective-permute-start | bytes 2359304 | tf_op jit(solution)/shard_map/ppermute | solution.py:36
  27.1 34.8 %collective-permute-start.4 = (bf16[512,768]{1,0:T(8,128)(2,1)S(1)}, bf16[512,768]{1,0:T(8,128)(2,1)S(1)}, u32[]{:S(2)}, u32[]{:S(2)}) collective-permute-start(bf16[512,768]{1,0:T(8,128)(2,1)S(1)} %collective-permute-done.1.rest_0_.refs_1_), channel_id=1, source_target_pairs={{0,4},{4,0},{8,12},{12,8},{16,20},{20,16},{24,28},{28,24},{1,5},{5... | collective-permute-start | bytes 2359304 | tf_op jit(solution)/shard_map/ppermute | solution.py:40
  29.3 22.9 %collective-permute-start.2 = (bf16[512,256]{1,0:T(8,128)(2,1)S(1)}, bf16[512,256]{1,0:T(8,128)(2,1)S(1)}, u32[]{:S(2)}, u32[]{:S(2)}) collective-permute-start(bf16[512,256]{1,0:T(8,128)(2,1)S(1)} %get-tuple-element.20), channel_id=1, source_target_pairs={{8,0},{28,4},{16,8},{4,12},{24,16},{12,20},{0,24},{20,28},{9,1},{2... | collective-permute-start | bytes 786440 | tf_op jit(solution)/shard_map/ppermute | solution.py:36
  46.0 10.6 %collective-permute-start.5 = (bf16[512,256]{1,0:T(8,128)(2,1)S(1)}, bf16[512,256]{1,0:T(8,128)(2,1)S(1)}, u32[]{:S(2)}, u32[]{:S(2)}) collective-permute-start(bf16[512,256]{1,0:T(8,128)(2,1)S(1)} %get-tuple-element.20), channel_id=1, source_target_pairs={{24,0},{12,4},{0,8},{20,12},{8,16},{28,20},{16,24},{4,28},{25,1},{... | collective-permute-start | bytes 786440 | tf_op jit(solution)/shard_map/ppermute | solution.py:36
  46.0 2.5 %copy-start.3 = (f32[512,2560]{1,0:T(8,128)S(1)}, f32[512,2560]{1,0:T(8,128)}, u32[]{:S(2)}) copy-start(f32[512,2560]{1,0:T(8,128)} %density_ref.1) | copy-start | bytes 15728644
  52.2 8.2 %collective-permute-start.6 = (bf16[512,256]{1,0:T(8,128)(2,1)S(1)}, bf16[512,256]{1,0:T(8,128)(2,1)S(1)}, u32[]{:S(2)}, u32[]{:S(2)}) collective-permute-start(bf16[512,256]{1,0:T(8,128)(2,1)S(1)} %collective-permute-done.2.rest_1_.refs_2_), channel_id=1, source_target_pairs={{0,4},{4,0},{8,12},{12,8},{16,20},{20,16},{24,28},{28,24},{1,5},{5... | collective-permute-start | bytes 786440 | tf_op jit(solution)/shard_map/ppermute | solution.py:40
  53.2 7.2 %copy-start.2 = (bf16[4,512,1024]{2,1,0:T(8,128)(2,1)S(1)}, bf16[4,512,1024]{2,1,0:T(8,128)(2,1)}, u32[]{:S(2)}) copy-start(bf16[4,512,1024]{2,1,0:T(8,128)(2,1)} %basis_ref.7) | copy-start | bytes 12582916
  53.2 7.2 %copy-start.5 = (s32[4,8]{1,0:T(4,128)S(1)}, s32[4,8]{1,0:T(4,128)}, u32[]{:S(2)}) copy-start(s32[4,8]{1,0:T(4,128)} %screen_ref.7) | copy-start | bytes 388
  61.8 11.1 %copy-start.8 = (s32[8]{0:T(128)S(1)}, s32[8]{0:T(128)}, u32[]{:S(2)}) copy-start(s32[8]{0:T(128)} %param.10) | copy-start | bytes 100
  61.8 15.2 %copy-start.6 = (f32[1024]{0:T(1024)S(1)}, f32[1024]{0:T(1024)}, u32[]{:S(2)}) copy-start(f32[1024]{0:T(1024)} %param.12) | copy-start | bytes 12292
  61.9 15.2 %copy-start.7 = (f32[1024]{0:T(1024)S(1)}, f32[1024]{0:T(1024)}, u32[]{:S(2)}) copy-start(f32[1024]{0:T(1024)} %param.13) | copy-start | bytes 12292
  64.8 3.8 %collective-permute-start.7 = (f32[4,1024]{1,0:T(4,128)S(1)}, f32[4,1024]{1,0:T(4,128)S(1)}, u32[]{:S(2)}, u32[]{:S(2)}) collective-permute-start(f32[4,1024]{1,0:T(4,128)S(1)} %pad_maximum_fusion), channel_id=1, source_target_pairs={{0,4},{4,0},{8,12},{12,8},{16,20},{20,16},{24,28},{28,24},{1,5},{5... | collective-permute-start | bytes 49160 | tf_op jit(solution)/shard_map/ppermute | solution.py:40
  68.6 3.8 %collective-permute-start.8 = (f32[4,1024]{1,0:T(4,128)S(1)}, f32[4,1024]{1,0:T(4,128)S(1)}, u32[]{:S(2)}, u32[]{:S(2)}) collective-permute-start(f32[4,1024]{1,0:T(4,128)S(1)} %fusion.2), channel_id=1, source_target_pairs={{0,8},{4,12},{8,0},{12,4},{16,24},{20,28},{24,16},{28,20},{1,9},{5... | collective-permute-start | bytes 49160 | tf_op jit(solution)/shard_map/ppermute | solution.py:40
  72.4 4.6 %collective-permute-start.9 = (f32[4,1024]{1,0:T(4,128)S(1)}, f32[4,1024]{1,0:T(4,128)S(1)}, u32[]{:S(2)}, u32[]{:S(2)}) collective-permute-start(f32[4,1024]{1,0:T(4,128)S(1)} %add.19), channel_id=1, source_target_pairs={{0,16},{4,20},{8,24},{12,28},{16,0},{20,4},{24,8},{28,12},{1,17},{... | collective-permute-start | bytes 49160 | tf_op jit(solution)/shard_map/ppermute | solution.py:40
  81.0 7.3 %collective-permute-start.11 = (f32[3,2,128,512]{3,2,1,0:T(8,128)S(1)}, f32[3,2,128,512]{3,2,1,0:T(8,128)S(1)}, u32[]{:S(2)}, u32[]{:S(2)}) collective-permute-start(f32[3,2,128,512]{3,2,1,0:T(8,128)S(1)} %shard_map.81), channel_id=1, source_target_pairs={{0,1},{1,0},{2,3},{3,2},{4,5},{5,4},{6,7},{7,6},{8,9},{9,8},{10,11... | collective-permute-start | bytes 4718600 | tf_op jit(solution)/shard_map/ppermute | solution.py:40
  81.1 4.9 %collective-permute-start.10 = (f32[2,2,128,512]{3,2,1,0:T(8,128)S(1)}, f32[2,2,128,512]{3,2,1,0:T(8,128)S(1)}, u32[]{:S(2)}, u32[]{:S(2)}) collective-permute-start(f32[2,2,128,512]{3,2,1,0:T(8,128)S(1)} %shard_map.79.earlier_ref), channel_id=1, source_target_pairs={{0,1},{1,0},{2,3},{3,2},{4,5},{5,4},{6,7},{7,6},{8,9},{9,8},{10,11... | collective-permute-start | bytes 3145736 | tf_op jit(solution)/shard_map/ppermute | solution.py:40
  86.8 9.2 %collective-permute-start.13 = (bf16[2,1,128,512]{3,2,1,0:T(8,128)(2,1)S(1)}, bf16[2,1,128,512]{3,2,1,0:T(8,128)(2,1)S(1)}, u32[]{:S(2)}, u32[]{:S(2)}) collective-permute-start(bf16[2,1,128,512]{3,2,1,0:T(8,128)(2,1)S(1)} %get-tuple-element.26), channel_id=1, source_target_pairs={{0,2},{1,3},{2,0},{3,1},{4,6},{5,7},{6,4},{7,5},{8,10},{9,11},{10,... | collective-permute-start | bytes 786440 | tf_op jit(solution)/shard_map/ppermute | solution.py:40
  89.9 14.7 %collective-permute-start.12 = (bf16[1,128,1664]{2,1,0:T(8,128)(2,1)S(1)}, bf16[1,128,1664]{2,1,0:T(8,128)(2,1)S(1)}, u32[]{:S(2)}, u32[]{:S(2)}) collective-permute-start(bf16[1,128,1664]{2,1,0:T(8,128)(2,1)S(1)} %get-tuple-element.25), channel_id=1, source_target_pairs={{0,2},{1,3},{2,0},{3,1},{4,6},{5,7},{6,4},{7,5},{8,10},{9,11},{10,... | collective-permute-start | bytes 1277960 | tf_op jit(solution)/shard_map/ppermute | solution.py:40
  96.1 6.3 %collective-permute-start.14 = (bf16[128,512]{1,0:T(8,128)(2,1)S(1)}, bf16[128,512]{1,0:T(8,128)(2,1)S(1)}, u32[]{:S(2)}, u32[]{:S(2)}) collective-permute-start(bf16[128,512]{1,0:T(8,128)(2,1)S(1)} %get-tuple-element.28), channel_id=1, source_target_pairs={{4,0},{8,4},{12,8},{16,12},{20,16},{24,20},{28,24},{0,28},{5,1},{9... | collective-permute-start | bytes 393224 | tf_op jit(solution)/shard_map/ppermute | solution.py:30
  99.6 5.0 %collective-permute-start.15 = (bf16[128,512]{1,0:T(8,128)(2,1)S(1)}, bf16[128,512]{1,0:T(8,128)(2,1)S(1)}, u32[]{:S(2)}, u32[]{:S(2)}) collective-permute-start(bf16[128,512]{1,0:T(8,128)(2,1)S(1)} %get-tuple-element.27), channel_id=1, source_target_pairs={{8,0},{12,4},{16,8},{20,12},{24,16},{28,20},{0,24},{4,28},{9,1},{1... | collective-permute-start | bytes 393224 | tf_op jit(solution)/shard_map/ppermute | solution.py:30
  (1 other events, 0.7 us)
where the time goes:
time: 106 us
  waiting for transfers between devices  49.6 us (47%)
  starting transfers between devices  33.3 us (31%)
  Pallas kernels  16.6 us (16%)
  local copies, waits for them, and re-layouts  5.42 us (5%)
    ppermute x10, waiting for transfers between devices, swap(): lax.ppermute(block, axis, [(i, i ^ bit) for i in range(lax.axis_size(axis...  24.8 us
    ppermute x4, starting transfers between devices, from_side(): return lax.ppermute(block, 'row', route)  22.9 us
    ppermute x4, waiting for transfers between devices, from_side(): return lax.ppermute(block, 'row', route)  19.9 us
    ppermute x10, starting transfers between devices, swap(): lax.ppermute(block, axis, [(i, i ^ bit) for i in range(lax.axis_size(axis...  6.92 us
    unnamed x18, local copies, waits for them, and re-layouts  5.4 us
    ppermute x2, waiting for transfers between devices, from_ahead(): lax.ppermute(block, 'row', [((i + distance) % size, i) for i in range(siz...  4.96 us
    pallas_call x2, Pallas kernels, body(): call(functools.partial(sums_kernel, sb, gb, first), shape((components, wi...  4.3 us
    ppermute x2, starting transfers between devices, from_ahead(): lax.ppermute(block, 'row', [((i + distance) % size, i) for i in range(siz...  3.5 us
  transfers between devices with their start and end apart: 16, of which 10 were waited for; matrix products, arithmetic and copies ran while one was open for 0% of the time, Pallas kernels for 7%

commit v1 on v0

--- a/solution.py
+++ b/solution.py
@@ -117,18 +117,14 @@
     return dot(high_ref[column], block) + dot(low_ref[column], block)
 
 
-def early_kernel(high_ref, low_ref, own, beside, *rest):
-    near, totals = rest[: len(rest) // 2], rest[len(rest) // 2 :]
+def early_kernel(start, high_ref, low_ref, own, beside, near, total_ref):
     sign = 1 - 2 * position()[0]
-    start = 0
-    for block, total in zip(near, totals):
-        cols = slice(start, start + block.shape[1])
-        total[...] = (
-            both(high_ref, low_ref, REACH, own[:, cols])
-            + both(high_ref, low_ref, REACH + sign, beside[:, cols])
-            + both(high_ref, low_ref, REACH + 2 * sign, block[...])
-        )
-        start += block.shape[1]
+    cols = slice(start, start + near.shape[1])
+    total_ref[...] = (
+        both(high_ref, low_ref, REACH, own[:, cols])
+        + both(high_ref, low_ref, REACH + sign, beside[:, cols])
+        + both(high_ref, low_ref, REACH + 2 * sign, near[...])
+    )
 
 
 def sums_kernel(sb, gb, first, screen_ref, high_ref, low_ref, partial_ref, far, across, basis_ref,
@@ -184,19 +180,12 @@
         start += width
 
 
-def mirrored_product(half_ref, one, two, side, share, count):
+def mirrored_product(half_ref, blocks, side, share, count):
     total = 0
-    for blocks in zip(pieces(two), pieces(one) if len(one) > 1 else pieces(two)):
-        (cols, second), (_, first) = blocks
-        if len(one) > 1:
-            first_rows = rows_of(first, slice(None), side, share, count)
-        else:
-            first_rows = rows_of(one[0], cols, side, share, count)
-        left = jnp.concatenate(
-            [first_rows, rows_of(second, slice(None), side, share, count)], axis=0
-        )
+    for cols, block in pieces(blocks):
+        left = rows_of(block, slice(None), side, share, count)
         total += dot_rows(left, half_ref[:, cols])
-    return total.reshape(REACH, count, share, half_ref.shape[0])
+    return total.reshape(count, share, half_ref.shape[0])
 
 
 def central_product(half_ref, own, side, share, count):
@@ -219,6 +208,18 @@
     return (beside, near), (across, far)
 
 
+def behind(first, second, run):
+    odd = position()[0]
+
+    @pl.when(odd != 0)
+    def _():
+        run(first)
+
+    @pl.when(odd == 0)
+    def _():
+        run(second)
+
+
 def on_side(refs, chunks, ahead, run):
     first, second = neighbours(refs, chunks)
     odd = position()[0]
@@ -239,91 +240,96 @@
         send_ref[..., step, :, :] = jnp.where(side == 0, high, low).astype(send_ref.dtype)
 
 
-def mirrored_other_kernel(share, count, chunks, half_ref, *refs):
+def mirrored_other_kernel(share, count, cut, half_ref, earlier_ref, *refs):
+    first, second, out = refs[:cut], refs[cut:-1], refs[-1]
+    side = 1 - position()[1]
+
+    def run(blocks):
+        out[...] = mirrored_product(half_ref, blocks, side, share, count)
+
+    behind(first, second, run)
+
+
+def mirrored_own_kernel(share, count, cut, half_ref, found_ref, *refs):
+    first, second, keep_ref, send_ref = refs[:cut], refs[cut:-2], refs[-2], refs[-1]
+    _, core, side = position()
+
+    def run(blocks):
+        total = mirrored_product(half_ref, blocks, core, share, count)
+        deposit(total + found_ref[...], side, keep_ref, send_ref)
+
+    behind(first, second, run)
+
+
+def central_other_kernel(share, count, half_ref, own, out):
+    out[...] = central_product(half_ref, own, 1 - position()[1], share, count)
+
+
+def direct_other_kernel(share, count, chunks, half_ref, earlier_ref, *refs):
     refs, out = refs[:-1], refs[-1]
     side = 1 - position()[1]
 
     def run(one, two):
-        out[...] = mirrored_product(half_ref, one, two, side, share, count)
-
-    on_side(refs, chunks, False, run)
-
-
-def mirrored_own_kernel(share, count, chunks, half_ref, found_ref, *refs):
-    refs, keep_ref, send_ref = refs[:-2], refs[-2], refs[-1]
-    _, core, side = position()
-
-    def run(one, two):
-        total = mirrored_product(half_ref, one, two, core, share, count)
-        deposit(total + found_ref[...], side, keep_ref, send_ref)
-
-    on_side(refs, chunks, False, run)
-
-
-def direct_other_kernel(share, count, chunks, half_ref, own, earlier_ref, *refs):
-    refs, out = refs[:-1], refs[-1]
-    side = 1 - position()[1]
-    out[0] = central_product(half_ref, own, side, share, count)
-
-    def run(one, two):
-        out[1] = direct_product(half_ref, one, side, share, count)
-        out[2] = direct_product(half_ref, two, side, share, count)
+        out[0] = direct_product(half_ref, one, side, share, count)
+        out[1] = direct_product(half_ref, two, side, share, count)
 
     on_side(refs, chunks, True, run)
 
 
-def direct_own_kernel(share, count, chunks, half_ref, own, earlier_ref, found_ref, *refs):
-    refs, keep_ref, send_ref = refs[:-2], refs[-2], refs[-1]
+def central_own_kernel(share, count, half_ref, own, found_ref, keep_ref, send_ref):
     _, core, side = position()
     size = half_ref.shape[0]
-    spare = send_ref.shape[-1] - 3 * size
-
-    def place(k, total):
-        for step in range(count // 2):
-            low, high = total[2 * step], total[2 * step + 1]
-            keep_ref[k, step] = jnp.where(side == 0, low, high)
-            send = jnp.where(side == 0, high, low)
-            rounded = send.astype(BF16)
-            send_ref[step, :, k * size : (k + 1) * size] = rounded
-            if k == 0:
-                for block in range(size // spare):
-                    quarter = (2 * step + 1 - side) * 2 + core
-
-                    @pl.when((quarter * share) // spare == block)
-                    def _():
-                        cols = slice(block * spare, (block + 1) * spare)
-                        rest = send[:, cols] - rounded[:, cols].astype(F32)
-                        send_ref[step, :, 3 * size :] = rest.astype(BF16)
-
-    place(0, central_product(half_ref, own, core, share, count) + found_ref[0])
-
-    def run(one, two):
-        place(1, direct_product(half_ref, one, core, share, count) + found_ref[1])
-        place(2, direct_product(half_ref, two, core, share, count) + found_ref[2])
-
-    on_side(refs, chunks, True, run)
-
-
-def joined_kernel(share, keep_ref, found_ref, out_ref):
-    _, core, side = position()
-    size = keep_ref.shape[-1]
-    spare = found_ref.shape[-1] - 3 * size
-    for step in range(found_ref.shape[0]):
-        for k in range(3):
-            part = found_ref[step, :, k * size : (k + 1) * size].astype(F32)
-            out_ref[step, :, k * size : (k + 1) * size] = keep_ref[k, step] + part
-        quarter = (2 * step + side) * 2 + core
+    spare = send_ref.shape[-1] - size
+    total = central_product(half_ref, own, core, share, count) + found_ref[...]
+    for step in range(count // 2):
+        low, high = total[2 * step], total[2 * step + 1]
+        keep_ref[step] = jnp.where(side == 0, low, high)
+        send = jnp.where(side == 0, high, low)
+        rounded = send.astype(BF16)
+        send_ref[step, :, :size] = rounded
+        quarter = (2 * step + 1 - side) * 2 + core
         for block in range(size // spare):
 
             @pl.when((quarter * share) // spare == block)
             def _():
                 cols = slice(block * spare, (block + 1) * spare)
-                out_ref[step, :, cols] += found_ref[step, :, 3 * size :].astype(F32)
-
-
-def final_kernel(share, keep_ref, found_ref, *refs):
+                rest = send[:, cols] - rounded[:, cols].astype(F32)
+                send_ref[step, :, size:] = rest.astype(BF16)
+
+
+def direct_own_kernel(share, count, chunks, half_ref, found_ref, earlier_ref, *refs):
+    refs, keep_ref, send_ref = refs[:-2], refs[-2], refs[-1]
+    _, core, side = position()
+
+    def run(one, two):
+        for k, blocks in enumerate((one, two)):
+            total = direct_product(half_ref, blocks, core, share, count) + found_ref[k]
+            deposit(total, side, keep_ref.at[k], send_ref.at[k])
+
+    on_side(refs, chunks, True, run)
+
+
+def joined_kernel(share, central_ref, found_ref, keep_ref, direct_ref, out_ref):
+    _, core, side = position()
+    size = keep_ref.shape[-1]
+    spare = found_ref.shape[-1] - size
+    for step in range(found_ref.shape[0]):
+        out_ref[step, :, :size] = central_ref[step] + found_ref[step, :, :size].astype(F32)
+        for k in range(REACH):
+            cols = slice((k + 1) * size, (k + 2) * size)
+            out_ref[step, :, cols] = keep_ref[k, step] + direct_ref[k, step].astype(F32)
+        quarter = (2 * step + side) * 2 + core
+        for block in range(size // spare):
+
+            @pl.when((quarter * share) // spare == block)
+            def _():
+                cols = slice(block * spare, (block + 1) * spare)
+                out_ref[step, :, cols] += found_ref[step, :, size:].astype(F32)
+
+
+def final_kernel(share, central_ref, found_ref, keep_ref, direct_ref, *refs):
     mirrored, out_ref = refs[:-1], refs[-1]
-    joined_kernel(share, keep_ref, found_ref, out_ref)
+    joined_kernel(share, central_ref, found_ref, keep_ref, direct_ref, out_ref)
     size = keep_ref.shape[-1]
     for k, block in enumerate(mirrored):
         cols = slice((k + 1) * size, (k + 2) * size)
@@ -339,8 +345,8 @@
     col = lax.axis_index("col")
     components, row_count, points = basis_values.shape
     sb, gb = row_count // screen.shape[0], points // screen.shape[1]
-    last = max(1, screen.shape[1] // 4) * gb
-    widths = (points - last, last)
+    eighth = max(1, screen.shape[1] // 8) * gb
+    widths = (points - 3 * eighth, 2 * eighth, eighth)
     chunks = len(widths)
     share, count = row_count // cols, cols // 2
     square = 2 * row_count * row_count
@@ -353,7 +359,7 @@
             pltpu.VMEM((row_count, points), BF16),
             pltpu.SemaphoreType.DMA((screen.shape[0],)),
         ],
-    )(screen, basis_values)
+    )(screen, pltpu.with_memory_space_constraint(basis_values, pltpu.HBM))
     near, far, across = [], [], []
     for chunk, block in enumerate(mine):
         near.append(from_side(block, 2))
@@ -365,20 +371,19 @@
         split_kernel, [shape((BAND, row_count, row_count), BF16)] * 2, [WHOLE],
         density.size * 4, density.size * 8,
     )(density)
-    partial = call(
-        early_kernel, [shape((row_count, width)) for width in widths], [WHOLE] * (4 + chunks),
-        6 * square * points, 10 * square,
-    )(high, low, own, beside, *near)
     sums, first = [], 0
     for chunk, width in enumerate(widths):
-        sums.append(
-            call(
-                functools.partial(sums_kernel, sb, gb, first), shape((components, width)),
-                [SCALARS] + [WHOLE] * 6, 4 * square * width, 6 * square,
-                scratch=[pltpu.VMEM((row_count, width), F32)],
-            )(screen, high, low, partial[chunk], far[chunk], across[chunk], basis_values)
-        )
-        first += width // gb
+        partial = call(
+            functools.partial(early_kernel, first), shape((row_count, width)), [WHOLE] * 5,
+            6 * square * width, 10 * square,
+        )(high, low, own, beside, near[chunk])
+        found = call(
+            functools.partial(sums_kernel, sb, gb, first // gb), shape((components, width)),
+            [SCALARS] + [WHOLE] * 6, 4 * square * width, 6 * square,
+            scratch=[pltpu.VMEM((row_count, width), F32)],
+        )(screen, high, low, partial, far[chunk], across[chunk], basis_values)
+        sums.append(found)
+        first += width
     summed = jnp.concatenate(sums, axis=1)
     bit = 1
     while bit < rows:
@@ -405,38 +410,54 @@
     )(screen, basis_values, parts)
 
     beyond = (beside, *near, *far, *across)
+    paired = {1: ((beside,), across), 2: (near, far)}
     product = 2 * row_count * points * share * count
-    mirrored_other = call(
-        functools.partial(mirrored_other_kernel, share, count, chunks),
-        shape((REACH, count, share, row_count)), [WHOLE] * (1 + len(beyond)),
-        product * 2, 4 * row_count * points,
-    )(half, *beyond)
-    mirrored_found = swap(mirrored_other, "col", 1)
+    kept = count // 2
+    block = (count, share, row_count)
+    mirrored_found, earlier = {}, half
+    for k in (2, 1):
+        first, second = paired[k]
+        earlier = call(
+            functools.partial(mirrored_other_kernel, share, count, len(first)), shape(block),
+            [WHOLE, ANYWHERE] + [WHOLE] * len((*first, *second)), product, 3 * half.size,
+        )(half, earlier, *first, *second)
+        mirrored_found[k] = swap(earlier, "col", 1)
+    central_other = call(
+        functools.partial(central_other_kernel, share, count), shape(block),
+        [WHOLE] * 2, 2 * product, 4 * half.size,
+    )(half, own)
+    central_found = swap(central_other, "col", 1)
+    mirrored_keep, mirrored_send = {}, {}
+    for k in (2, 1):
+        first, second = paired[k]
+        mirrored_keep[k], mirrored_send[k] = call(
+            functools.partial(mirrored_own_kernel, share, count, len(first)),
+            [shape((kept, share, row_count)), shape((kept, share, row_count), BF16)],
+            [WHOLE] * len((half, half, *first, *second)), product, 4 * half.size,
+        )(half, mirrored_found[k], *first, *second)
     direct_other = call(
-        functools.partial(direct_other_kernel, share, count, chunks),
-        shape((REACH + 1, count, share, row_count)),
-        [WHOLE] * 2 + [ANYWHERE] + [WHOLE] * len(beyond),
-        product * 4, 6 * row_count * points,
-    )(half, own, mirrored_other, *beyond)
+        functools.partial(direct_other_kernel, share, count, chunks), shape((REACH, *block)),
+        [WHOLE, ANYWHERE] + [WHOLE] * len(beyond), product * 2, 4 * half.size,
+    )(half, central_other, *beyond)
     direct_found = swap(direct_other, "col", 1)
-    kept = count // 2
-    mirrored_keep, mirrored_send = call(
-        functools.partial(mirrored_own_kernel, share, count, chunks),
+    spare = max(share, 128)
+    central_keep, central_send = call(
+        functools.partial(central_own_kernel, share, count),
+        [
+            shape((kept, share, row_count)),
+            shape((kept, share, row_count + spare), BF16),
+        ],
+        [WHOLE] * 3, product * 2, 4 * half.size,
+    )(half, own, central_found)
+    central_found = swap(central_send, "col", 2)
+    direct_keep, direct_send = call(
+        functools.partial(direct_own_kernel, share, count, chunks),
         [
             shape((REACH, kept, share, row_count)),
             shape((REACH, kept, share, row_count), BF16),
         ],
-        [WHOLE] * (2 + len(beyond)), product * 2, 6 * row_count * points,
-    )(half, mirrored_found, *beyond)
-    spare = max(share, 128)
-    direct_keep, direct_send = call(
-        functools.partial(direct_own_kernel, share, count, chunks),
-        [
-            shape((REACH + 1, kept, share, row_count)),
-            shape((kept, share, 3 * row_count + spare), BF16),
-        ],
-        [WHOLE] * 2 + [ANYWHERE] + [WHOLE] * (1 + len(beyond)), product * 4, 8 * row_count * points,
-    )(half, own, mirrored_keep, direct_found, *beyond)
+        [WHOLE] * 2 + [ANYWHERE] + [WHOLE] * len(beyond), product * 2, 4 * half.size,
+    )(half, direct_found, central_keep, *beyond)
 
     def scatter(total, axis):
         bit = 4
@@ -449,23 +470,25 @@
             bit *= 2
         return total
 
-    found = swap(mirrored_send, "col", 2)
-    mirrored = mirrored_keep + found.astype(F32)
-    mirrored = scatter(mirrored, 1).astype(BF16)
-    mirrored = [from_ahead(mirrored[k, 0], k + 1) for k in range(REACH)]
+    mirrored = []
+    for k in (2, 1):
+        found = swap(mirrored_send[k], "col", 2)
+        total = scatter(mirrored_keep[k] + found.astype(F32), 0).astype(BF16)
+        mirrored.insert(0, from_ahead(total[0], k))
     found = swap(direct_send, "col", 2)
+    partial = (central_keep, central_found, direct_keep, found)
     if kept > 1:
         total = call(
             functools.partial(joined_kernel, share), shape((kept, share, 3 * row_count)),
-            [WHOLE] * 2, direct_keep.size, 8 * direct_keep.size,
-        )(direct_keep, found)
+            [WHOLE] * 4, direct_keep.size, 8 * direct_keep.size,
+        )(*partial)
         total = scatter(total, 0)[0]
         zero = jnp.zeros((share, row_count), BF16)
         return total + jnp.concatenate([zero, *mirrored], axis=1).astype(F32)
     return call(
         functools.partial(final_kernel, share), shape((1, share, 3 * row_count)),
-        [WHOLE] * (2 + REACH), direct_keep.size, 10 * direct_keep.size,
-    )(direct_keep, found, *mirrored)[0]
+        [WHOLE] * (4 + REACH), direct_keep.size, 10 * direct_keep.size,
+    )(*partial, *mirrored)[0]
 
 
 def solution(mesh):

time: 106 us -> 109 us (1.028)
  Pallas kernels: 16.6 us -> 20.8 us
  waiting for transfers between devices: 49.6 us -> 53 us
  starting transfers between devices: 33.3 us -> 30.7 us
  local copies, waits for them, and re-layouts: 5.42 us -> 3.22 us
    ppermute x4 -> x6, waiting for transfers between devices: 19.9 us -> 36 us  [from_side(): return lax.ppermute(block, 'row', route)]
    ppermute x4 -> x6, starting transfers between devices: 22.9 us -> 8.11 us  [from_side(): return lax.ppermute(block, 'row', route)]
    ppermute x10 -> x15, starting transfers between devices: 6.92 us -> 18.2 us  [swap(): lax.ppermute(block, axis, [(i, i ^ bit) for i in range(lax.axis_size(axis...]
    ppermute x10 -> x15, waiting for transfers between devices: 24.8 us -> 13.7 us  [swap(): lax.ppermute(block, axis, [(i, i ^ bit) for i in range(lax.axis_size(axis...]
    pallas_call x5 -> x12, Pallas kernels: 9.22 us -> 14 us  [the longest x3 5.52 us: body(): call(functools.partial(sums_kernel, sb, gb, first // gb), shape((componen...]
    unnamed x18 -> x16, local copies, waits for them, and re-layouts: 5.4 us -> 3.22 us
    ppermute x2, waiting for transfers between devices: 4.96 us -> 3.36 us  [from_ahead(): lax.ppermute(block, 'row', [((i + distance) % size, i) for i in range(siz...]
  transfers between devices with their start and end apart: 16 -> 23, of which waited for: 10 -> 11; matrix products, arithmetic and copies ran while one was open for 0% -> 0% of each run, Pallas kernels for 7% -> 11%
where the time goes in v1:
time: 109 us; the launch traced here: 108 us
  waiting for transfers between devices  53 us (49%)
  starting transfers between devices  30.7 us (28%)
  Pallas kernels  20.8 us (19%)
  local copies, waits for them, and re-layouts  3.22 us (3%)
    ppermute x6, waiting for transfers between devices, from_side(): return lax.ppermute(block, 'row', route)  36 us
    ppermute x15, starting transfers between devices, swap(): lax.ppermute(block, axis, [(i, i ^ bit) for i in range(lax.axis_size(axis...  18.2 us
    ppermute x15, waiting for transfers between devices, swap(): lax.ppermute(block, axis, [(i, i ^ bit) for i in range(lax.axis_size(axis...  13.7 us
    ppermute x6, starting transfers between devices, from_side(): return lax.ppermute(block, 'row', route)  8.11 us
    pallas_call x3, Pallas kernels, body(): call(functools.partial(sums_kernel, sb, gb, first // gb), shape((componen...  5.52 us
    pallas_call x3, Pallas kernels, body(): call(functools.partial(early_kernel, first), shape((row_count, width)), [...  4.57 us
    ppermute x2, starting transfers between devices, from_ahead(): lax.ppermute(block, 'row', [((i + distance) % size, i) for i in range(siz...  4.35 us
    ppermute x2, waiting for transfers between devices, from_ahead(): lax.ppermute(block, 'row', [((i + distance) % size, i) for i in range(siz...  3.36 us
  transfers between devices with their start and end apart: 23, of which 11 were waited for; matrix products, arithmetic and copies ran while one was open for 0% of the time, Pallas kernels for 11%

profile of v1, /device:TPU:0, one launch (start us, length us, event | category | flops | bytes accessed | tf_op | source)
XLA Modules:
  0.0 108.4 jit_solution(2464923367460427243)
XLA Ops:
  0.7 1.9 %shard_map.74 = (bf16[512,1024]{1,0:T(8,128)(2,1)S(1)}, bf16[512,640]{1,0:T(8,128)(2,1)S(1)}, bf16[512,256]{1,0:T(8,128)(2,1)S(1)}, bf16[512,128]{1,0:T(8,128)(2,1)S(1)}) custom-call(s32[4,8]{1,0:T(4,128)S(1)} %copy-done.3, bf16[4,512,1024]{2,1,0:T(8,128)(2,1)} %basis_ref.9), custom_call_target="tpu_custom_call" | custom-call | flops 524288 | bytes 3145728 | tf_op jit(solution)/shard_map/pallas_call | solution.py:354
  2.6 3.1 %collective-permute-start = (bf16[512,1024]{1,0:T(8,128)(2,1)S(1)}, bf16[512,1024]{1,0:T(8,128)(2,1)S(1)}, u32[]{:S(2)}, u32[]{:S(2)}) collective-permute-start(bf16[512,1024]{1,0:T(8,128)(2,1)S(1)} %get-tuple-element.21.own), channel_id=1, source_target_pairs={{0,4},{4,0},{8,12},{12,8},{16,20},{20,16},{24,28},{28,24},{1,5},{5... | collective-permute-start | bytes 3145736 | tf_op jit(solution)/shard_map/ppermute | solution.py:40
  5.7 3.6 %collective-permute-start.1 = (bf16[512,640]{1,0:T(8,128)(2,1)S(1)}, bf16[512,640]{1,0:T(8,128)(2,1)S(1)}, u32[]{:S(2)}, u32[]{:S(2)}) collective-permute-start(bf16[512,640]{1,0:T(8,128)(2,1)S(1)} %get-tuple-element.22), channel_id=1, source_target_pairs={{8,0},{28,4},{16,8},{4,12},{24,16},{12,20},{0,24},{20,28},{9,1},{2... | collective-permute-start | bytes 1966088 | tf_op jit(solution)/shard_map/ppermute | solution.py:36
  10.2 1.6 %collective-permute-start.2 = (bf16[512,640]{1,0:T(8,128)(2,1)S(1)}, bf16[512,640]{1,0:T(8,128)(2,1)S(1)}, u32[]{:S(2)}, u32[]{:S(2)}) collective-permute-start(bf16[512,640]{1,0:T(8,128)(2,1)S(1)} %get-tuple-element.22), channel_id=1, source_target_pairs={{24,0},{12,4},{0,8},{20,12},{8,16},{28,20},{16,24},{4,28},{25,1},{... | collective-permute-start | bytes 1966088 | tf_op jit(solution)/shard_map/ppermute | solution.py:36
  11.7 12.7 %collective-permute-done.1.near.refs_1_.refs_0_ = bf16[512,640]{1,0:T(8,128)(2,1)S(1)} collective-permute-done((bf16[512,640]{1,0:T(8,128)(2,1)S(1)}, bf16[512,640]{1,0:T(8,128)(2,1)S(1)}, u32[]{:S(2)}, u32[]{:S(2)}) %collective-permute-start.1) | collective-permute-done | bytes 655392 | tf_op jit(solution)/shard_map/ppermute | solution.py:36
  25.5 1.8 %collective-permute-done.7.near.refs_3_.refs_2_ = bf16[512,128]{1,0:T(8,128)(2,1)S(1)} collective-permute-done((bf16[512,128]{1,0:T(8,128)(2,1)S(1)}, bf16[512,128]{1,0:T(8,128)(2,1)S(1)}, u32[]{:S(2)}, u32[]{:S(2)}) %collective-permute-start.7) | collective-permute-done | bytes 131104 | tf_op jit(solution)/shard_map/ppermute | solution.py:36
  27.6 21.5 %collective-permute-done.8.far.refs_6_.refs_5_ = bf16[512,128]{1,0:T(8,128)(2,1)S(1)} collective-permute-done((bf16[512,128]{1,0:T(8,128)(2,1)S(1)}, bf16[512,128]{1,0:T(8,128)(2,1)S(1)}, u32[]{:S(2)}, u32[]{:S(2)}) %collective-permute-start.8) | collective-permute-done | bytes 131104 | tf_op jit(solution)/shard_map/ppermute | solution.py:36
  49.1 1.6 %collective-permute-start.5 = (bf16[512,256]{1,0:T(8,128)(2,1)S(1)}, bf16[512,256]{1,0:T(8,128)(2,1)S(1)}, u32[]{:S(2)}, u32[]{:S(2)}) collective-permute-start(bf16[512,256]{1,0:T(8,128)(2,1)S(1)} %get-tuple-element.23), channel_id=1, source_target_pairs={{24,0},{12,4},{0,8},{20,12},{8,16},{28,20},{16,24},{4,28},{25,1},{... | collective-permute-start | bytes 786440 | tf_op jit(solution)/shard_map/ppermute | solution.py:36
  51.1 1.7 %collective-permute-start.9 = (bf16[512,128]{1,0:T(8,128)(2,1)S(1)}, bf16[512,128]{1,0:T(8,128)(2,1)S(1)}, u32[]{:S(2)}, u32[]{:S(2)}) collective-permute-start(bf16[512,128]{1,0:T(8,128)(2,1)S(1)} %collective-permute-done.7.near.refs_3_.refs_2_), channel_id=1, source_target_pairs={{0,4},{4,0},{8,12},{12,8},{16,20},{20,16},{24,28},{28,24},{1,5},{5... | collective-permute-start | bytes 393224 | tf_op jit(solution)/shard_map/ppermute | solution.py:40
  52.8 2.5 %copy-done.2 = f32[512,2560]{1,0:T(8,128)S(1)} copy-done((f32[512,2560]{1,0:T(8,128)S(1)}, f32[512,2560]{1,0:T(8,128)}, u32[]{:S(2)}) %copy-start.2) | copy-done | bytes 5242904
  57.0 3.5 %collective-permute-done.9.across.refs_9_.refs_3_ = bf16[512,128]{1,0:T(8,128)(2,1)S(1)} collective-permute-done((bf16[512,128]{1,0:T(8,128)(2,1)S(1)}, bf16[512,128]{1,0:T(8,128)(2,1)S(1)}, u32[]{:S(2)}, u32[]{:S(2)}) %collective-permute-start.9) | collective-permute-done | bytes 131104 | tf_op jit(solution)/shard_map/ppermute | solution.py:40
  64.2 2.6 %shard_map.75.partial_ref = f32[512,640]{1,0:T(8,128)S(1)} custom-call(bf16[5,512,512]{2,1,0:T(8,128)(2,1)S(1)} %get-tuple-element.19.high_ref, bf16[5,512,512]{2,1,0:T(8,128)(2,1)S(1)} %get-tuple-element.20.low_ref, bf16[512,1024]{1,0:T(8,128)(2,1)S(1)} %get-tuple-element.21.own, bf16[512,1024]{1,0:T(8,128)(2,1)S(1)} %collective-permute-done.beside.refs_0_, ...), custom_call_target="tpu_custom_call" | custom-call | flops 2013265920 | bytes 5242880 | tf_op jit(solution)/shard_map/pallas_call | solution.py:376
  66.9 2.8 %shard_map.76 = f32[4,640]{1,0:T(4,128)S(1)} custom-call(s32[4,8]{1,0:T(4,128)S(1)} %copy-done.4, bf16[5,512,512]{2,1,0:T(8,128)(2,1)S(1)} %get-tuple-element.19.high_ref, bf16[5,512,512]{2,1,0:T(8,128)(2,1)S(1)} %get-tuple-element.20.low_ref, f32[512,640]{1,0:T(8,128)S(1)} %shard_map.75.partial_ref, ...), custom_call_target="tpu_custom_call" | custom-call | flops 1342177280 | bytes 3145728 | tf_op jit(solution)/shard_map/pallas_call | solution.py:380
  70.1 3.5 %collective-permute-done.10 = f32[4,1024]{1,0:T(4,128)S(1)} collective-permute-done((f32[4,1024]{1,0:T(4,128)S(1)}, f32[4,1024]{1,0:T(4,128)S(1)}, u32[]{:S(2)}, u32[]{:S(2)}) %collective-permute-start.10) | collective-permute-done | bytes 16416 | tf_op jit(solution)/shard_map/ppermute | solution.py:40
  73.5 2.5 %collective-permute-start.11 = (f32[4,1024]{1,0:T(4,128)S(1)}, f32[4,1024]{1,0:T(4,128)S(1)}, u32[]{:S(2)}, u32[]{:S(2)}) collective-permute-start(f32[4,1024]{1,0:T(4,128)S(1)} %fusion.4), channel_id=1, source_target_pairs={{0,8},{4,12},{8,0},{12,4},{16,24},{20,28},{24,16},{28,20},{1,9},{5... | collective-permute-start | bytes 49160 | tf_op jit(solution)/shard_map/ppermute | solution.py:40
  76.1 1.7 %collective-permute-done.11 = f32[4,1024]{1,0:T(4,128)S(1)} collective-permute-done((f32[4,1024]{1,0:T(4,128)S(1)}, f32[4,1024]{1,0:T(4,128)S(1)}, u32[]{:S(2)}, u32[]{:S(2)}) %collective-permute-start.11) | collective-permute-done | bytes 16416 | tf_op jit(solution)/shard_map/ppermute | solution.py:40
  77.8 2.9 %collective-permute-start.12 = (f32[4,1024]{1,0:T(4,128)S(1)}, f32[4,1024]{1,0:T(4,128)S(1)}, u32[]{:S(2)}, u32[]{:S(2)}) collective-permute-start(f32[4,1024]{1,0:T(4,128)S(1)} %add.22), channel_id=1, source_target_pairs={{0,16},{4,20},{8,24},{12,28},{16,0},{20,4},{24,8},{28,12},{1,17},{... | collective-permute-start | bytes 49160 | tf_op jit(solution)/shard_map/ppermute | solution.py:40
  82.6 1.6 %shard_map.81.half_ref.earlier_ref = bf16[512,1024]{1,0:T(8,128)(2,1)S(1)} custom-call(s32[4,8]{1,0:T(4,128)S(1)} %copy-done.4, bf16[4,512,1024]{2,1,0:T(8,128)(2,1)S(1)} %copy-done.1, f32[4,1024]{1,0:T(4,128)S(1)} %pad_maximum_fusion.1.parts_ref), custom_call_target="tpu_custom_call" | custom-call | flops 16777216 | bytes 4194304 | tf_op jit(solution)/shard_map/pallas_call | solution.py:407
  89.8 1.6 %collective-permute-start.21 = (bf16[1,128,512]{2,1,0:T(8,128)(2,1)S(1)}, bf16[1,128,512]{2,1,0:T(8,128)(2,1)S(1)}, u32[]{:S(2)}, u32[]{:S(2)}) collective-permute-start(bf16[1,128,512]{2,1,0:T(8,128)(2,1)S(1)} %get-tuple-element.32), channel_id=1, source_target_pairs={{0,2},{1,3},{2,0},{3,1},{4,6},{5,7},{6,4},{7,5},{8,10},{9,11},{10,... | collective-permute-start | bytes 393224 | tf_op jit(solution)/shard_map/ppermute | solution.py:40
  93.3 1.6 %collective-permute-start.14 = (bf16[1,128,640]{2,1,0:T(8,128)(2,1)S(1)}, bf16[1,128,640]{2,1,0:T(8,128)(2,1)S(1)}, u32[]{:S(2)}, u32[]{:S(2)}) collective-permute-start(bf16[1,128,640]{2,1,0:T(8,128)(2,1)S(1)} %get-tuple-element.26), channel_id=1, source_target_pairs={{0,2},{1,3},{2,0},{3,1},{4,6},{5,7},{6,4},{7,5},{8,10},{9,11},{10,... | collective-permute-start | bytes 491528 | tf_op jit(solution)/shard_map/ppermute | solution.py:40
  96.3 2.7 %collective-permute-start.22 = (bf16[128,512]{1,0:T(8,128)(2,1)S(1)}, bf16[128,512]{1,0:T(8,128)(2,1)S(1)}, u32[]{:S(2)}, u32[]{:S(2)}) collective-permute-start(bf16[128,512]{1,0:T(8,128)(2,1)S(1)} %fusion.1), channel_id=1, source_target_pairs={{8,0},{12,4},{16,8},{20,12},{24,16},{28,20},{0,24},{4,28},{9,1},{1... | collective-permute-start | bytes 393224 | tf_op jit(solution)/shard_map/ppermute | solution.py:30
  99.8 1.6 %collective-permute-start.16 = (bf16[2,1,128,512]{3,2,1,0:T(8,128)(2,1)S(1)}, bf16[2,1,128,512]{3,2,1,0:T(8,128)(2,1)S(1)}, u32[]{:S(2)}, u32[]{:S(2)}) collective-permute-start(bf16[2,1,128,512]{3,2,1,0:T(8,128)(2,1)S(1)} %get-tuple-element.28), channel_id=1, source_target_pairs={{0,2},{1,3},{2,0},{3,1},{4,6},{5,7},{6,4},{7,5},{8,10},{9,11},{10,... | collective-permute-start | bytes 786440 | tf_op jit(solution)/shard_map/ppermute | solution.py:40
  101.4 1.7 %collective-permute-start.19 = (bf16[128,512]{1,0:T(8,128)(2,1)S(1)}, bf16[128,512]{1,0:T(8,128)(2,1)S(1)}, u32[]{:S(2)}, u32[]{:S(2)}) collective-permute-start(bf16[128,512]{1,0:T(8,128)(2,1)S(1)} %fusion), channel_id=1, source_target_pairs={{4,0},{8,4},{12,8},{16,12},{20,16},{24,20},{28,24},{0,28},{5,1},{9... | collective-permute-start | bytes 393224 | tf_op jit(solution)/shard_map/ppermute | solution.py:30
  103.1 3.4 %collective-permute-done.19.refs_0_ = bf16[128,512]{1,0:T(8,128)(2,1)S(1)} collective-permute-done((bf16[128,512]{1,0:T(8,128)(2,1)S(1)}, bf16[128,512]{1,0:T(8,128)(2,1)S(1)}, u32[]{:S(2)}, u32[]{:S(2)}) %collective-permute-start.19) | collective-permute-done | bytes 131104 | tf_op jit(solution)/shard_map/ppermute | solution.py:30
  (68 shorter events, 22.8 us)
Async XLA Ops:
  0.0 80.7 %copy-start = (f32[64]{0:T(128)S(1)}, f32[64]{0:T(128)}, u32[]{:S(2)}) copy-start(f32[64]{0:T(128)} %param.11) | copy-start | bytes 772
  2.6 48.5 %collective-permute-start = (bf16[512,1024]{1,0:T(8,128)(2,1)S(1)}, bf16[512,1024]{1,0:T(8,128)(2,1)S(1)}, u32[]{:S(2)}, u32[]{:S(2)}) collective-permute-start(bf16[512,1024]{1,0:T(8,128)(2,1)S(1)} %get-tuple-element.21.own), channel_id=1, source_target_pairs={{0,4},{4,0},{8,12},{12,8},{16,20},{20,16},{24,28},{28,24},{1,5},{5... | collective-permute-start | bytes 3145736 | tf_op jit(solution)/shard_map/ppermute | solution.py:40
  5.7 18.8 %collective-permute-start.1 = (bf16[512,640]{1,0:T(8,128)(2,1)S(1)}, bf16[512,640]{1,0:T(8,128)(2,1)S(1)}, u32[]{:S(2)}, u32[]{:S(2)}) collective-permute-start(bf16[512,640]{1,0:T(8,128)(2,1)S(1)} %get-tuple-element.22), channel_id=1, source_target_pairs={{8,0},{28,4},{16,8},{4,12},{24,16},{12,20},{0,24},{20,28},{9,1},{2... | collective-permute-start | bytes 1966088 | tf_op jit(solution)/shard_map/ppermute | solution.py:36
  9.3 18.0 %collective-permute-start.7 = (bf16[512,128]{1,0:T(8,128)(2,1)S(1)}, bf16[512,128]{1,0:T(8,128)(2,1)S(1)}, u32[]{:S(2)}, u32[]{:S(2)}) collective-permute-start(bf16[512,128]{1,0:T(8,128)(2,1)S(1)} %get-tuple-element.24), channel_id=1, source_target_pairs={{8,0},{28,4},{16,8},{4,12},{24,16},{12,20},{0,24},{20,28},{9,1},{2... | collective-permute-start | bytes 393224 | tf_op jit(solution)/shard_map/ppermute | solution.py:36
  9.7 41.1 %collective-permute-start.4 = (bf16[512,256]{1,0:T(8,128)(2,1)S(1)}, bf16[512,256]{1,0:T(8,128)(2,1)S(1)}, u32[]{:S(2)}, u32[]{:S(2)}) collective-permute-start(bf16[512,256]{1,0:T(8,128)(2,1)S(1)} %get-tuple-element.23), channel_id=1, source_target_pairs={{8,0},{28,4},{16,8},{4,12},{24,16},{12,20},{0,24},{20,28},{9,1},{2... | collective-permute-start | bytes 786440 | tf_op jit(solution)/shard_map/ppermute | solution.py:36
  10.2 56.7 %collective-permute-start.2 = (bf16[512,640]{1,0:T(8,128)(2,1)S(1)}, bf16[512,640]{1,0:T(8,128)(2,1)S(1)}, u32[]{:S(2)}, u32[]{:S(2)}) collective-permute-start(bf16[512,640]{1,0:T(8,128)(2,1)S(1)} %get-tuple-element.22), channel_id=1, source_target_pairs={{24,0},{12,4},{0,8},{20,12},{8,16},{28,20},{16,24},{4,28},{25,1},{... | collective-permute-start | bytes 1966088 | tf_op jit(solution)/shard_map/ppermute | solution.py:36
  24.4 42.5 %collective-permute-start.3 = (bf16[512,640]{1,0:T(8,128)(2,1)S(1)}, bf16[512,640]{1,0:T(8,128)(2,1)S(1)}, u32[]{:S(2)}, u32[]{:S(2)}) collective-permute-start(bf16[512,640]{1,0:T(8,128)(2,1)S(1)} %collective-permute-done.1.near.refs_1_.refs_0_), channel_id=1, source_target_pairs={{0,4},{4,0},{8,12},{12,8},{16,20},{20,16},{24,28},{28,24},{1,5},{5... | collective-permute-start | bytes 1966088 | tf_op jit(solution)/shard_map/ppermute | solution.py:40
  27.2 21.9 %collective-permute-start.8 = (bf16[512,128]{1,0:T(8,128)(2,1)S(1)}, bf16[512,128]{1,0:T(8,128)(2,1)S(1)}, u32[]{:S(2)}, u32[]{:S(2)}) collective-permute-start(bf16[512,128]{1,0:T(8,128)(2,1)S(1)} %get-tuple-element.24), channel_id=1, source_target_pairs={{24,0},{12,4},{0,8},{20,12},{8,16},{28,20},{16,24},{4,28},{25,1},{... | collective-permute-start | bytes 393224 | tf_op jit(solution)/shard_map/ppermute | solution.py:36
  49.1 13.6 %collective-permute-start.5 = (bf16[512,256]{1,0:T(8,128)(2,1)S(1)}, bf16[512,256]{1,0:T(8,128)(2,1)S(1)}, u32[]{:S(2)}, u32[]{:S(2)}) collective-permute-start(bf16[512,256]{1,0:T(8,128)(2,1)S(1)} %get-tuple-element.23), channel_id=1, source_target_pairs={{24,0},{12,4},{0,8},{20,12},{8,16},{28,20},{16,24},{4,28},{25,1},{... | collective-permute-start | bytes 786440 | tf_op jit(solution)/shard_map/ppermute | solution.py:36
  50.8 12.0 %collective-permute-start.6 = (bf16[512,256]{1,0:T(8,128)(2,1)S(1)}, bf16[512,256]{1,0:T(8,128)(2,1)S(1)}, u32[]{:S(2)}, u32[]{:S(2)}) collective-permute-start(bf16[512,256]{1,0:T(8,128)(2,1)S(1)} %collective-permute-done.4.near.refs_2_.refs_1_), channel_id=1, source_target_pairs={{0,4},{4,0},{8,12},{12,8},{16,20},{20,16},{24,28},{28,24},{1,5},{5... | collective-permute-start | bytes 786440 | tf_op jit(solution)/shard_map/ppermute | solution.py:40
  51.1 9.3 %collective-permute-start.9 = (bf16[512,128]{1,0:T(8,128)(2,1)S(1)}, bf16[512,128]{1,0:T(8,128)(2,1)S(1)}, u32[]{:S(2)}, u32[]{:S(2)}) collective-permute-start(bf16[512,128]{1,0:T(8,128)(2,1)S(1)} %collective-permute-done.7.near.refs_3_.refs_2_), channel_id=1, source_target_pairs={{0,4},{4,0},{8,12},{12,8},{16,20},{20,16},{24,28},{28,24},{1,5},{5... | collective-permute-start | bytes 393224 | tf_op jit(solution)/shard_map/ppermute | solution.py:40
  69.7 3.8 %collective-permute-start.10 = (f32[4,1024]{1,0:T(4,128)S(1)}, f32[4,1024]{1,0:T(4,128)S(1)}, u32[]{:S(2)}, u32[]{:S(2)}) collective-permute-start(f32[4,1024]{1,0:T(4,128)S(1)} %pad_maximum_fusion), channel_id=1, source_target_pairs={{0,4},{4,0},{8,12},{12,8},{16,20},{20,16},{24,28},{28,24},{1,5},{5... | collective-permute-start | bytes 49160 | tf_op jit(solution)/shard_map/ppermute | solution.py:40
  73.5 4.3 %collective-permute-start.11 = (f32[4,1024]{1,0:T(4,128)S(1)}, f32[4,1024]{1,0:T(4,128)S(1)}, u32[]{:S(2)}, u32[]{:S(2)}) collective-permute-start(f32[4,1024]{1,0:T(4,128)S(1)} %fusion.4), channel_id=1, source_target_pairs={{0,8},{4,12},{8,0},{12,4},{16,24},{20,28},{24,16},{28,20},{1,9},{5... | collective-permute-start | bytes 49160 | tf_op jit(solution)/shard_map/ppermute | solution.py:40
  77.8 4.6 %collective-permute-start.12 = (f32[4,1024]{1,0:T(4,128)S(1)}, f32[4,1024]{1,0:T(4,128)S(1)}, u32[]{:S(2)}, u32[]{:S(2)}) collective-permute-start(f32[4,1024]{1,0:T(4,128)S(1)} %add.22), channel_id=1, source_target_pairs={{0,16},{4,20},{8,24},{12,28},{16,0},{20,4},{24,8},{28,12},{1,17},{... | collective-permute-start | bytes 49160 | tf_op jit(solution)/shard_map/ppermute | solution.py:40
  85.8 13.2 %collective-permute-start.15 = (f32[2,2,128,512]{3,2,1,0:T(8,128)S(1)}, f32[2,2,128,512]{3,2,1,0:T(8,128)S(1)}, u32[]{:S(2)}, u32[]{:S(2)}) collective-permute-start(f32[2,2,128,512]{3,2,1,0:T(8,128)S(1)} %shard_map.84), channel_id=1, source_target_pairs={{0,1},{1,0},{2,3},{3,2},{4,5},{5,4},{6,7},{7,6},{8,9},{9,8},{10,11... | collective-permute-start | bytes 3145736 | tf_op jit(solution)/shard_map/ppermute | solution.py:40
  86.6 2.6 %collective-permute-start.20 = (f32[2,128,512]{2,1,0:T(8,128)S(1)}, f32[2,128,512]{2,1,0:T(8,128)S(1)}, u32[]{:S(2)}, u32[]{:S(2)}) collective-permute-start(f32[2,128,512]{2,1,0:T(8,128)S(1)} %shard_map.86.earlier_ref), channel_id=1, source_target_pairs={{0,1},{1,0},{2,3},{3,2},{4,5},{5,4},{6,7},{7,6},{8,9},{9,8},{10,11... | collective-permute-start | bytes 1572872 | tf_op jit(solution)/shard_map/ppermute | solution.py:40
  87.5 3.9 %collective-permute-start.17 = (f32[2,128,512]{2,1,0:T(8,128)S(1)}, f32[2,128,512]{2,1,0:T(8,128)S(1)}, u32[]{:S(2)}, u32[]{:S(2)}) collective-permute-start(f32[2,128,512]{2,1,0:T(8,128)S(1)} %shard_map.87), channel_id=1, source_target_pairs={{0,1},{1,0},{2,3},{3,2},{4,5},{5,4},{6,7},{7,6},{8,9},{9,8},{10,11... | collective-permute-start | bytes 1572872 | tf_op jit(solution)/shard_map/ppermute | solution.py:40
  87.8 4.7 %collective-permute-start.13 = (f32[2,128,512]{2,1,0:T(8,128)S(1)}, f32[2,128,512]{2,1,0:T(8,128)S(1)}, u32[]{:S(2)}, u32[]{:S(2)}) collective-permute-start(f32[2,128,512]{2,1,0:T(8,128)S(1)} %shard_map.82.earlier_ref), channel_id=1, source_target_pairs={{0,1},{1,0},{2,3},{3,2},{4,5},{5,4},{6,7},{7,6},{8,9},{9,8},{10,11... | collective-permute-start | bytes 1572872 | tf_op jit(solution)/shard_map/ppermute | solution.py:40
  89.8 6.4 %collective-permute-start.21 = (bf16[1,128,512]{2,1,0:T(8,128)(2,1)S(1)}, bf16[1,128,512]{2,1,0:T(8,128)(2,1)S(1)}, u32[]{:S(2)}, u32[]{:S(2)}) collective-permute-start(bf16[1,128,512]{2,1,0:T(8,128)(2,1)S(1)} %get-tuple-element.32), channel_id=1, source_target_pairs={{0,2},{1,3},{2,0},{3,1},{4,6},{5,7},{6,4},{7,5},{8,10},{9,11},{10,... | collective-permute-start | bytes 393224 | tf_op jit(solution)/shard_map/ppermute | solution.py:40
  91.9 9.4 %collective-permute-start.18 = (bf16[1,128,512]{2,1,0:T(8,128)(2,1)S(1)}, bf16[1,128,512]{2,1,0:T(8,128)(2,1)S(1)}, u32[]{:S(2)}, u32[]{:S(2)}) collective-permute-start(bf16[1,128,512]{2,1,0:T(8,128)(2,1)S(1)} %get-tuple-element.30), channel_id=1, source_target_pairs={{0,2},{1,3},{2,0},{3,1},{4,6},{5,7},{6,4},{7,5},{8,10},{9,11},{10,... | collective-permute-start | bytes 393224 | tf_op jit(solution)/shard_map/ppermute | solution.py:40
  93.3 9.8 %collective-permute-start.14 = (bf16[1,128,640]{2,1,0:T(8,128)(2,1)S(1)}, bf16[1,128,640]{2,1,0:T(8,128)(2,1)S(1)}, u32[]{:S(2)}, u32[]{:S(2)}) collective-permute-start(bf16[1,128,640]{2,1,0:T(8,128)(2,1)S(1)} %get-tuple-element.26), channel_id=1, source_target_pairs={{0,2},{1,3},{2,0},{3,1},{4,6},{5,7},{6,4},{7,5},{8,10},{9,11},{10,... | collective-permute-start | bytes 491528 | tf_op jit(solution)/shard_map/ppermute | solution.py:40
  96.3 6.8 %collective-permute-start.22 = (bf16[128,512]{1,0:T(8,128)(2,1)S(1)}, bf16[128,512]{1,0:T(8,128)(2,1)S(1)}, u32[]{:S(2)}, u32[]{:S(2)}) collective-permute-start(bf16[128,512]{1,0:T(8,128)(2,1)S(1)} %fusion.1), channel_id=1, source_target_pairs={{8,0},{12,4},{16,8},{20,12},{24,16},{28,20},{0,24},{4,28},{9,1},{1... | collective-permute-start | bytes 393224 | tf_op jit(solution)/shard_map/ppermute | solution.py:30
  99.8 7.5 %collective-permute-start.16 = (bf16[2,1,128,512]{3,2,1,0:T(8,128)(2,1)S(1)}, bf16[2,1,128,512]{3,2,1,0:T(8,128)(2,1)S(1)}, u32[]{:S(2)}, u32[]{:S(2)}) collective-permute-start(bf16[2,1,128,512]{3,2,1,0:T(8,128)(2,1)S(1)} %get-tuple-element.28), channel_id=1, source_target_pairs={{0,2},{1,3},{2,0},{3,1},{4,6},{5,7},{6,4},{7,5},{8,10},{9,11},{10,... | collective-permute-start | bytes 786440 | tf_op jit(solution)/shard_map/ppermute | solution.py:40
  101.4 5.0 %collective-permute-start.19 = (bf16[128,512]{1,0:T(8,128)(2,1)S(1)}, bf16[128,512]{1,0:T(8,128)(2,1)S(1)}, u32[]{:S(2)}, u32[]{:S(2)}) collective-permute-start(bf16[128,512]{1,0:T(8,128)(2,1)S(1)} %fusion), channel_id=1, source_target_pairs={{4,0},{8,4},{12,8},{16,12},{20,16},{24,20},{28,24},{0,28},{5,1},{9... | collective-permute-start | bytes 393224 | tf_op jit(solution)/shard_map/ppermute | solution.py:30
  (7 other events, 57.2 us)

commit v2 on v1

--- a/solution.py
+++ b/solution.py
@@ -82,15 +82,18 @@
     return lax.axis_index("row") % 2, col % 2, (col // 2) % 2
 
 
-def mask_kernel(sb, gb, screen_ref, basis_ref, own_ref, *rest):
-    chunk_refs, (tile_ref, sems) = rest[:-2], rest[-2:]
+def mask_kernel(sb, gb, screen_hbm, basis_ref, own_ref, *rest):
+    chunk_refs, (screen_ref, tile_ref, sem, sems) = rest[:-4], rest[-4:]
     row_count, _ = own_ref.shape
+    screen_copy = pltpu.make_async_copy(screen_hbm, screen_ref, sem)
+    screen_copy.start()
     copies = []
     for row in range(row_count // sb):
         window = pl.ds(row * sb, sb)
         copy = pltpu.make_async_copy(basis_ref.at[0, window], tile_ref.at[window], sems.at[row])
         copy.start()
         copies.append(copy)
+    screen_copy.wait()
     for row, copy in enumerate(copies):
         rows = slice(row * sb, (row + 1) * sb)
         copy.wait()
@@ -127,110 +130,90 @@
     )
 
 
-def sums_kernel(sb, gb, first, screen_ref, high_ref, low_ref, partial_ref, far, across, basis_ref,
-                sums_ref, total_ref):
+def later_kernel(high_ref, low_ref, partial_ref, across, total_ref):
     sign = 1 - 2 * position()[0]
-    total_ref[...] = (
-        partial_ref[...]
-        + both(high_ref, low_ref, REACH - 2 * sign, far[...])
-        + both(high_ref, low_ref, REACH - sign, across[...])
-    )
-    components, row_count, width = basis_ref.shape[0], far.shape[0], far.shape[1]
-    for part in range(width // gb):
-        cols = slice(part * gb, (part + 1) * gb)
-        source = slice((first + part) * gb, (first + part + 1) * gb)
-        found = [jnp.zeros((1, gb), F32) for _ in range(components)]
-        for row in range(row_count // sb):
-            rows = slice(row * sb, (row + 1) * sb)
-            keep = screen_ref[row, first + part].astype(F32)
-            applied = total_ref[rows, cols]
-            for c in range(components):
-                product = basis_ref[c, rows, source].astype(F32) * applied
-                found[c] += keep * jnp.sum(product, axis=0, keepdims=True)
-        for c in range(components):
-            sums_ref[c : c + 1, cols] = found[c]
-
-
-def half_kernel(sb, gb, screen_ref, basis_ref, parts_ref, half_ref):
+    total_ref[...] = partial_ref[...] + both(high_ref, low_ref, REACH - sign, across[...])
+
+
+def sums_kernel(start, high_ref, low_ref, partial_ref, far, masked_ref, sums_ref, total_ref):
+    sign = 1 - 2 * position()[0]
+    width = far.shape[1]
+    total_ref[...] = partial_ref[...] + both(high_ref, low_ref, REACH - 2 * sign, far[...])
+    for c in range(masked_ref.shape[0]):
+        product = masked_ref[c, :, start : start + width] * total_ref[...]
+        sums_ref[c : c + 1, :] = jnp.sum(product, axis=0, keepdims=True)
+
+
+def widen_kernel(sb, gb, screen_ref, basis_ref, masked_ref):
     components, row_count, points = basis_ref.shape
     for part in range(points // gb):
         cols = slice(part * gb, (part + 1) * gb)
         for row in range(row_count // sb):
             rows = slice(row * sb, (row + 1) * sb)
             keep = screen_ref[row, part].astype(F32)
-            total = (parts_ref[0:1, cols] * keep) * basis_ref[0, rows, cols].astype(F32)
+            for c in range(components):
+                masked_ref[c, rows, cols] = basis_ref[c, rows, cols].astype(F32) * keep
+
+
+def half_kernel(masked_ref, parts_ref, half_ref):
+    components, row_count, points = masked_ref.shape
+    for start in range(0, points, 128):
+        cols = slice(start, start + 128)
+        for row in range(0, row_count, 128):
+            rows = slice(row, row + 128)
+            total = parts_ref[0:1, cols] * masked_ref[0, rows, cols]
             for c in range(1, components):
-                total += (parts_ref[c : c + 1, cols] * keep) * basis_ref[c, rows, cols].astype(F32)
+                total += parts_ref[c : c + 1, cols] * masked_ref[c, rows, cols]
             half_ref[rows, cols] = total.astype(BF16)
 
 
-def rows_of(ref, cols, side, share, count):
+def sorted_kernel(chunks, beside, *refs):
+    near, far, across = (refs[i * chunks : (i + 1) * chunks] for i in range(3))
+    ahead_ref, behind_ref = refs[3 * chunks :]
+
+    def fill(here_ref, there_ref):
+        here_ref[0] = beside[...]
+        start = 0
+        for one, two, three in zip(near, across, far):
+            cols = slice(start, start + one.shape[1])
+            here_ref[1, :, cols] = one[...]
+            there_ref[0, :, cols] = two[...]
+            there_ref[1, :, cols] = three[...]
+            start += one.shape[1]
+
+    odd = position()[0]
+
+    @pl.when(odd == 0)
+    def _():
+        fill(ahead_ref, behind_ref)
+
+    @pl.when(odd != 0)
+    def _():
+        fill(behind_ref, ahead_ref)
+
+
+def rows_of(ref, side, share, count):
     blocks = []
     for step in range(count):
         window = pl.ds(pl.multiple_of((2 * step + side) * share, share), share)
-        blocks.append(ref[window, cols])
+        blocks.append(ref[window, :])
     return jnp.concatenate(blocks, axis=0) if count > 1 else blocks[0]
 
 
-def pieces(blocks):
-    start = 0
-    for block in blocks:
-        width = block.shape[1]
-        yield slice(start, start + width), block
-        start += width
-
-
-def mirrored_product(half_ref, blocks, side, share, count):
-    total = 0
-    for cols, block in pieces(blocks):
-        left = rows_of(block, slice(None), side, share, count)
-        total += dot_rows(left, half_ref[:, cols])
+def mirrored_product(half_ref, block, side, share, count):
+    total = dot_rows(rows_of(block, side, share, count), half_ref[...])
     return total.reshape(count, share, half_ref.shape[0])
 
 
 def central_product(half_ref, own, side, share, count):
-    cols = slice(None)
-    total = dot_rows(rows_of(own, cols, side, share, count), half_ref[...])
-    total += dot_rows(rows_of(half_ref, cols, side, share, count), own[...])
+    total = dot_rows(rows_of(own, side, share, count), half_ref[...])
+    total += dot_rows(rows_of(half_ref, side, share, count), own[...])
     return total.reshape(count, share, half_ref.shape[0])
 
 
-def direct_product(half_ref, blocks, side, share, count):
-    total = 0
-    for cols, block in pieces(blocks):
-        total += dot_rows(rows_of(half_ref, cols, side, share, count), block[...])
+def direct_product(half_ref, block, side, share, count):
+    total = dot_rows(rows_of(half_ref, side, share, count), block[...])
     return total.reshape(count, share, half_ref.shape[0])
-
-
-def neighbours(refs, chunks):
-    beside, near = refs[:1], refs[1 : 1 + chunks]
-    far, across = refs[1 + chunks : 1 + 2 * chunks], refs[1 + 2 * chunks : 1 + 3 * chunks]
-    return (beside, near), (across, far)
-
-
-def behind(first, second, run):
-    odd = position()[0]
-
-    @pl.when(odd != 0)
-    def _():
-        run(first)
-
-    @pl.when(odd == 0)
-    def _():
-        run(second)
-
-
-def on_side(refs, chunks, ahead, run):
-    first, second = neighbours(refs, chunks)
-    odd = position()[0]
-
-    @pl.when(odd == (0 if ahead else 1))
-    def _():
-        run(*first)
-
-    @pl.when(odd == (1 if ahead else 0))
-    def _():
-        run(*second)
 
 
 def deposit(total, side, keep_ref, send_ref):
@@ -240,40 +223,25 @@
         send_ref[..., step, :, :] = jnp.where(side == 0, high, low).astype(send_ref.dtype)
 
 
-def mirrored_other_kernel(share, count, cut, half_ref, earlier_ref, *refs):
-    first, second, out = refs[:cut], refs[cut:-1], refs[-1]
+def mirrored_other_kernel(share, count, k, half_ref, earlier_ref, behind_ref, out):
     side = 1 - position()[1]
-
-    def run(blocks):
-        out[...] = mirrored_product(half_ref, blocks, side, share, count)
-
-    behind(first, second, run)
-
-
-def mirrored_own_kernel(share, count, cut, half_ref, found_ref, *refs):
-    first, second, keep_ref, send_ref = refs[:cut], refs[cut:-2], refs[-2], refs[-1]
+    out[...] = mirrored_product(half_ref, behind_ref.at[k], side, share, count)
+
+
+def mirrored_own_kernel(share, count, k, half_ref, found_ref, behind_ref, keep_ref, send_ref):
     _, core, side = position()
-
-    def run(blocks):
-        total = mirrored_product(half_ref, blocks, core, share, count)
-        deposit(total + found_ref[...], side, keep_ref, send_ref)
-
-    behind(first, second, run)
-
-
-def central_other_kernel(share, count, half_ref, own, out):
+    total = mirrored_product(half_ref, behind_ref.at[k], core, share, count)
+    deposit(total + found_ref[...], side, keep_ref, send_ref)
+
+
+def central_other_kernel(share, count, half_ref, own, earlier_ref, out):
     out[...] = central_product(half_ref, own, 1 - position()[1], share, count)
 
 
-def direct_other_kernel(share, count, chunks, half_ref, earlier_ref, *refs):
-    refs, out = refs[:-1], refs[-1]
+def direct_other_kernel(share, count, half_ref, earlier_ref, ahead_ref, out):
     side = 1 - position()[1]
-
-    def run(one, two):
-        out[0] = direct_product(half_ref, one, side, share, count)
-        out[1] = direct_product(half_ref, two, side, share, count)
-
-    on_side(refs, chunks, True, run)
+    for k in range(REACH):
+        out[k] = direct_product(half_ref, ahead_ref.at[k], side, share, count)
 
 
 def central_own_kernel(share, count, half_ref, own, found_ref, keep_ref, send_ref):
@@ -297,16 +265,11 @@
                 send_ref[step, :, size:] = rest.astype(BF16)
 
 
-def direct_own_kernel(share, count, chunks, half_ref, found_ref, earlier_ref, *refs):
-    refs, keep_ref, send_ref = refs[:-2], refs[-2], refs[-1]
+def direct_own_kernel(share, count, half_ref, found_ref, earlier_ref, ahead_ref, keep_ref, send_ref):
     _, core, side = position()
-
-    def run(one, two):
-        for k, blocks in enumerate((one, two)):
-            total = direct_product(half_ref, blocks, core, share, count) + found_ref[k]
-            deposit(total, side, keep_ref.at[k], send_ref.at[k])
-
-    on_side(refs, chunks, True, run)
+    for k in range(REACH):
+        total = direct_product(half_ref, ahead_ref.at[k], core, share, count) + found_ref[k]
+        deposit(total, side, keep_ref.at[k], send_ref.at[k])
 
 
 def joined_kernel(share, central_ref, found_ref, keep_ref, direct_ref, out_ref):
@@ -354,12 +317,14 @@
     own, *mine = call(
         functools.partial(mask_kernel, sb, gb),
         [shape((row_count, width), BF16) for width in (points, *widths)],
-        [SCALARS, pl.BlockSpec(memory_space=pltpu.HBM)], row_count * points, 6 * row_count * points,
+        [pl.BlockSpec(memory_space=pltpu.HBM)] * 2, row_count * points, 6 * row_count * points,
         scratch=[
+            pltpu.SMEM(screen.shape, jnp.int32),
             pltpu.VMEM((row_count, points), BF16),
+            pltpu.SemaphoreType.DMA,
             pltpu.SemaphoreType.DMA((screen.shape[0],)),
         ],
-    )(screen, pltpu.with_memory_space_constraint(basis_values, pltpu.HBM))
+    )(pltpu.with_memory_space_constraint(screen, pltpu.HBM), pltpu.with_memory_space_constraint(basis_values, pltpu.HBM))
     near, far, across = [], [], []
     for chunk, block in enumerate(mine):
         near.append(from_side(block, 2))
@@ -371,23 +336,37 @@
         split_kernel, [shape((BAND, row_count, row_count), BF16)] * 2, [WHOLE],
         density.size * 4, density.size * 8,
     )(density)
+    masked = call(
+        functools.partial(widen_kernel, sb, gb), shape(basis_values.shape), [SCALARS, WHOLE],
+        basis_values.size, 6 * basis_values.size,
+    )(screen, basis_values)
     sums, first = [], 0
     for chunk, width in enumerate(widths):
+        total = shape((row_count, width))
         partial = call(
-            functools.partial(early_kernel, first), shape((row_count, width)), [WHOLE] * 5,
+            functools.partial(early_kernel, first), total, [WHOLE] * 5,
             6 * square * width, 10 * square,
         )(high, low, own, beside, near[chunk])
+        partial = call(later_kernel, total, [WHOLE] * 4, 2 * square * width, 4 * square)(
+            high, low, partial, across[chunk]
+        )
         found = call(
-            functools.partial(sums_kernel, sb, gb, first // gb), shape((components, width)),
-            [SCALARS] + [WHOLE] * 6, 4 * square * width, 6 * square,
+            functools.partial(sums_kernel, first), shape((components, width)),
+            [WHOLE] * 5, 2 * square * width, 6 * square,
             scratch=[pltpu.VMEM((row_count, width), F32)],
-        )(screen, high, low, partial, far[chunk], across[chunk], basis_values)
+        )(high, low, partial, far[chunk], masked)
         sums.append(found)
         first += width
+    ahead, behind = call(
+        functools.partial(sorted_kernel, chunks),
+        [shape((REACH, row_count, points), BF16)] * 2, [WHOLE] * (1 + 3 * chunks),
+        row_count * points, 16 * row_count * points,
+    )(beside, *near, *far, *across)
     summed = jnp.concatenate(sums, axis=1)
     bit = 1
     while bit < rows:
-        summed = summed + swap(summed, "row", bit)
+        found = swap(summed, "row", bit)
+        summed = summed + found
         bit *= 2
 
     point_density = summed[0]
@@ -405,40 +384,36 @@
     vector_part = 2.0 * weights * gradient_pot * gradient
     parts = jnp.concatenate([scalar_part[None], vector_part], axis=0)
     half = call(
-        functools.partial(half_kernel, sb, gb), shape((row_count, points), BF16),
-        [SCALARS, WHOLE, WHOLE], 8 * basis_values.size, 2 * basis_values.size,
-    )(screen, basis_values, parts)
-
-    beyond = (beside, *near, *far, *across)
-    paired = {1: ((beside,), across), 2: (near, far)}
+        half_kernel, shape((row_count, points), BF16), [WHOLE] * 2,
+        8 * basis_values.size, 4 * basis_values.size,
+    )(masked, parts)
+
     product = 2 * row_count * points * share * count
     kept = count // 2
     block = (count, share, row_count)
     mirrored_found, earlier = {}, half
     for k in (2, 1):
-        first, second = paired[k]
         earlier = call(
-            functools.partial(mirrored_other_kernel, share, count, len(first)), shape(block),
-            [WHOLE, ANYWHERE] + [WHOLE] * len((*first, *second)), product, 3 * half.size,
-        )(half, earlier, *first, *second)
+            functools.partial(mirrored_other_kernel, share, count, k - 1), shape(block),
+            [WHOLE, ANYWHERE, WHOLE], product, 3 * half.size,
+        )(half, earlier, behind)
         mirrored_found[k] = swap(earlier, "col", 1)
     central_other = call(
         functools.partial(central_other_kernel, share, count), shape(block),
-        [WHOLE] * 2, 2 * product, 4 * half.size,
-    )(half, own)
+        [WHOLE] * 2 + [ANYWHERE], 2 * product, 4 * half.size,
+    )(half, own, earlier)
     central_found = swap(central_other, "col", 1)
     mirrored_keep, mirrored_send = {}, {}
     for k in (2, 1):
-        first, second = paired[k]
         mirrored_keep[k], mirrored_send[k] = call(
-            functools.partial(mirrored_own_kernel, share, count, len(first)),
+            functools.partial(mirrored_own_kernel, share, count, k - 1),
             [shape((kept, share, row_count)), shape((kept, share, row_count), BF16)],
-            [WHOLE] * len((half, half, *first, *second)), product, 4 * half.size,
-        )(half, mirrored_found[k], *first, *second)
+            [WHOLE] * 3, product, 4 * half.size,
+        )(half, mirrored_found[k], behind)
     direct_other = call(
-        functools.partial(direct_other_kernel, share, count, chunks), shape((REACH, *block)),
-        [WHOLE, ANYWHERE] + [WHOLE] * len(beyond), product * 2, 4 * half.size,
-    )(half, central_other, *beyond)
+        functools.partial(direct_other_kernel, share, count), shape((REACH, *block)),
+        [WHOLE, ANYWHERE, WHOLE], product * 2, 4 * half.size,
+    )(half, central_other, ahead)
     direct_found = swap(direct_other, "col", 1)
     spare = max(share, 128)
     central_keep, central_send = call(
@@ -451,13 +426,13 @@
     )(half, own, central_found)
     central_found = swap(central_send, "col", 2)
     direct_keep, direct_send = call(
-        functools.partial(direct_own_kernel, share, count, chunks),
+        functools.partial(direct_own_kernel, share, count),
         [
             shape((REACH, kept, share, row_count)),
             shape((REACH, kept, share, row_count), BF16),
         ],
-        [WHOLE] * 2 + [ANYWHERE] + [WHOLE] * len(beyond), product * 2, 4 * half.size,
-    )(half, direct_found, central_keep, *beyond)
+        [WHOLE] * 2 + [ANYWHERE, WHOLE], product * 2, 4 * half.size,
+    )(half, direct_found, central_keep, ahead)
 
     def scatter(total, axis):
         bit = 4

time: 109 us -> 103 us (0.945)
  local copies, waits for them, and re-layouts: 3.22 us -> 0.04 us
  waiting for transfers between devices: 53 us -> 50.5 us
    ppermute x6, waiting for transfers between devices: 36 us -> 24.3 us  [from_side(): return lax.ppermute(block, 'row', route)]
    ppermute x15, waiting for transfers between devices: 13.7 us -> 23.1 us  [swap(): lax.ppermute(block, axis, [(i, i ^ bit) for i in range(lax.axis_size(axis...]
    unnamed x16, local copies, waits for them, and re-layouts: 3.22 us -> 0.04 us
    pallas_call x13 -> x18, Pallas kernels: 15.7 us -> 15.7 us  [the longest x3 4.63 us: body(): call(functools.partial(early_kernel, first), total, [WHOLE] * 5, 6 * squa...]
  transfers between devices with their start and end apart: 23 -> 23, of which waited for: 11 -> 11; matrix products, arithmetic and copies ran while one was open for 0% -> 0% of each run, Pallas kernels for 11% -> 13%
where the time goes in v2:
time: 103 us
  waiting for transfers between devices  50.5 us (49%)
  starting transfers between devices  31.5 us (31%)
  Pallas kernels  20.4 us (20%)
    ppermute x6, waiting for transfers between devices, from_side(): return lax.ppermute(block, 'row', route)  24.3 us
    ppermute x15, waiting for transfers between devices, swap(): lax.ppermute(block, axis, [(i, i ^ bit) for i in range(lax.axis_size(axis...  23.1 us
    ppermute x15, starting transfers between devices, swap(): lax.ppermute(block, axis, [(i, i ^ bit) for i in range(lax.axis_size(axis...  18.6 us
    ppermute x6, starting transfers between devices, from_side(): return lax.ppermute(block, 'row', route)  8.16 us
    ppermute x2, starting transfers between devices, from_ahead(): lax.ppermute(block, 'row', [((i + distance) % size, i) for i in range(siz...  4.68 us
    pallas_call x3, Pallas kernels, body(): call(functools.partial(early_kernel, first), total, [WHOLE] * 5, 6 * squa...  4.63 us
    ppermute x2, waiting for transfers between devices, from_ahead(): lax.ppermute(block, 'row', [((i + distance) % size, i) for i in range(siz...  3.13 us
    pallas_call x3, Pallas kernels, body(): call(functools.partial(sums_kernel, first), shape((components, width)), [...  2.31 us
  transfers between devices with their start and end apart: 23, of which 11 were waited for; matrix products, arithmetic and copies ran while one was open for 0% of the time, Pallas kernels for 13%

profile of v2, /device:TPU:0, one launch (start us, length us, event | category | flops | bytes accessed | tf_op | source)
XLA Modules:
  0.0 103.1 jit_solution(6696107809623173860)
XLA Ops:
  0.0 1.5 %shard_map.75 = (bf16[512,1024]{1,0:T(8,128)(2,1)S(1)}, bf16[512,640]{1,0:T(8,128)(2,1)S(1)}, bf16[512,256]{1,0:T(8,128)(2,1)S(1)}, bf16[512,128]{1,0:T(8,128)(2,1)S(1)}) custom-call(s32[4,8]{1,0:T(4,128)} %screen_hbm.1, bf16[4,512,1024]{2,1,0:T(8,128)(2,1)} %basis_ref.3), custom_call_target="tpu_custom_call" | custom-call | flops 524288 | bytes 3145728 | tf_op jit(solution)/shard_map/pallas_call | solution.py:317
  1.5 3.1 %collective-permute-start = (bf16[512,1024]{1,0:T(8,128)(2,1)S(1)}, bf16[512,1024]{1,0:T(8,128)(2,1)S(1)}, u32[]{:S(2)}, u32[]{:S(2)}) collective-permute-start(bf16[512,1024]{1,0:T(8,128)(2,1)S(1)} %get-tuple-element.23.own), channel_id=1, source_target_pairs={{0,4},{4,0},{8,12},{12,8},{16,20},{20,16},{24,28},{28,24},{1,5},{5... | collective-permute-start | bytes 3145736 | tf_op jit(solution)/shard_map/ppermute | solution.py:40
  4.6 3.6 %collective-permute-start.1 = (bf16[512,640]{1,0:T(8,128)(2,1)S(1)}, bf16[512,640]{1,0:T(8,128)(2,1)S(1)}, u32[]{:S(2)}, u32[]{:S(2)}) collective-permute-start(bf16[512,640]{1,0:T(8,128)(2,1)S(1)} %get-tuple-element.24), channel_id=1, source_target_pairs={{8,0},{28,4},{16,8},{4,12},{24,16},{12,20},{0,24},{20,28},{9,1},{2... | collective-permute-start | bytes 1966088 | tf_op jit(solution)/shard_map/ppermute | solution.py:36
  9.1 14.2 %collective-permute-done.1.near.refs_0_ = bf16[512,640]{1,0:T(8,128)(2,1)S(1)} collective-permute-done((bf16[512,640]{1,0:T(8,128)(2,1)S(1)}, bf16[512,640]{1,0:T(8,128)(2,1)S(1)}, u32[]{:S(2)}, u32[]{:S(2)}) %collective-permute-start.1) | collective-permute-done | bytes 655392 | tf_op jit(solution)/shard_map/ppermute | solution.py:36
  24.2 6.1 %collective-permute-done.7.near.refs_2_ = bf16[512,128]{1,0:T(8,128)(2,1)S(1)} collective-permute-done((bf16[512,128]{1,0:T(8,128)(2,1)S(1)}, bf16[512,128]{1,0:T(8,128)(2,1)S(1)}, u32[]{:S(2)}, u32[]{:S(2)}) %collective-permute-start.7) | collective-permute-done | bytes 131104 | tf_op jit(solution)/shard_map/ppermute | solution.py:36
  31.6 5.1 %collective-permute-start.5 = (bf16[512,256]{1,0:T(8,128)(2,1)S(1)}, bf16[512,256]{1,0:T(8,128)(2,1)S(1)}, u32[]{:S(2)}, u32[]{:S(2)}) collective-permute-start(bf16[512,256]{1,0:T(8,128)(2,1)S(1)} %collective-permute-done.4.near.refs_1_), channel_id=1, source_target_pairs={{0,4},{4,0},{8,12},{12,8},{16,20},{20,16},{24,28},{28,24},{1,5},{5... | collective-permute-start | bytes 786440 | tf_op jit(solution)/shard_map/ppermute | solution.py:40
  36.6 8.8 %collective-permute-done.8.across.refs_8_ = bf16[512,128]{1,0:T(8,128)(2,1)S(1)} collective-permute-done((bf16[512,128]{1,0:T(8,128)(2,1)S(1)}, bf16[512,128]{1,0:T(8,128)(2,1)S(1)}, u32[]{:S(2)}, u32[]{:S(2)}) %collective-permute-start.8) | collective-permute-done | bytes 131104 | tf_op jit(solution)/shard_map/ppermute | solution.py:40
  45.4 2.1 %collective-permute-start.6 = (bf16[512,256]{1,0:T(8,128)(2,1)S(1)}, bf16[512,256]{1,0:T(8,128)(2,1)S(1)}, u32[]{:S(2)}, u32[]{:S(2)}) collective-permute-start(bf16[512,256]{1,0:T(8,128)(2,1)S(1)} %get-tuple-element.25), channel_id=1, source_target_pairs={{24,0},{12,4},{0,8},{20,12},{8,16},{28,20},{16,24},{4,28},{25,1},{... | collective-permute-start | bytes 786440 | tf_op jit(solution)/shard_map/ppermute | solution.py:36
  47.5 1.6 %collective-permute-start.9 = (bf16[512,128]{1,0:T(8,128)(2,1)S(1)}, bf16[512,128]{1,0:T(8,128)(2,1)S(1)}, u32[]{:S(2)}, u32[]{:S(2)}) collective-permute-start(bf16[512,128]{1,0:T(8,128)(2,1)S(1)} %get-tuple-element.26), channel_id=1, source_target_pairs={{24,0},{12,4},{0,8},{20,12},{8,16},{28,20},{16,24},{4,28},{25,1},{... | collective-permute-start | bytes 393224 | tf_op jit(solution)/shard_map/ppermute | solution.py:36
  49.1 1.8 %shard_map.73.masked_ref = f32[4,512,1024]{2,1,0:T(8,128)S(1)} custom-call(s32[4,8]{1,0:T(4,128)S(1)} %copy-done.2, bf16[4,512,1024]{2,1,0:T(8,128)(2,1)S(1)} %copy-done.1), custom_call_target="tpu_custom_call" | custom-call | flops 2097152 | bytes 12582912 | tf_op jit(solution)/shard_map/pallas_call | solution.py:339
  53.1 4.0 %collective-permute-done.9.far.refs_5_ = bf16[512,128]{1,0:T(8,128)(2,1)S(1)} collective-permute-done((bf16[512,128]{1,0:T(8,128)(2,1)S(1)}, bf16[512,128]{1,0:T(8,128)(2,1)S(1)}, u32[]{:S(2)}, u32[]{:S(2)}) %collective-permute-start.9) | collective-permute-done | bytes 131104 | tf_op jit(solution)/shard_map/ppermute | solution.py:36
  59.6 2.7 %shard_map.76.partial_ref = f32[512,640]{1,0:T(8,128)S(1)} custom-call(bf16[5,512,512]{2,1,0:T(8,128)(2,1)S(1)} %get-tuple-element.21.high_ref, bf16[5,512,512]{2,1,0:T(8,128)(2,1)S(1)} %get-tuple-element.22.low_ref, bf16[512,1024]{1,0:T(8,128)(2,1)S(1)} %get-tuple-element.23.own, bf16[512,1024]{1,0:T(8,128)(2,1)S(1)} %collective-permute-done.beside, ...), custom_call_target="tpu_custom_call" | custom-call | flops 2013265920 | bytes 5242880 | tf_op jit(solution)/shard_map/pallas_call | solution.py:346
  63.3 1.3 %shard_map.78 = f32[4,640]{1,0:T(4,128)S(1)} custom-call(bf16[5,512,512]{2,1,0:T(8,128)(2,1)S(1)} %get-tuple-element.21.high_ref, bf16[5,512,512]{2,1,0:T(8,128)(2,1)S(1)} %get-tuple-element.22.low_ref, f32[512,640]{1,0:T(8,128)S(1)} %shard_map.77.partial_ref, bf16[512,640]{1,0:T(8,128)(2,1)S(1)} %collective-permute-done.3.far.refs_3_, ...), custom_call_target="tpu_custom_call" | custom-call | flops 671088640 | bytes 3145728 | tf_op jit(solution)/shard_map/pallas_call | solution.py:353
  65.2 3.2 %collective-permute-done.10 = f32[4,1024]{1,0:T(4,128)S(1)} collective-permute-done((f32[4,1024]{1,0:T(4,128)S(1)}, f32[4,1024]{1,0:T(4,128)S(1)}, u32[]{:S(2)}, u32[]{:S(2)}) %collective-permute-start.10) | collective-permute-done | bytes 16416 | tf_op jit(solution)/shard_map/ppermute | solution.py:40
  68.5 3.7 %collective-permute-done.11 = f32[4,1024]{1,0:T(4,128)S(1)} collective-permute-done((f32[4,1024]{1,0:T(4,128)S(1)}, f32[4,1024]{1,0:T(4,128)S(1)}, u32[]{:S(2)}, u32[]{:S(2)}) %collective-permute-start.11) | collective-permute-done | bytes 16416 | tf_op jit(solution)/shard_map/ppermute | solution.py:40
  74.4 2.5 %collective-permute-done.12 = f32[4,1024]{1,0:T(4,128)S(1)} collective-permute-done((f32[4,1024]{1,0:T(4,128)S(1)}, f32[4,1024]{1,0:T(4,128)S(1)}, u32[]{:S(2)}, u32[]{:S(2)}) %collective-permute-start.12) | collective-permute-done | bytes 16416 | tf_op jit(solution)/shard_map/ppermute | solution.py:40
  81.7 2.4 %collective-permute-done.20.found_ref = f32[2,128,512]{2,1,0:T(8,128)S(1)} collective-permute-done((f32[2,128,512]{2,1,0:T(8,128)S(1)}, f32[2,128,512]{2,1,0:T(8,128)S(1)}, u32[]{:S(2)}, u32[]{:S(2)}) %collective-permute-start.20) | collective-permute-done | bytes 524320 | tf_op jit(solution)/shard_map/ppermute | solution.py:40
  84.5 1.5 %collective-permute-start.21 = (bf16[1,128,512]{2,1,0:T(8,128)(2,1)S(1)}, bf16[1,128,512]{2,1,0:T(8,128)(2,1)S(1)}, u32[]{:S(2)}, u32[]{:S(2)}) collective-permute-start(bf16[1,128,512]{2,1,0:T(8,128)(2,1)S(1)} %get-tuple-element.36), channel_id=1, source_target_pairs={{0,2},{1,3},{2,0},{3,1},{4,6},{5,7},{6,4},{7,5},{8,10},{9,11},{10,... | collective-permute-start | bytes 393224 | tf_op jit(solution)/shard_map/ppermute | solution.py:40
  88.0 1.5 %collective-permute-start.14 = (bf16[1,128,640]{2,1,0:T(8,128)(2,1)S(1)}, bf16[1,128,640]{2,1,0:T(8,128)(2,1)S(1)}, u32[]{:S(2)}, u32[]{:S(2)}) collective-permute-start(bf16[1,128,640]{2,1,0:T(8,128)(2,1)S(1)} %get-tuple-element.29), channel_id=1, source_target_pairs={{0,2},{1,3},{2,0},{3,1},{4,6},{5,7},{6,4},{7,5},{8,10},{9,11},{10,... | collective-permute-start | bytes 491528 | tf_op jit(solution)/shard_map/ppermute | solution.py:40
  89.5 1.5 %collective-permute-done.21 = bf16[1,128,512]{2,1,0:T(8,128)(2,1)S(1)} collective-permute-done((bf16[1,128,512]{2,1,0:T(8,128)(2,1)S(1)}, bf16[1,128,512]{2,1,0:T(8,128)(2,1)S(1)}, u32[]{:S(2)}, u32[]{:S(2)}) %collective-permute-start.21) | collective-permute-done | bytes 131104 | tf_op jit(solution)/shard_map/ppermute | solution.py:40
  91.0 2.8 %collective-permute-start.22 = (bf16[128,512]{1,0:T(8,128)(2,1)S(1)}, bf16[128,512]{1,0:T(8,128)(2,1)S(1)}, u32[]{:S(2)}, u32[]{:S(2)}) collective-permute-start(bf16[128,512]{1,0:T(8,128)(2,1)S(1)} %fusion.1), channel_id=1, source_target_pairs={{8,0},{12,4},{16,8},{20,12},{24,16},{28,20},{0,24},{4,28},{9,1},{1... | collective-permute-start | bytes 393224 | tf_op jit(solution)/shard_map/ppermute | solution.py:30
  94.6 1.6 %collective-permute-start.16 = (bf16[2,1,128,512]{3,2,1,0:T(8,128)(2,1)S(1)}, bf16[2,1,128,512]{3,2,1,0:T(8,128)(2,1)S(1)}, u32[]{:S(2)}, u32[]{:S(2)}) collective-permute-start(bf16[2,1,128,512]{3,2,1,0:T(8,128)(2,1)S(1)} %get-tuple-element.32), channel_id=1, source_target_pairs={{0,2},{1,3},{2,0},{3,1},{4,6},{5,7},{6,4},{7,5},{8,10},{9,11},{10,... | collective-permute-start | bytes 786440 | tf_op jit(solution)/shard_map/ppermute | solution.py:40
  96.2 1.9 %collective-permute-start.19 = (bf16[128,512]{1,0:T(8,128)(2,1)S(1)}, bf16[128,512]{1,0:T(8,128)(2,1)S(1)}, u32[]{:S(2)}, u32[]{:S(2)}) collective-permute-start(bf16[128,512]{1,0:T(8,128)(2,1)S(1)} %fusion), channel_id=1, source_target_pairs={{4,0},{8,4},{12,8},{16,12},{20,16},{24,20},{28,24},{0,28},{5,1},{9... | collective-permute-start | bytes 393224 | tf_op jit(solution)/shard_map/ppermute | solution.py:30
  98.1 3.1 %collective-permute-done.19.refs_0_ = bf16[128,512]{1,0:T(8,128)(2,1)S(1)} collective-permute-done((bf16[128,512]{1,0:T(8,128)(2,1)S(1)}, bf16[128,512]{1,0:T(8,128)(2,1)S(1)}, u32[]{:S(2)}, u32[]{:S(2)}) %collective-permute-start.19) | collective-permute-done | bytes 131104 | tf_op jit(solution)/shard_map/ppermute | solution.py:30
  (74 shorter events, 21.3 us)
Async XLA Ops:
  0.0 73.6 %copy-start = (f32[64]{0:T(128)S(1)}, f32[64]{0:T(128)}, u32[]{:S(2)}) copy-start(f32[64]{0:T(128)} %param.11) | copy-start | bytes 772
  1.5 46.0 %collective-permute-start = (bf16[512,1024]{1,0:T(8,128)(2,1)S(1)}, bf16[512,1024]{1,0:T(8,128)(2,1)S(1)}, u32[]{:S(2)}, u32[]{:S(2)}) collective-permute-start(bf16[512,1024]{1,0:T(8,128)(2,1)S(1)} %get-tuple-element.23.own), channel_id=1, source_target_pairs={{0,4},{4,0},{8,12},{12,8},{16,20},{20,16},{24,28},{28,24},{1,5},{5... | collective-permute-start | bytes 3145736 | tf_op jit(solution)/shard_map/ppermute | solution.py:40
  4.6 18.7 %collective-permute-start.1 = (bf16[512,640]{1,0:T(8,128)(2,1)S(1)}, bf16[512,640]{1,0:T(8,128)(2,1)S(1)}, u32[]{:S(2)}, u32[]{:S(2)}) collective-permute-start(bf16[512,640]{1,0:T(8,128)(2,1)S(1)} %get-tuple-element.24), channel_id=1, source_target_pairs={{8,0},{28,4},{16,8},{4,12},{24,16},{12,20},{0,24},{20,28},{9,1},{2... | collective-permute-start | bytes 1966088 | tf_op jit(solution)/shard_map/ppermute | solution.py:36
  8.2 23.4 %collective-permute-start.4 = (bf16[512,256]{1,0:T(8,128)(2,1)S(1)}, bf16[512,256]{1,0:T(8,128)(2,1)S(1)}, u32[]{:S(2)}, u32[]{:S(2)}) collective-permute-start(bf16[512,256]{1,0:T(8,128)(2,1)S(1)} %get-tuple-element.25), channel_id=1, source_target_pairs={{8,0},{28,4},{16,8},{4,12},{24,16},{12,20},{0,24},{20,28},{9,1},{2... | collective-permute-start | bytes 786440 | tf_op jit(solution)/shard_map/ppermute | solution.py:36
  8.6 21.7 %collective-permute-start.7 = (bf16[512,128]{1,0:T(8,128)(2,1)S(1)}, bf16[512,128]{1,0:T(8,128)(2,1)S(1)}, u32[]{:S(2)}, u32[]{:S(2)}) collective-permute-start(bf16[512,128]{1,0:T(8,128)(2,1)S(1)} %get-tuple-element.26), channel_id=1, source_target_pairs={{8,0},{28,4},{16,8},{4,12},{24,16},{12,20},{0,24},{20,28},{9,1},{2... | collective-permute-start | bytes 393224 | tf_op jit(solution)/shard_map/ppermute | solution.py:36
  23.3 39.0 %collective-permute-start.2 = (bf16[512,640]{1,0:T(8,128)(2,1)S(1)}, bf16[512,640]{1,0:T(8,128)(2,1)S(1)}, u32[]{:S(2)}, u32[]{:S(2)}) collective-permute-start(bf16[512,640]{1,0:T(8,128)(2,1)S(1)} %collective-permute-done.1.near.refs_0_), channel_id=1, source_target_pairs={{0,4},{4,0},{8,12},{12,8},{16,20},{20,16},{24,28},{28,24},{1,5},{5... | collective-permute-start | bytes 1966088 | tf_op jit(solution)/shard_map/ppermute | solution.py:40
  30.3 15.1 %collective-permute-start.8 = (bf16[512,128]{1,0:T(8,128)(2,1)S(1)}, bf16[512,128]{1,0:T(8,128)(2,1)S(1)}, u32[]{:S(2)}, u32[]{:S(2)}) collective-permute-start(bf16[512,128]{1,0:T(8,128)(2,1)S(1)} %collective-permute-done.7.near.refs_2_), channel_id=1, source_target_pairs={{0,4},{4,0},{8,12},{12,8},{16,20},{20,16},{24,28},{28,24},{1,5},{5... | collective-permute-start | bytes 393224 | tf_op jit(solution)/shard_map/ppermute | solution.py:40
  31.5 31.7 %collective-permute-start.3 = (bf16[512,640]{1,0:T(8,128)(2,1)S(1)}, bf16[512,640]{1,0:T(8,128)(2,1)S(1)}, u32[]{:S(2)}, u32[]{:S(2)}) collective-permute-start(bf16[512,640]{1,0:T(8,128)(2,1)S(1)} %get-tuple-element.24), channel_id=1, source_target_pairs={{24,0},{12,4},{0,8},{20,12},{8,16},{28,20},{16,24},{4,28},{25,1},{... | collective-permute-start | bytes 1966088 | tf_op jit(solution)/shard_map/ppermute | solution.py:36
  31.6 27.0 %collective-permute-start.5 = (bf16[512,256]{1,0:T(8,128)(2,1)S(1)}, bf16[512,256]{1,0:T(8,128)(2,1)S(1)}, u32[]{:S(2)}, u32[]{:S(2)}) collective-permute-start(bf16[512,256]{1,0:T(8,128)(2,1)S(1)} %collective-permute-done.4.near.refs_1_), channel_id=1, source_target_pairs={{0,4},{4,0},{8,12},{12,8},{16,20},{20,16},{24,28},{28,24},{1,5},{5... | collective-permute-start | bytes 786440 | tf_op jit(solution)/shard_map/ppermute | solution.py:40
  45.4 13.6 %collective-permute-start.6 = (bf16[512,256]{1,0:T(8,128)(2,1)S(1)}, bf16[512,256]{1,0:T(8,128)(2,1)S(1)}, u32[]{:S(2)}, u32[]{:S(2)}) collective-permute-start(bf16[512,256]{1,0:T(8,128)(2,1)S(1)} %get-tuple-element.25), channel_id=1, source_target_pairs={{24,0},{12,4},{0,8},{20,12},{8,16},{28,20},{16,24},{4,28},{25,1},{... | collective-permute-start | bytes 786440 | tf_op jit(solution)/shard_map/ppermute | solution.py:36
  47.5 9.6 %collective-permute-start.9 = (bf16[512,128]{1,0:T(8,128)(2,1)S(1)}, bf16[512,128]{1,0:T(8,128)(2,1)S(1)}, u32[]{:S(2)}, u32[]{:S(2)}) collective-permute-start(bf16[512,128]{1,0:T(8,128)(2,1)S(1)} %get-tuple-element.26), channel_id=1, source_target_pairs={{24,0},{12,4},{0,8},{20,12},{8,16},{28,20},{16,24},{4,28},{25,1},{... | collective-permute-start | bytes 393224 | tf_op jit(solution)/shard_map/ppermute | solution.py:36
  64.6 3.8 %collective-permute-start.10 = (f32[4,1024]{1,0:T(4,128)S(1)}, f32[4,1024]{1,0:T(4,128)S(1)}, u32[]{:S(2)}, u32[]{:S(2)}) collective-permute-start(f32[4,1024]{1,0:T(4,128)S(1)} %pad_maximum_fusion), channel_id=1, source_target_pairs={{0,4},{4,0},{8,12},{12,8},{16,20},{20,16},{24,28},{28,24},{1,5},{5... | collective-permute-start | bytes 49160 | tf_op jit(solution)/shard_map/ppermute | solution.py:40
  68.5 3.8 %collective-permute-start.11 = (f32[4,1024]{1,0:T(4,128)S(1)}, f32[4,1024]{1,0:T(4,128)S(1)}, u32[]{:S(2)}, u32[]{:S(2)}) collective-permute-start(f32[4,1024]{1,0:T(4,128)S(1)} %fusion.4), channel_id=1, source_target_pairs={{0,8},{4,12},{8,0},{12,4},{16,24},{20,28},{24,16},{28,20},{1,9},{5... | collective-permute-start | bytes 49160 | tf_op jit(solution)/shard_map/ppermute | solution.py:40
  72.3 4.7 %collective-permute-start.12 = (f32[4,1024]{1,0:T(4,128)S(1)}, f32[4,1024]{1,0:T(4,128)S(1)}, u32[]{:S(2)}, u32[]{:S(2)}) collective-permute-start(f32[4,1024]{1,0:T(4,128)S(1)} %add.22), channel_id=1, source_target_pairs={{0,16},{4,20},{8,24},{12,28},{16,0},{20,4},{24,8},{28,12},{1,17},{... | collective-permute-start | bytes 49160 | tf_op jit(solution)/shard_map/ppermute | solution.py:40
  80.6 13.2 %collective-permute-start.15 = (f32[2,2,128,512]{3,2,1,0:T(8,128)S(1)}, f32[2,2,128,512]{3,2,1,0:T(8,128)S(1)}, u32[]{:S(2)}, u32[]{:S(2)}) collective-permute-start(f32[2,2,128,512]{3,2,1,0:T(8,128)S(1)} %shard_map.91), channel_id=1, source_target_pairs={{0,1},{1,0},{2,3},{3,2},{4,5},{5,4},{6,7},{7,6},{8,9},{9,8},{10,11... | collective-permute-start | bytes 3145736 | tf_op jit(solution)/shard_map/ppermute | solution.py:40
  80.7 3.4 %collective-permute-start.20 = (f32[2,128,512]{2,1,0:T(8,128)S(1)}, f32[2,128,512]{2,1,0:T(8,128)S(1)}, u32[]{:S(2)}, u32[]{:S(2)}) collective-permute-start(f32[2,128,512]{2,1,0:T(8,128)S(1)} %shard_map.87.earlier_ref), channel_id=1, source_target_pairs={{0,1},{1,0},{2,3},{3,2},{4,5},{5,4},{6,7},{7,6},{8,9},{9,8},{10,11... | collective-permute-start | bytes 1572872 | tf_op jit(solution)/shard_map/ppermute | solution.py:40
  81.2 4.9 %collective-permute-start.17 = (f32[2,128,512]{2,1,0:T(8,128)S(1)}, f32[2,128,512]{2,1,0:T(8,128)S(1)}, u32[]{:S(2)}, u32[]{:S(2)}) collective-permute-start(f32[2,128,512]{2,1,0:T(8,128)S(1)} %shard_map.88.earlier_ref), channel_id=1, source_target_pairs={{0,1},{1,0},{2,3},{3,2},{4,5},{5,4},{6,7},{7,6},{8,9},{9,8},{10,11... | collective-permute-start | bytes 1572872 | tf_op jit(solution)/shard_map/ppermute | solution.py:40
  81.2 5.9 %collective-permute-start.13 = (f32[2,128,512]{2,1,0:T(8,128)S(1)}, f32[2,128,512]{2,1,0:T(8,128)S(1)}, u32[]{:S(2)}, u32[]{:S(2)}) collective-permute-start(f32[2,128,512]{2,1,0:T(8,128)S(1)} %shard_map.89.earlier_ref), channel_id=1, source_target_pairs={{0,1},{1,0},{2,3},{3,2},{4,5},{5,4},{6,7},{7,6},{8,9},{9,8},{10,11... | collective-permute-start | bytes 1572872 | tf_op jit(solution)/shard_map/ppermute | solution.py:40
  84.5 6.4 %collective-permute-start.21 = (bf16[1,128,512]{2,1,0:T(8,128)(2,1)S(1)}, bf16[1,128,512]{2,1,0:T(8,128)(2,1)S(1)}, u32[]{:S(2)}, u32[]{:S(2)}) collective-permute-start(bf16[1,128,512]{2,1,0:T(8,128)(2,1)S(1)} %get-tuple-element.36), channel_id=1, source_target_pairs={{0,2},{1,3},{2,0},{3,1},{4,6},{5,7},{6,4},{7,5},{8,10},{9,11},{10,... | collective-permute-start | bytes 393224 | tf_op jit(solution)/shard_map/ppermute | solution.py:40
  86.5 9.6 %collective-permute-start.18 = (bf16[1,128,512]{2,1,0:T(8,128)(2,1)S(1)}, bf16[1,128,512]{2,1,0:T(8,128)(2,1)S(1)}, u32[]{:S(2)}, u32[]{:S(2)}) collective-permute-start(bf16[1,128,512]{2,1,0:T(8,128)(2,1)S(1)} %get-tuple-element.34), channel_id=1, source_target_pairs={{0,2},{1,3},{2,0},{3,1},{4,6},{5,7},{6,4},{7,5},{8,10},{9,11},{10,... | collective-permute-start | bytes 393224 | tf_op jit(solution)/shard_map/ppermute | solution.py:40
  88.0 10.1 %collective-permute-start.14 = (bf16[1,128,640]{2,1,0:T(8,128)(2,1)S(1)}, bf16[1,128,640]{2,1,0:T(8,128)(2,1)S(1)}, u32[]{:S(2)}, u32[]{:S(2)}) collective-permute-start(bf16[1,128,640]{2,1,0:T(8,128)(2,1)S(1)} %get-tuple-element.29), channel_id=1, source_target_pairs={{0,2},{1,3},{2,0},{3,1},{4,6},{5,7},{6,4},{7,5},{8,10},{9,11},{10,... | collective-permute-start | bytes 491528 | tf_op jit(solution)/shard_map/ppermute | solution.py:40
  91.0 7.1 %collective-permute-start.22 = (bf16[128,512]{1,0:T(8,128)(2,1)S(1)}, bf16[128,512]{1,0:T(8,128)(2,1)S(1)}, u32[]{:S(2)}, u32[]{:S(2)}) collective-permute-start(bf16[128,512]{1,0:T(8,128)(2,1)S(1)} %fusion.1), channel_id=1, source_target_pairs={{8,0},{12,4},{16,8},{20,12},{24,16},{28,20},{0,24},{4,28},{9,1},{1... | collective-permute-start | bytes 393224 | tf_op jit(solution)/shard_map/ppermute | solution.py:30
  94.6 7.5 %collective-permute-start.16 = (bf16[2,1,128,512]{3,2,1,0:T(8,128)(2,1)S(1)}, bf16[2,1,128,512]{3,2,1,0:T(8,128)(2,1)S(1)}, u32[]{:S(2)}, u32[]{:S(2)}) collective-permute-start(bf16[2,1,128,512]{3,2,1,0:T(8,128)(2,1)S(1)} %get-tuple-element.32), channel_id=1, source_target_pairs={{0,2},{1,3},{2,0},{3,1},{4,6},{5,7},{6,4},{7,5},{8,10},{9,11},{10,... | collective-permute-start | bytes 786440 | tf_op jit(solution)/shard_map/ppermute | solution.py:40
  96.2 5.0 %collective-permute-start.19 = (bf16[128,512]{1,0:T(8,128)(2,1)S(1)}, bf16[128,512]{1,0:T(8,128)(2,1)S(1)}, u32[]{:S(2)}, u32[]{:S(2)}) collective-permute-start(bf16[128,512]{1,0:T(8,128)(2,1)S(1)} %fusion), channel_id=1, source_target_pairs={{4,0},{8,4},{12,8},{16,12},{20,16},{24,20},{28,24},{0,28},{5,1},{9... | collective-permute-start | bytes 393224 | tf_op jit(solution)/shard_map/ppermute | solution.py:30
  (7 other events, 226.3 us)

commit v3 on v2

--- a/solution.py
+++ b/solution.py
@@ -244,25 +244,36 @@
         out[k] = direct_product(half_ref, ahead_ref.at[k], side, share, count)
 
 
+def diagonal_tiles(quarter, share, size, run):
+    width = max(share, 128)
+    for block in range(size // width):
+
+        @pl.when((quarter * share) // width == block)
+        def _():
+            row = lax.broadcasted_iota(jnp.int32, (share, width), 0)
+            lane = lax.broadcasted_iota(jnp.int32, (share, width), 1)
+            run(slice(block * width, (block + 1) * width), lane == row + quarter * share - block * width)
+
+
 def central_own_kernel(share, count, half_ref, own, found_ref, keep_ref, send_ref):
     _, core, side = position()
     size = half_ref.shape[0]
-    spare = send_ref.shape[-1] - size
     total = central_product(half_ref, own, core, share, count) + found_ref[...]
     for step in range(count // 2):
         low, high = total[2 * step], total[2 * step + 1]
         keep_ref[step] = jnp.where(side == 0, low, high)
         send = jnp.where(side == 0, high, low)
         rounded = send.astype(BF16)
-        send_ref[step, :, :size] = rounded
-        quarter = (2 * step + 1 - side) * 2 + core
-        for block in range(size // spare):
-
-            @pl.when((quarter * share) // spare == block)
-            def _():
-                cols = slice(block * spare, (block + 1) * spare)
-                rest = send[:, cols] - rounded[:, cols].astype(F32)
-                send_ref[step, :, size:] = rest.astype(BF16)
+        send_ref[step, :share, :] = rounded
+        send_ref[step, share:, :] = jnp.zeros((send_ref.shape[1] - share, size), BF16)
+
+        def store(cols, mask):
+            rest = jnp.where(mask, send[:, cols] - rounded[:, cols].astype(F32), 0.0)
+            rest = jnp.sum(rest, axis=0, keepdims=True)
+            rest = jnp.broadcast_to(rest, (send_ref.shape[1] - share, rest.shape[1]))
+            send_ref[step, share:, : rest.shape[1]] = rest.astype(BF16)
+
+        diagonal_tiles((2 * step + 1 - side) * 2 + core, share, size, store)
 
 
 def direct_own_kernel(share, count, half_ref, found_ref, earlier_ref, ahead_ref, keep_ref, send_ref):
@@ -272,31 +283,48 @@
         deposit(total, side, keep_ref.at[k], send_ref.at[k])
 
 
+def central_sum(share, step, central_ref, found_ref, out_ref):
+    _, core, side = position()
+    size = central_ref.shape[-1]
+    out_ref[step, :, :size] = central_ref[step] + found_ref[step, :share, :].astype(F32)
+
+    def add(cols, mask):
+        width = mask.shape[1]
+        rest = found_ref[step, share : share + 16, :width].astype(F32)[0:1]
+        out_ref[step, :, cols] += jnp.where(mask, jnp.broadcast_to(rest, mask.shape), 0.0)
+
+    diagonal_tiles((2 * step + side) * 2 + core, share, size, add)
+
+
 def joined_kernel(share, central_ref, found_ref, keep_ref, direct_ref, out_ref):
-    _, core, side = position()
     size = keep_ref.shape[-1]
-    spare = found_ref.shape[-1] - size
     for step in range(found_ref.shape[0]):
-        out_ref[step, :, :size] = central_ref[step] + found_ref[step, :, :size].astype(F32)
+        central_sum(share, step, central_ref, found_ref, out_ref)
         for k in range(REACH):
             cols = slice((k + 1) * size, (k + 2) * size)
             out_ref[step, :, cols] = keep_ref[k, step] + direct_ref[k, step].astype(F32)
-        quarter = (2 * step + side) * 2 + core
-        for block in range(size // spare):
-
-            @pl.when((quarter * share) // spare == block)
-            def _():
-                cols = slice(block * spare, (block + 1) * spare)
-                out_ref[step, :, cols] += found_ref[step, :, size:].astype(F32)
-
-
-def final_kernel(share, central_ref, found_ref, keep_ref, direct_ref, *refs):
-    mirrored, out_ref = refs[:-1], refs[-1]
-    joined_kernel(share, central_ref, found_ref, keep_ref, direct_ref, out_ref)
+
+
+def final_kernel(share, central_ref, found_ref, keep_ref, direct_ref, one, two, out_hbm, out_ref, sems):
     size = keep_ref.shape[-1]
-    for k, block in enumerate(mirrored):
+    copies = []
+
+    def release(k):
+        cols = slice(k * size, (k + 1) * size)
+        copy = pltpu.make_async_copy(out_ref.at[:, :, cols], out_hbm.at[:, :, cols], sems.at[k])
+        copy.start()
+        copies.append(copy)
+
+    for k, block in enumerate((one, two)):
         cols = slice((k + 1) * size, (k + 2) * size)
-        out_ref[0, :, cols] += block[...].astype(F32)
+        out_ref[0, :, cols] = (
+            keep_ref[k, 0] + direct_ref[k, 0].astype(F32) + block[...].astype(F32)
+        )
+        release(k + 1)
+    central_sum(share, 0, central_ref, found_ref, out_ref)
+    release(0)
+    for copy in copies:
+        copy.wait()
 
 
 def shape(dims, kind=F32):
@@ -363,11 +391,13 @@
         row_count * points, 16 * row_count * points,
     )(beside, *near, *far, *across)
     summed = jnp.concatenate(sums, axis=1)
-    bit = 1
-    while bit < rows:
-        found = swap(summed, "row", bit)
-        summed = summed + found
-        bit *= 2
+    groups = [(1, 2, 3)] + [(1 << bit,) for bit in range(2, rows.bit_length() - 1)]
+    for group in groups:
+        found = []
+        for distance in group:
+            found.append(swap(summed, "row", distance))
+        for other in found:
+            summed = summed + other
 
     point_density = summed[0]
     gradient = 2.0 * summed[1:]
@@ -415,12 +445,11 @@
         [WHOLE, ANYWHERE, WHOLE], product * 2, 4 * half.size,
     )(half, central_other, ahead)
     direct_found = swap(direct_other, "col", 1)
-    spare = max(share, 128)
     central_keep, central_send = call(
         functools.partial(central_own_kernel, share, count),
         [
             shape((kept, share, row_count)),
-            shape((kept, share, row_count + spare), BF16),
+            shape((kept, share + 16, row_count), BF16),
         ],
         [WHOLE] * 3, product * 2, 4 * half.size,
     )(half, own, central_found)
@@ -462,7 +491,11 @@
         return total + jnp.concatenate([zero, *mirrored], axis=1).astype(F32)
     return call(
         functools.partial(final_kernel, share), shape((1, share, 3 * row_count)),
-        [WHOLE] * (4 + REACH), direct_keep.size, 10 * direct_keep.size,
+        [WHOLE] * (4 + REACH), direct_keep.size, 10 * direct_keep.size, out_specs=ANYWHERE,
+        scratch=[
+            pltpu.VMEM((1, share, 3 * row_count), F32),
+            pltpu.SemaphoreType.DMA((3,)),
+        ],
     )(*partial, *mirrored)[0]
 
 

time: 103 us -> 103 us (level)
  waiting for transfers between devices: 50.5 us -> 44.1 us
  starting transfers between devices: 31.5 us -> 37.1 us
    ppermute x15 -> x16, waiting for transfers between devices: 23.1 us -> 16.4 us  [swap(): lax.ppermute(block, axis, [(i, i ^ bit) for i in range(lax.axis_size(axis...]
    ppermute x15 -> x16, starting transfers between devices: 18.6 us -> 24.9 us  [swap(): lax.ppermute(block, axis, [(i, i ^ bit) for i in range(lax.axis_size(axis...]
  transfers between devices with their start and end apart: 23 -> 24, of which waited for: 11 -> 12; matrix products, arithmetic and copies ran while one was open for 0% -> 0% of each run, Pallas kernels for 13% -> 13%
where the time goes in v3:
time: 103 us; the launch traced here: 102 us
  waiting for transfers between devices  44.1 us (43%)
  starting transfers between devices  37.1 us (36%)
  Pallas kernels  20.3 us (20%)
    ppermute x16, starting transfers between devices, swap(): lax.ppermute(block, axis, [(i, i ^ bit) for i in range(lax.axis_size(axis...  24.9 us
    ppermute x6, waiting for transfers between devices, from_side(): return lax.ppermute(block, 'row', route)  24.3 us
    ppermute x16, waiting for transfers between devices, swap(): lax.ppermute(block, axis, [(i, i ^ bit) for i in range(lax.axis_size(axis...  16.4 us
    ppermute x6, starting transfers between devices, from_side(): return lax.ppermute(block, 'row', route)  8.16 us
    pallas_call x3, Pallas kernels, body(): call(functools.partial(early_kernel, first), total, [WHOLE] * 5, 6 * squa...  4.63 us
    ppermute x2, starting transfers between devices, from_ahead(): lax.ppermute(block, 'row', [((i + distance) % size, i) for i in range(siz...  4 us
    ppermute x2, waiting for transfers between devices, from_ahead(): lax.ppermute(block, 'row', [((i + distance) % size, i) for i in range(siz...  3.43 us
    pallas_call x3, Pallas kernels, body(): call(functools.partial(sums_kernel, first), shape((components, width)), [...  2.31 us
  transfers between devices with their start and end apart: 24, of which 12 were waited for; matrix products, arithmetic and copies ran while one was open for 0% of the time, Pallas kernels for 13%

profile of v3, /device:TPU:0, one launch (start us, length us, event | category | flops | bytes accessed | tf_op | source)
XLA Modules:
  0.0 102.4 jit_solution(10496292599792425500)
XLA Ops:
  0.0 1.5 %shard_map.75 = (bf16[512,1024]{1,0:T(8,128)(2,1)S(1)}, bf16[512,640]{1,0:T(8,128)(2,1)S(1)}, bf16[512,256]{1,0:T(8,128)(2,1)S(1)}, bf16[512,128]{1,0:T(8,128)(2,1)S(1)}) custom-call(s32[4,8]{1,0:T(4,128)} %screen_hbm.1, bf16[4,512,1024]{2,1,0:T(8,128)(2,1)} %basis_ref.3), custom_call_target="tpu_custom_call" | custom-call | flops 524288 | bytes 3145728 | tf_op jit(solution)/shard_map/pallas_call | solution.py:345
  1.5 3.1 %collective-permute-start = (bf16[512,1024]{1,0:T(8,128)(2,1)S(1)}, bf16[512,1024]{1,0:T(8,128)(2,1)S(1)}, u32[]{:S(2)}, u32[]{:S(2)}) collective-permute-start(bf16[512,1024]{1,0:T(8,128)(2,1)S(1)} %get-tuple-element.23.own), channel_id=1, source_target_pairs={{0,4},{4,0},{8,12},{12,8},{16,20},{20,16},{24,28},{28,24},{1,5},{5... | collective-permute-start | bytes 3145736 | tf_op jit(solution)/shard_map/ppermute | solution.py:40
  4.6 3.6 %collective-permute-start.1 = (bf16[512,640]{1,0:T(8,128)(2,1)S(1)}, bf16[512,640]{1,0:T(8,128)(2,1)S(1)}, u32[]{:S(2)}, u32[]{:S(2)}) collective-permute-start(bf16[512,640]{1,0:T(8,128)(2,1)S(1)} %get-tuple-element.24), channel_id=1, source_target_pairs={{8,0},{28,4},{16,8},{4,12},{24,16},{12,20},{0,24},{20,28},{9,1},{2... | collective-permute-start | bytes 1966088 | tf_op jit(solution)/shard_map/ppermute | solution.py:36
  9.1 14.2 %collective-permute-done.1.near.refs_0_ = bf16[512,640]{1,0:T(8,128)(2,1)S(1)} collective-permute-done((bf16[512,640]{1,0:T(8,128)(2,1)S(1)}, bf16[512,640]{1,0:T(8,128)(2,1)S(1)}, u32[]{:S(2)}, u32[]{:S(2)}) %collective-permute-start.1) | collective-permute-done | bytes 655392 | tf_op jit(solution)/shard_map/ppermute | solution.py:36
  24.2 6.1 %collective-permute-done.7.near.refs_2_ = bf16[512,128]{1,0:T(8,128)(2,1)S(1)} collective-permute-done((bf16[512,128]{1,0:T(8,128)(2,1)S(1)}, bf16[512,128]{1,0:T(8,128)(2,1)S(1)}, u32[]{:S(2)}, u32[]{:S(2)}) %collective-permute-start.7) | collective-permute-done | bytes 131104 | tf_op jit(solution)/shard_map/ppermute | solution.py:36
  30.3 1.2 %collective-permute-start.8 = (bf16[512,128]{1,0:T(8,128)(2,1)S(1)}, bf16[512,128]{1,0:T(8,128)(2,1)S(1)}, u32[]{:S(2)}, u32[]{:S(2)}) collective-permute-start(bf16[512,128]{1,0:T(8,128)(2,1)S(1)} %collective-permute-done.7.near.refs_2_), channel_id=1, source_target_pairs={{0,4},{4,0},{8,12},{12,8},{16,20},{20,16},{24,28},{28,24},{1,5},{5... | collective-permute-start | bytes 393224 | tf_op jit(solution)/shard_map/ppermute | solution.py:40
  31.6 5.1 %collective-permute-start.5 = (bf16[512,256]{1,0:T(8,128)(2,1)S(1)}, bf16[512,256]{1,0:T(8,128)(2,1)S(1)}, u32[]{:S(2)}, u32[]{:S(2)}) collective-permute-start(bf16[512,256]{1,0:T(8,128)(2,1)S(1)} %collective-permute-done.4.near.refs_1_), channel_id=1, source_target_pairs={{0,4},{4,0},{8,12},{12,8},{16,20},{20,16},{24,28},{28,24},{1,5},{5... | collective-permute-start | bytes 786440 | tf_op jit(solution)/shard_map/ppermute | solution.py:40
  36.6 8.8 %collective-permute-done.8.across.refs_8_ = bf16[512,128]{1,0:T(8,128)(2,1)S(1)} collective-permute-done((bf16[512,128]{1,0:T(8,128)(2,1)S(1)}, bf16[512,128]{1,0:T(8,128)(2,1)S(1)}, u32[]{:S(2)}, u32[]{:S(2)}) %collective-permute-start.8) | collective-permute-done | bytes 131104 | tf_op jit(solution)/shard_map/ppermute | solution.py:40
  45.4 2.1 %collective-permute-start.6 = (bf16[512,256]{1,0:T(8,128)(2,1)S(1)}, bf16[512,256]{1,0:T(8,128)(2,1)S(1)}, u32[]{:S(2)}, u32[]{:S(2)}) collective-permute-start(bf16[512,256]{1,0:T(8,128)(2,1)S(1)} %get-tuple-element.25), channel_id=1, source_target_pairs={{24,0},{12,4},{0,8},{20,12},{8,16},{28,20},{16,24},{4,28},{25,1},{... | collective-permute-start | bytes 786440 | tf_op jit(solution)/shard_map/ppermute | solution.py:36
  47.5 1.6 %collective-permute-start.9 = (bf16[512,128]{1,0:T(8,128)(2,1)S(1)}, bf16[512,128]{1,0:T(8,128)(2,1)S(1)}, u32[]{:S(2)}, u32[]{:S(2)}) collective-permute-start(bf16[512,128]{1,0:T(8,128)(2,1)S(1)} %get-tuple-element.26), channel_id=1, source_target_pairs={{24,0},{12,4},{0,8},{20,12},{8,16},{28,20},{16,24},{4,28},{25,1},{... | collective-permute-start | bytes 393224 | tf_op jit(solution)/shard_map/ppermute | solution.py:36
  49.1 1.8 %shard_map.73.masked_ref = f32[4,512,1024]{2,1,0:T(8,128)S(1)} custom-call(s32[4,8]{1,0:T(4,128)S(1)} %copy-done.2, bf16[4,512,1024]{2,1,0:T(8,128)(2,1)S(1)} %copy-done.1), custom_call_target="tpu_custom_call" | custom-call | flops 2097152 | bytes 12582912 | tf_op jit(solution)/shard_map/pallas_call | solution.py:367
  53.1 4.0 %collective-permute-done.9.far.refs_5_ = bf16[512,128]{1,0:T(8,128)(2,1)S(1)} collective-permute-done((bf16[512,128]{1,0:T(8,128)(2,1)S(1)}, bf16[512,128]{1,0:T(8,128)(2,1)S(1)}, u32[]{:S(2)}, u32[]{:S(2)}) %collective-permute-start.9) | collective-permute-done | bytes 131104 | tf_op jit(solution)/shard_map/ppermute | solution.py:36
  59.6 2.7 %shard_map.76.partial_ref = f32[512,640]{1,0:T(8,128)S(1)} custom-call(bf16[5,512,512]{2,1,0:T(8,128)(2,1)S(1)} %get-tuple-element.21.high_ref, bf16[5,512,512]{2,1,0:T(8,128)(2,1)S(1)} %get-tuple-element.22.low_ref, bf16[512,1024]{1,0:T(8,128)(2,1)S(1)} %get-tuple-element.23.own, bf16[512,1024]{1,0:T(8,128)(2,1)S(1)} %collective-permute-done.beside, ...), custom_call_target="tpu_custom_call" | custom-call | flops 2013265920 | bytes 5242880 | tf_op jit(solution)/shard_map/pallas_call | solution.py:374
  63.3 1.3 %shard_map.78 = f32[4,640]{1,0:T(4,128)S(1)} custom-call(bf16[5,512,512]{2,1,0:T(8,128)(2,1)S(1)} %get-tuple-element.21.high_ref, bf16[5,512,512]{2,1,0:T(8,128)(2,1)S(1)} %get-tuple-element.22.low_ref, f32[512,640]{1,0:T(8,128)S(1)} %shard_map.77.partial_ref, bf16[512,640]{1,0:T(8,128)(2,1)S(1)} %collective-permute-done.3.far.refs_3_, ...), custom_call_target="tpu_custom_call" | custom-call | flops 671088640 | bytes 3145728 | tf_op jit(solution)/shard_map/pallas_call | solution.py:381
  65.5 2.7 %collective-permute-start.12 = (f32[4,1024]{1,0:T(4,128)S(1)}, f32[4,1024]{1,0:T(4,128)S(1)}, u32[]{:S(2)}, u32[]{:S(2)}) collective-permute-start(f32[4,1024]{1,0:T(4,128)S(1)} %pad_maximum_fusion), channel_id=1, source_target_pairs={{0,12},{4,8},{8,4},{12,0},{16,28},{20,24},{24,20},{28,16},{1,13},{... | collective-permute-start | bytes 49160 | tf_op jit(solution)/shard_map/ppermute | solution.py:40
  70.1 4.6 %collective-permute-start.13 = (f32[4,1024]{1,0:T(4,128)S(1)}, f32[4,1024]{1,0:T(4,128)S(1)}, u32[]{:S(2)}, u32[]{:S(2)}) collective-permute-start(f32[4,1024]{1,0:T(4,128)S(1)} %add_add_fusion), channel_id=1, source_target_pairs={{0,16},{4,20},{8,24},{12,28},{16,0},{20,4},{24,8},{28,12},{1,17},{... | collective-permute-start | bytes 49160 | tf_op jit(solution)/shard_map/ppermute | solution.py:40
  81.2 2.4 %collective-permute-done.21.found_ref = f32[2,128,512]{2,1,0:T(8,128)S(1)} collective-permute-done((f32[2,128,512]{2,1,0:T(8,128)S(1)}, f32[2,128,512]{2,1,0:T(8,128)S(1)}, u32[]{:S(2)}, u32[]{:S(2)}) %collective-permute-start.21) | collective-permute-done | bytes 524320 | tf_op jit(solution)/shard_map/ppermute | solution.py:40
  84.1 1.6 %collective-permute-start.22 = (bf16[1,128,512]{2,1,0:T(8,128)(2,1)S(1)}, bf16[1,128,512]{2,1,0:T(8,128)(2,1)S(1)}, u32[]{:S(2)}, u32[]{:S(2)}) collective-permute-start(bf16[1,128,512]{2,1,0:T(8,128)(2,1)S(1)} %get-tuple-element.36), channel_id=1, source_target_pairs={{0,2},{1,3},{2,0},{3,1},{4,6},{5,7},{6,4},{7,5},{8,10},{9,11},{10,... | collective-permute-start | bytes 393224 | tf_op jit(solution)/shard_map/ppermute | solution.py:40
  87.5 1.6 %collective-permute-start.15 = (bf16[1,144,512]{2,1,0:T(8,128)(2,1)S(1)}, bf16[1,144,512]{2,1,0:T(8,128)(2,1)S(1)}, u32[]{:S(2)}, u32[]{:S(2)}) collective-permute-start(bf16[1,144,512]{2,1,0:T(8,128)(2,1)S(1)} %get-tuple-element.29), channel_id=1, source_target_pairs={{0,2},{1,3},{2,0},{3,1},{4,6},{5,7},{6,4},{7,5},{8,10},{9,11},{10,... | collective-permute-start | bytes 442376 | tf_op jit(solution)/shard_map/ppermute | solution.py:40
  89.1 1.4 %collective-permute-done.22 = bf16[1,128,512]{2,1,0:T(8,128)(2,1)S(1)} collective-permute-done((bf16[1,128,512]{2,1,0:T(8,128)(2,1)S(1)}, bf16[1,128,512]{2,1,0:T(8,128)(2,1)S(1)}, u32[]{:S(2)}, u32[]{:S(2)}) %collective-permute-start.22) | collective-permute-done | bytes 131104 | tf_op jit(solution)/shard_map/ppermute | solution.py:40
  90.6 2.4 %collective-permute-start.23 = (bf16[128,512]{1,0:T(8,128)(2,1)S(1)}, bf16[128,512]{1,0:T(8,128)(2,1)S(1)}, u32[]{:S(2)}, u32[]{:S(2)}) collective-permute-start(bf16[128,512]{1,0:T(8,128)(2,1)S(1)} %fusion.1), channel_id=1, source_target_pairs={{8,0},{12,4},{16,8},{20,12},{24,16},{28,20},{0,24},{4,28},{9,1},{1... | collective-permute-start | bytes 393224 | tf_op jit(solution)/shard_map/ppermute | solution.py:30
  93.8 1.6 %collective-permute-start.17 = (bf16[2,1,128,512]{3,2,1,0:T(8,128)(2,1)S(1)}, bf16[2,1,128,512]{3,2,1,0:T(8,128)(2,1)S(1)}, u32[]{:S(2)}, u32[]{:S(2)}) collective-permute-start(bf16[2,1,128,512]{3,2,1,0:T(8,128)(2,1)S(1)} %get-tuple-element.32), channel_id=1, source_target_pairs={{0,2},{1,3},{2,0},{3,1},{4,6},{5,7},{6,4},{7,5},{8,10},{9,11},{10,... | collective-permute-start | bytes 786440 | tf_op jit(solution)/shard_map/ppermute | solution.py:40
  95.4 1.6 %collective-permute-start.20 = (bf16[128,512]{1,0:T(8,128)(2,1)S(1)}, bf16[128,512]{1,0:T(8,128)(2,1)S(1)}, u32[]{:S(2)}, u32[]{:S(2)}) collective-permute-start(bf16[128,512]{1,0:T(8,128)(2,1)S(1)} %fusion), channel_id=1, source_target_pairs={{4,0},{8,4},{12,8},{16,12},{20,16},{24,20},{28,24},{0,28},{5,1},{9... | collective-permute-start | bytes 393224 | tf_op jit(solution)/shard_map/ppermute | solution.py:30
  97.0 3.4 %collective-permute-done.20.one = bf16[128,512]{1,0:T(8,128)(2,1)S(1)} collective-permute-done((bf16[128,512]{1,0:T(8,128)(2,1)S(1)}, bf16[128,512]{1,0:T(8,128)(2,1)S(1)}, u32[]{:S(2)}, u32[]{:S(2)}) %collective-permute-start.20) | collective-permute-done | bytes 131104 | tf_op jit(solution)/shard_map/ppermute | solution.py:30
  (75 shorter events, 21.7 us)
Async XLA Ops:
  1.5 46.0 %collective-permute-start = (bf16[512,1024]{1,0:T(8,128)(2,1)S(1)}, bf16[512,1024]{1,0:T(8,128)(2,1)S(1)}, u32[]{:S(2)}, u32[]{:S(2)}) collective-permute-start(bf16[512,1024]{1,0:T(8,128)(2,1)S(1)} %get-tuple-element.23.own), channel_id=1, source_target_pairs={{0,4},{4,0},{8,12},{12,8},{16,20},{20,16},{24,28},{28,24},{1,5},{5... | collective-permute-start | bytes 3145736 | tf_op jit(solution)/shard_map/ppermute | solution.py:40
  4.6 18.7 %collective-permute-start.1 = (bf16[512,640]{1,0:T(8,128)(2,1)S(1)}, bf16[512,640]{1,0:T(8,128)(2,1)S(1)}, u32[]{:S(2)}, u32[]{:S(2)}) collective-permute-start(bf16[512,640]{1,0:T(8,128)(2,1)S(1)} %get-tuple-element.24), channel_id=1, source_target_pairs={{8,0},{28,4},{16,8},{4,12},{24,16},{12,20},{0,24},{20,28},{9,1},{2... | collective-permute-start | bytes 1966088 | tf_op jit(solution)/shard_map/ppermute | solution.py:36
  8.2 23.4 %collective-permute-start.4 = (bf16[512,256]{1,0:T(8,128)(2,1)S(1)}, bf16[512,256]{1,0:T(8,128)(2,1)S(1)}, u32[]{:S(2)}, u32[]{:S(2)}) collective-permute-start(bf16[512,256]{1,0:T(8,128)(2,1)S(1)} %get-tuple-element.25), channel_id=1, source_target_pairs={{8,0},{28,4},{16,8},{4,12},{24,16},{12,20},{0,24},{20,28},{9,1},{2... | collective-permute-start | bytes 786440 | tf_op jit(solution)/shard_map/ppermute | solution.py:36
  8.6 21.7 %collective-permute-start.7 = (bf16[512,128]{1,0:T(8,128)(2,1)S(1)}, bf16[512,128]{1,0:T(8,128)(2,1)S(1)}, u32[]{:S(2)}, u32[]{:S(2)}) collective-permute-start(bf16[512,128]{1,0:T(8,128)(2,1)S(1)} %get-tuple-element.26), channel_id=1, source_target_pairs={{8,0},{28,4},{16,8},{4,12},{24,16},{12,20},{0,24},{20,28},{9,1},{2... | collective-permute-start | bytes 393224 | tf_op jit(solution)/shard_map/ppermute | solution.py:36
  23.3 39.0 %collective-permute-start.2 = (bf16[512,640]{1,0:T(8,128)(2,1)S(1)}, bf16[512,640]{1,0:T(8,128)(2,1)S(1)}, u32[]{:S(2)}, u32[]{:S(2)}) collective-permute-start(bf16[512,640]{1,0:T(8,128)(2,1)S(1)} %collective-permute-done.1.near.refs_0_), channel_id=1, source_target_pairs={{0,4},{4,0},{8,12},{12,8},{16,20},{20,16},{24,28},{28,24},{1,5},{5... | collective-permute-start | bytes 1966088 | tf_op jit(solution)/shard_map/ppermute | solution.py:40
  30.3 15.1 %collective-permute-start.8 = (bf16[512,128]{1,0:T(8,128)(2,1)S(1)}, bf16[512,128]{1,0:T(8,128)(2,1)S(1)}, u32[]{:S(2)}, u32[]{:S(2)}) collective-permute-start(bf16[512,128]{1,0:T(8,128)(2,1)S(1)} %collective-permute-done.7.near.refs_2_), channel_id=1, source_target_pairs={{0,4},{4,0},{8,12},{12,8},{16,20},{20,16},{24,28},{28,24},{1,5},{5... | collective-permute-start | bytes 393224 | tf_op jit(solution)/shard_map/ppermute | solution.py:40
  31.5 31.7 %collective-permute-start.3 = (bf16[512,640]{1,0:T(8,128)(2,1)S(1)}, bf16[512,640]{1,0:T(8,128)(2,1)S(1)}, u32[]{:S(2)}, u32[]{:S(2)}) collective-permute-start(bf16[512,640]{1,0:T(8,128)(2,1)S(1)} %get-tuple-element.24), channel_id=1, source_target_pairs={{24,0},{12,4},{0,8},{20,12},{8,16},{28,20},{16,24},{4,28},{25,1},{... | collective-permute-start | bytes 1966088 | tf_op jit(solution)/shard_map/ppermute | solution.py:36
  31.6 27.0 %collective-permute-start.5 = (bf16[512,256]{1,0:T(8,128)(2,1)S(1)}, bf16[512,256]{1,0:T(8,128)(2,1)S(1)}, u32[]{:S(2)}, u32[]{:S(2)}) collective-permute-start(bf16[512,256]{1,0:T(8,128)(2,1)S(1)} %collective-permute-done.4.near.refs_1_), channel_id=1, source_target_pairs={{0,4},{4,0},{8,12},{12,8},{16,20},{20,16},{24,28},{28,24},{1,5},{5... | collective-permute-start | bytes 786440 | tf_op jit(solution)/shard_map/ppermute | solution.py:40
  45.4 13.6 %collective-permute-start.6 = (bf16[512,256]{1,0:T(8,128)(2,1)S(1)}, bf16[512,256]{1,0:T(8,128)(2,1)S(1)}, u32[]{:S(2)}, u32[]{:S(2)}) collective-permute-start(bf16[512,256]{1,0:T(8,128)(2,1)S(1)} %get-tuple-element.25), channel_id=1, source_target_pairs={{24,0},{12,4},{0,8},{20,12},{8,16},{28,20},{16,24},{4,28},{25,1},{... | collective-permute-start | bytes 786440 | tf_op jit(solution)/shard_map/ppermute | solution.py:36
  47.5 9.6 %collective-permute-start.9 = (bf16[512,128]{1,0:T(8,128)(2,1)S(1)}, bf16[512,128]{1,0:T(8,128)(2,1)S(1)}, u32[]{:S(2)}, u32[]{:S(2)}) collective-permute-start(bf16[512,128]{1,0:T(8,128)(2,1)S(1)} %get-tuple-element.26), channel_id=1, source_target_pairs={{24,0},{12,4},{0,8},{20,12},{8,16},{28,20},{16,24},{4,28},{25,1},{... | collective-permute-start | bytes 393224 | tf_op jit(solution)/shard_map/ppermute | solution.py:36
  64.6 3.8 %collective-permute-start.10 = (f32[4,1024]{1,0:T(4,128)S(1)}, f32[4,1024]{1,0:T(4,128)S(1)}, u32[]{:S(2)}, u32[]{:S(2)}) collective-permute-start(f32[4,1024]{1,0:T(4,128)S(1)} %pad_maximum_fusion), channel_id=1, source_target_pairs={{0,4},{4,0},{8,12},{12,8},{16,20},{20,16},{24,28},{28,24},{1,5},{5... | collective-permute-start | bytes 49160 | tf_op jit(solution)/shard_map/ppermute | solution.py:40
  65.2 3.7 %collective-permute-start.11 = (f32[4,1024]{1,0:T(4,128)S(1)}, f32[4,1024]{1,0:T(4,128)S(1)}, u32[]{:S(2)}, u32[]{:S(2)}) collective-permute-start(f32[4,1024]{1,0:T(4,128)S(1)} %pad_maximum_fusion), channel_id=1, source_target_pairs={{0,8},{4,12},{8,0},{12,4},{16,24},{20,28},{24,16},{28,20},{1,9},{5... | collective-permute-start | bytes 49160 | tf_op jit(solution)/shard_map/ppermute | solution.py:40
  65.5 4.6 %collective-permute-start.12 = (f32[4,1024]{1,0:T(4,128)S(1)}, f32[4,1024]{1,0:T(4,128)S(1)}, u32[]{:S(2)}, u32[]{:S(2)}) collective-permute-start(f32[4,1024]{1,0:T(4,128)S(1)} %pad_maximum_fusion), channel_id=1, source_target_pairs={{0,12},{4,8},{8,4},{12,0},{16,28},{20,24},{24,20},{28,16},{1,13},{... | collective-permute-start | bytes 49160 | tf_op jit(solution)/shard_map/ppermute | solution.py:40
  70.1 6.3 %collective-permute-start.13 = (f32[4,1024]{1,0:T(4,128)S(1)}, f32[4,1024]{1,0:T(4,128)S(1)}, u32[]{:S(2)}, u32[]{:S(2)}) collective-permute-start(f32[4,1024]{1,0:T(4,128)S(1)} %add_add_fusion), channel_id=1, source_target_pairs={{0,16},{4,20},{8,24},{12,28},{16,0},{20,4},{24,8},{28,12},{1,17},{... | collective-permute-start | bytes 49160 | tf_op jit(solution)/shard_map/ppermute | solution.py:40
  80.2 12.8 %collective-permute-start.16 = (f32[2,2,128,512]{3,2,1,0:T(8,128)S(1)}, f32[2,2,128,512]{3,2,1,0:T(8,128)S(1)}, u32[]{:S(2)}, u32[]{:S(2)}) collective-permute-start(f32[2,2,128,512]{3,2,1,0:T(8,128)S(1)} %shard_map.91), channel_id=1, source_target_pairs={{0,1},{1,0},{2,3},{3,2},{4,5},{5,4},{6,7},{7,6},{8,9},{9,8},{10,11... | collective-permute-start | bytes 3145736 | tf_op jit(solution)/shard_map/ppermute | solution.py:40
  80.2 3.4 %collective-permute-start.21 = (f32[2,128,512]{2,1,0:T(8,128)S(1)}, f32[2,128,512]{2,1,0:T(8,128)S(1)}, u32[]{:S(2)}, u32[]{:S(2)}) collective-permute-start(f32[2,128,512]{2,1,0:T(8,128)S(1)} %shard_map.87.earlier_ref), channel_id=1, source_target_pairs={{0,1},{1,0},{2,3},{3,2},{4,5},{5,4},{6,7},{7,6},{8,9},{9,8},{10,11... | collective-permute-start | bytes 1572872 | tf_op jit(solution)/shard_map/ppermute | solution.py:40
  80.7 4.9 %collective-permute-start.18 = (f32[2,128,512]{2,1,0:T(8,128)S(1)}, f32[2,128,512]{2,1,0:T(8,128)S(1)}, u32[]{:S(2)}, u32[]{:S(2)}) collective-permute-start(f32[2,128,512]{2,1,0:T(8,128)S(1)} %shard_map.88.earlier_ref), channel_id=1, source_target_pairs={{0,1},{1,0},{2,3},{3,2},{4,5},{5,4},{6,7},{7,6},{8,9},{9,8},{10,11... | collective-permute-start | bytes 1572872 | tf_op jit(solution)/shard_map/ppermute | solution.py:40
  80.8 5.9 %collective-permute-start.14 = (f32[2,128,512]{2,1,0:T(8,128)S(1)}, f32[2,128,512]{2,1,0:T(8,128)S(1)}, u32[]{:S(2)}, u32[]{:S(2)}) collective-permute-start(f32[2,128,512]{2,1,0:T(8,128)S(1)} %shard_map.89.earlier_ref), channel_id=1, source_target_pairs={{0,1},{1,0},{2,3},{3,2},{4,5},{5,4},{6,7},{7,6},{8,9},{9,8},{10,11... | collective-permute-start | bytes 1572872 | tf_op jit(solution)/shard_map/ppermute | solution.py:40
  84.1 6.4 %collective-permute-start.22 = (bf16[1,128,512]{2,1,0:T(8,128)(2,1)S(1)}, bf16[1,128,512]{2,1,0:T(8,128)(2,1)S(1)}, u32[]{:S(2)}, u32[]{:S(2)}) collective-permute-start(bf16[1,128,512]{2,1,0:T(8,128)(2,1)S(1)} %get-tuple-element.36), channel_id=1, source_target_pairs={{0,2},{1,3},{2,0},{3,1},{4,6},{5,7},{6,4},{7,5},{8,10},{9,11},{10,... | collective-permute-start | bytes 393224 | tf_op jit(solution)/shard_map/ppermute | solution.py:40
  86.2 9.2 %collective-permute-start.19 = (bf16[1,128,512]{2,1,0:T(8,128)(2,1)S(1)}, bf16[1,128,512]{2,1,0:T(8,128)(2,1)S(1)}, u32[]{:S(2)}, u32[]{:S(2)}) collective-permute-start(bf16[1,128,512]{2,1,0:T(8,128)(2,1)S(1)} %get-tuple-element.34), channel_id=1, source_target_pairs={{0,2},{1,3},{2,0},{3,1},{4,6},{5,7},{6,4},{7,5},{8,10},{9,11},{10,... | collective-permute-start | bytes 393224 | tf_op jit(solution)/shard_map/ppermute | solution.py:40
  87.5 9.4 %collective-permute-start.15 = (bf16[1,144,512]{2,1,0:T(8,128)(2,1)S(1)}, bf16[1,144,512]{2,1,0:T(8,128)(2,1)S(1)}, u32[]{:S(2)}, u32[]{:S(2)}) collective-permute-start(bf16[1,144,512]{2,1,0:T(8,128)(2,1)S(1)} %get-tuple-element.29), channel_id=1, source_target_pairs={{0,2},{1,3},{2,0},{3,1},{4,6},{5,7},{6,4},{7,5},{8,10},{9,11},{10,... | collective-permute-start | bytes 442376 | tf_op jit(solution)/shard_map/ppermute | solution.py:40
  90.6 6.4 %collective-permute-start.23 = (bf16[128,512]{1,0:T(8,128)(2,1)S(1)}, bf16[128,512]{1,0:T(8,128)(2,1)S(1)}, u32[]{:S(2)}, u32[]{:S(2)}) collective-permute-start(bf16[128,512]{1,0:T(8,128)(2,1)S(1)} %fusion.1), channel_id=1, source_target_pairs={{8,0},{12,4},{16,8},{20,12},{24,16},{28,20},{0,24},{4,28},{9,1},{1... | collective-permute-start | bytes 393224 | tf_op jit(solution)/shard_map/ppermute | solution.py:30
  93.8 7.5 %collective-permute-start.17 = (bf16[2,1,128,512]{3,2,1,0:T(8,128)(2,1)S(1)}, bf16[2,1,128,512]{3,2,1,0:T(8,128)(2,1)S(1)}, u32[]{:S(2)}, u32[]{:S(2)}) collective-permute-start(bf16[2,1,128,512]{3,2,1,0:T(8,128)(2,1)S(1)} %get-tuple-element.32), channel_id=1, source_target_pairs={{0,2},{1,3},{2,0},{3,1},{4,6},{5,7},{6,4},{7,5},{8,10},{9,11},{10,... | collective-permute-start | bytes 786440 | tf_op jit(solution)/shard_map/ppermute | solution.py:40
  95.4 5.0 %collective-permute-start.20 = (bf16[128,512]{1,0:T(8,128)(2,1)S(1)}, bf16[128,512]{1,0:T(8,128)(2,1)S(1)}, u32[]{:S(2)}, u32[]{:S(2)}) collective-permute-start(bf16[128,512]{1,0:T(8,128)(2,1)S(1)} %fusion), channel_id=1, source_target_pairs={{4,0},{8,4},{12,8},{16,12},{20,16},{24,20},{28,24},{0,28},{5,1},{9... | collective-permute-start | bytes 393224 | tf_op jit(solution)/shard_map/ppermute | solution.py:30
  (8 other events, 301.4 us)

commit v4 on v3

--- a/solution.py
+++ b/solution.py
@@ -101,7 +101,7 @@
         for chunk in chunk_refs:
             for start in range(0, chunk.shape[1], gb):
                 keep = screen_ref[row, col // gb].astype(F32)
-                tile = (tile_ref[rows, col : col + gb].astype(F32) * keep).astype(BF16)
+                tile = tile_ref[rows, col : col + gb] * jnp.full((sb, gb), keep).astype(BF16)
                 own_ref[rows, col : col + gb] = tile
                 chunk[rows, start : start + gb] = tile
                 col += gb
@@ -155,16 +155,33 @@
                 masked_ref[c, rows, cols] = basis_ref[c, rows, cols].astype(F32) * keep
 
 
-def half_kernel(masked_ref, parts_ref, half_ref):
+def half_kernel(share, count, step, masked_ref, parts_ref, behind_ref, half_ref, *outs):
     components, row_count, points = masked_ref.shape
-    for start in range(0, points, 128):
-        cols = slice(start, start + 128)
-        for row in range(0, row_count, 128):
-            rows = slice(row, row + 128)
-            total = parts_ref[0:1, cols] * masked_ref[0, rows, cols]
-            for c in range(1, components):
-                total += parts_ref[c : c + 1, cols] * masked_ref[c, rows, cols]
-            half_ref[rows, cols] = total.astype(BF16)
+    side = 1 - position()[1]
+    for first in range(0, points, step):
+        for start in range(first, first + step, 128):
+            cols = slice(start, start + 128)
+            for row in range(0, row_count, 128):
+                rows = slice(row, row + 128)
+                total = parts_ref[0:1, cols] * masked_ref[0, rows, cols]
+                for c in range(1, components):
+                    total += parts_ref[c : c + 1, cols] * masked_ref[c, rows, cols]
+                half_ref[rows, cols] = total.astype(BF16)
+        cols = slice(first, first + step)
+        for k, out in outs_of(outs):
+            left = jnp.concatenate(
+                [
+                    behind_ref[k, pl.ds(pl.multiple_of((2 * i + side) * share, share), share), cols]
+                    for i in range(count)
+                ],
+                axis=0,
+            )
+            found = dot_rows(left, half_ref[:, cols]).reshape(out.shape)
+            out[...] = found if first == 0 else out[...] + found
+
+
+def outs_of(outs):
+    return tuple(zip((1, 0), outs))
 
 
 def sorted_kernel(chunks, beside, *refs):
@@ -413,20 +430,24 @@
     scalar_part = 0.5 * weights * density_pot
     vector_part = 2.0 * weights * gradient_pot * gradient
     parts = jnp.concatenate([scalar_part[None], vector_part], axis=0)
-    half = call(
-        half_kernel, shape((row_count, points), BF16), [WHOLE] * 2,
-        8 * basis_values.size, 4 * basis_values.size,
-    )(masked, parts)
-
     product = 2 * row_count * points * share * count
     kept = count // 2
     block = (count, share, row_count)
+    fused = 1
+    half, *mirrored_other = call(
+        functools.partial(half_kernel, share, count, 256),
+        [shape((row_count, points), BF16)] + [shape(block)] * fused, [WHOLE] * 3,
+        8 * basis_values.size + fused * product, 4 * basis_values.size,
+    )(masked, parts, behind)
     mirrored_found, earlier = {}, half
     for k in (2, 1):
-        earlier = call(
-            functools.partial(mirrored_other_kernel, share, count, k - 1), shape(block),
-            [WHOLE, ANYWHERE, WHOLE], product, 3 * half.size,
-        )(half, earlier, behind)
+        if k > REACH - fused:
+            earlier = mirrored_other[REACH - k]
+        else:
+            earlier = call(
+                functools.partial(mirrored_other_kernel, share, count, k - 1), shape(block),
+                [WHOLE, ANYWHERE, WHOLE], product, 3 * half.size,
+            )(half, earlier, behind)
         mirrored_found[k] = swap(earlier, "col", 1)
     central_other = call(
         functools.partial(central_other_kernel, share, count), shape(block),

time: 103 us -> 102 us (level)
  no operation moved by 1% of the time
where the time goes in v4:
time: 102 us
  waiting for transfers between devices  44.1 us (43%)
  starting transfers between devices  37.1 us (36%)
  Pallas kernels  19.9 us (20%)
    ppermute x16, starting transfers between devices, swap(): lax.ppermute(block, axis, [(i, i ^ bit) for i in range(lax.axis_size(axis...  24.9 us
    ppermute x6, waiting for transfers between devices, from_side(): return lax.ppermute(block, 'row', route)  24.3 us
    ppermute x16, waiting for transfers between devices, swap(): lax.ppermute(block, axis, [(i, i ^ bit) for i in range(lax.axis_size(axis...  16.4 us
    ppermute x6, starting transfers between devices, from_side(): return lax.ppermute(block, 'row', route)  8.16 us
    pallas_call x3, Pallas kernels, body(): call(functools.partial(early_kernel, first), total, [WHOLE] * 5, 6 * squa...  4.64 us
    ppermute x2, starting transfers between devices, from_ahead(): lax.ppermute(block, 'row', [((i + distance) % size, i) for i in range(siz...  4 us
    ppermute x2, waiting for transfers between devices, from_ahead(): lax.ppermute(block, 'row', [((i + distance) % size, i) for i in range(siz...  3.43 us
    pallas_call x3, Pallas kernels, body(): call(functools.partial(sums_kernel, first), shape((components, width)), [...  2.31 us
  transfers between devices with their start and end apart: 24, of which 12 were waited for; matrix products, arithmetic and copies ran while one was open for 0% of the time, Pallas kernels for 13%

profile of v4, /device:TPU:0, one launch (start us, length us, event | category | flops | bytes accessed | tf_op | source)
XLA Modules:
  0.0 102.0 jit_solution(17849292023592862397)
XLA Ops:
  0.0 1.5 %shard_map.75 = (bf16[512,1024]{1,0:T(8,128)(2,1)S(1)}, bf16[512,640]{1,0:T(8,128)(2,1)S(1)}, bf16[512,256]{1,0:T(8,128)(2,1)S(1)}, bf16[512,128]{1,0:T(8,128)(2,1)S(1)}) custom-call(s32[4,8]{1,0:T(4,128)} %screen_hbm.1, bf16[4,512,1024]{2,1,0:T(8,128)(2,1)} %basis_ref.3), custom_call_target="tpu_custom_call" | custom-call | flops 524288 | bytes 3145728 | tf_op jit(solution)/shard_map/pallas_call | solution.py:362
  1.5 3.1 %collective-permute-start = (bf16[512,1024]{1,0:T(8,128)(2,1)S(1)}, bf16[512,1024]{1,0:T(8,128)(2,1)S(1)}, u32[]{:S(2)}, u32[]{:S(2)}) collective-permute-start(bf16[512,1024]{1,0:T(8,128)(2,1)S(1)} %get-tuple-element.25.own), channel_id=1, source_target_pairs={{0,4},{4,0},{8,12},{12,8},{16,20},{20,16},{24,28},{28,24},{1,5},{5... | collective-permute-start | bytes 3145736 | tf_op jit(solution)/shard_map/ppermute | solution.py:40
  4.6 3.6 %collective-permute-start.1 = (bf16[512,640]{1,0:T(8,128)(2,1)S(1)}, bf16[512,640]{1,0:T(8,128)(2,1)S(1)}, u32[]{:S(2)}, u32[]{:S(2)}) collective-permute-start(bf16[512,640]{1,0:T(8,128)(2,1)S(1)} %get-tuple-element.26), channel_id=1, source_target_pairs={{8,0},{28,4},{16,8},{4,12},{24,16},{12,20},{0,24},{20,28},{9,1},{2... | collective-permute-start | bytes 1966088 | tf_op jit(solution)/shard_map/ppermute | solution.py:36
  9.1 14.2 %collective-permute-done.1.near.refs_0_ = bf16[512,640]{1,0:T(8,128)(2,1)S(1)} collective-permute-done((bf16[512,640]{1,0:T(8,128)(2,1)S(1)}, bf16[512,640]{1,0:T(8,128)(2,1)S(1)}, u32[]{:S(2)}, u32[]{:S(2)}) %collective-permute-start.1) | collective-permute-done | bytes 655392 | tf_op jit(solution)/shard_map/ppermute | solution.py:36
  24.3 6.1 %collective-permute-done.7.near.refs_2_ = bf16[512,128]{1,0:T(8,128)(2,1)S(1)} collective-permute-done((bf16[512,128]{1,0:T(8,128)(2,1)S(1)}, bf16[512,128]{1,0:T(8,128)(2,1)S(1)}, u32[]{:S(2)}, u32[]{:S(2)}) %collective-permute-start.7) | collective-permute-done | bytes 131104 | tf_op jit(solution)/shard_map/ppermute | solution.py:36
  30.3 1.2 %collective-permute-start.8 = (bf16[512,128]{1,0:T(8,128)(2,1)S(1)}, bf16[512,128]{1,0:T(8,128)(2,1)S(1)}, u32[]{:S(2)}, u32[]{:S(2)}) collective-permute-start(bf16[512,128]{1,0:T(8,128)(2,1)S(1)} %collective-permute-done.7.near.refs_2_), channel_id=1, source_target_pairs={{0,4},{4,0},{8,12},{12,8},{16,20},{20,16},{24,28},{28,24},{1,5},{5... | collective-permute-start | bytes 393224 | tf_op jit(solution)/shard_map/ppermute | solution.py:40
  31.6 5.1 %collective-permute-start.5 = (bf16[512,256]{1,0:T(8,128)(2,1)S(1)}, bf16[512,256]{1,0:T(8,128)(2,1)S(1)}, u32[]{:S(2)}, u32[]{:S(2)}) collective-permute-start(bf16[512,256]{1,0:T(8,128)(2,1)S(1)} %collective-permute-done.4.near.refs_1_), channel_id=1, source_target_pairs={{0,4},{4,0},{8,12},{12,8},{16,20},{20,16},{24,28},{28,24},{1,5},{5... | collective-permute-start | bytes 786440 | tf_op jit(solution)/shard_map/ppermute | solution.py:40
  36.7 8.8 %collective-permute-done.8.across.refs_8_ = bf16[512,128]{1,0:T(8,128)(2,1)S(1)} collective-permute-done((bf16[512,128]{1,0:T(8,128)(2,1)S(1)}, bf16[512,128]{1,0:T(8,128)(2,1)S(1)}, u32[]{:S(2)}, u32[]{:S(2)}) %collective-permute-start.8) | collective-permute-done | bytes 131104 | tf_op jit(solution)/shard_map/ppermute | solution.py:40
  45.4 2.1 %collective-permute-start.6 = (bf16[512,256]{1,0:T(8,128)(2,1)S(1)}, bf16[512,256]{1,0:T(8,128)(2,1)S(1)}, u32[]{:S(2)}, u32[]{:S(2)}) collective-permute-start(bf16[512,256]{1,0:T(8,128)(2,1)S(1)} %get-tuple-element.27), channel_id=1, source_target_pairs={{24,0},{12,4},{0,8},{20,12},{8,16},{28,20},{16,24},{4,28},{25,1},{... | collective-permute-start | bytes 786440 | tf_op jit(solution)/shard_map/ppermute | solution.py:36
  47.5 1.6 %collective-permute-start.9 = (bf16[512,128]{1,0:T(8,128)(2,1)S(1)}, bf16[512,128]{1,0:T(8,128)(2,1)S(1)}, u32[]{:S(2)}, u32[]{:S(2)}) collective-permute-start(bf16[512,128]{1,0:T(8,128)(2,1)S(1)} %get-tuple-element.28), channel_id=1, source_target_pairs={{24,0},{12,4},{0,8},{20,12},{8,16},{28,20},{16,24},{4,28},{25,1},{... | collective-permute-start | bytes 393224 | tf_op jit(solution)/shard_map/ppermute | solution.py:36
  49.1 1.8 %shard_map.73.masked_ref = f32[4,512,1024]{2,1,0:T(8,128)S(1)} custom-call(s32[4,8]{1,0:T(4,128)S(1)} %copy-done.2, bf16[4,512,1024]{2,1,0:T(8,128)(2,1)S(1)} %copy-done.1), custom_call_target="tpu_custom_call" | custom-call | flops 2097152 | bytes 12582912 | tf_op jit(solution)/shard_map/pallas_call | solution.py:384
  53.1 4.0 %collective-permute-done.9.far.refs_5_ = bf16[512,128]{1,0:T(8,128)(2,1)S(1)} collective-permute-done((bf16[512,128]{1,0:T(8,128)(2,1)S(1)}, bf16[512,128]{1,0:T(8,128)(2,1)S(1)}, u32[]{:S(2)}, u32[]{:S(2)}) %collective-permute-start.9) | collective-permute-done | bytes 131104 | tf_op jit(solution)/shard_map/ppermute | solution.py:36
  59.6 2.7 %shard_map.76.partial_ref = f32[512,640]{1,0:T(8,128)S(1)} custom-call(bf16[5,512,512]{2,1,0:T(8,128)(2,1)S(1)} %get-tuple-element.23.high_ref, bf16[5,512,512]{2,1,0:T(8,128)(2,1)S(1)} %get-tuple-element.24.low_ref, bf16[512,1024]{1,0:T(8,128)(2,1)S(1)} %get-tuple-element.25.own, bf16[512,1024]{1,0:T(8,128)(2,1)S(1)} %collective-permute-done.beside, ...), custom_call_target="tpu_custom_call" | custom-call | flops 2013265920 | bytes 5242880 | tf_op jit(solution)/shard_map/pallas_call | solution.py:391
  63.3 1.3 %shard_map.78 = f32[4,640]{1,0:T(4,128)S(1)} custom-call(bf16[5,512,512]{2,1,0:T(8,128)(2,1)S(1)} %get-tuple-element.23.high_ref, bf16[5,512,512]{2,1,0:T(8,128)(2,1)S(1)} %get-tuple-element.24.low_ref, f32[512,640]{1,0:T(8,128)S(1)} %shard_map.77.partial_ref, bf16[512,640]{1,0:T(8,128)(2,1)S(1)} %collective-permute-done.3.far.refs_3_, ...), custom_call_target="tpu_custom_call" | custom-call | flops 671088640 | bytes 3145728 | tf_op jit(solution)/shard_map/pallas_call | solution.py:398
  65.5 2.7 %collective-permute-start.12 = (f32[4,1024]{1,0:T(4,128)S(1)}, f32[4,1024]{1,0:T(4,128)S(1)}, u32[]{:S(2)}, u32[]{:S(2)}) collective-permute-start(f32[4,1024]{1,0:T(4,128)S(1)} %pad_maximum_fusion), channel_id=1, source_target_pairs={{0,12},{4,8},{8,4},{12,0},{16,28},{20,24},{24,20},{28,16},{1,13},{... | collective-permute-start | bytes 49160 | tf_op jit(solution)/shard_map/ppermute | solution.py:40
  70.1 4.6 %collective-permute-start.13 = (f32[4,1024]{1,0:T(4,128)S(1)}, f32[4,1024]{1,0:T(4,128)S(1)}, u32[]{:S(2)}, u32[]{:S(2)}) collective-permute-start(f32[4,1024]{1,0:T(4,128)S(1)} %add_add_fusion), channel_id=1, source_target_pairs={{0,16},{4,20},{8,24},{12,28},{16,0},{20,4},{24,8},{28,12},{1,17},{... | collective-permute-start | bytes 49160 | tf_op jit(solution)/shard_map/ppermute | solution.py:40
  80.8 2.4 %collective-permute-done.21.found_ref = f32[2,128,512]{2,1,0:T(8,128)S(1)} collective-permute-done((f32[2,128,512]{2,1,0:T(8,128)S(1)}, f32[2,128,512]{2,1,0:T(8,128)S(1)}, u32[]{:S(2)}, u32[]{:S(2)}) %collective-permute-start.21) | collective-permute-done | bytes 524320 | tf_op jit(solution)/shard_map/ppermute | solution.py:40
  83.7 1.6 %collective-permute-start.22 = (bf16[1,128,512]{2,1,0:T(8,128)(2,1)S(1)}, bf16[1,128,512]{2,1,0:T(8,128)(2,1)S(1)}, u32[]{:S(2)}, u32[]{:S(2)}) collective-permute-start(bf16[1,128,512]{2,1,0:T(8,128)(2,1)S(1)} %get-tuple-element.40), channel_id=1, source_target_pairs={{0,2},{1,3},{2,0},{3,1},{4,6},{5,7},{6,4},{7,5},{8,10},{9,11},{10,... | collective-permute-start | bytes 393224 | tf_op jit(solution)/shard_map/ppermute | solution.py:40
  87.1 1.6 %collective-permute-start.15 = (bf16[1,144,512]{2,1,0:T(8,128)(2,1)S(1)}, bf16[1,144,512]{2,1,0:T(8,128)(2,1)S(1)}, u32[]{:S(2)}, u32[]{:S(2)}) collective-permute-start(bf16[1,144,512]{2,1,0:T(8,128)(2,1)S(1)} %get-tuple-element.33), channel_id=1, source_target_pairs={{0,2},{1,3},{2,0},{3,1},{4,6},{5,7},{6,4},{7,5},{8,10},{9,11},{10,... | collective-permute-start | bytes 442376 | tf_op jit(solution)/shard_map/ppermute | solution.py:40
  88.7 1.4 %collective-permute-done.22 = bf16[1,128,512]{2,1,0:T(8,128)(2,1)S(1)} collective-permute-done((bf16[1,128,512]{2,1,0:T(8,128)(2,1)S(1)}, bf16[1,128,512]{2,1,0:T(8,128)(2,1)S(1)}, u32[]{:S(2)}, u32[]{:S(2)}) %collective-permute-start.22) | collective-permute-done | bytes 131104 | tf_op jit(solution)/shard_map/ppermute | solution.py:40
  90.1 2.4 %collective-permute-start.23 = (bf16[128,512]{1,0:T(8,128)(2,1)S(1)}, bf16[128,512]{1,0:T(8,128)(2,1)S(1)}, u32[]{:S(2)}, u32[]{:S(2)}) collective-permute-start(bf16[128,512]{1,0:T(8,128)(2,1)S(1)} %fusion.1), channel_id=1, source_target_pairs={{8,0},{12,4},{16,8},{20,12},{24,16},{28,20},{0,24},{4,28},{9,1},{1... | collective-permute-start | bytes 393224 | tf_op jit(solution)/shard_map/ppermute | solution.py:30
  93.3 1.6 %collective-permute-start.17 = (bf16[2,1,128,512]{3,2,1,0:T(8,128)(2,1)S(1)}, bf16[2,1,128,512]{3,2,1,0:T(8,128)(2,1)S(1)}, u32[]{:S(2)}, u32[]{:S(2)}) collective-permute-start(bf16[2,1,128,512]{3,2,1,0:T(8,128)(2,1)S(1)} %get-tuple-element.36), channel_id=1, source_target_pairs={{0,2},{1,3},{2,0},{3,1},{4,6},{5,7},{6,4},{7,5},{8,10},{9,11},{10,... | collective-permute-start | bytes 786440 | tf_op jit(solution)/shard_map/ppermute | solution.py:40
  94.9 1.6 %collective-permute-start.20 = (bf16[128,512]{1,0:T(8,128)(2,1)S(1)}, bf16[128,512]{1,0:T(8,128)(2,1)S(1)}, u32[]{:S(2)}, u32[]{:S(2)}) collective-permute-start(bf16[128,512]{1,0:T(8,128)(2,1)S(1)} %fusion), channel_id=1, source_target_pairs={{4,0},{8,4},{12,8},{16,12},{20,16},{24,20},{28,24},{0,28},{5,1},{9... | collective-permute-start | bytes 393224 | tf_op jit(solution)/shard_map/ppermute | solution.py:30
  96.5 3.4 %collective-permute-done.20.one = bf16[128,512]{1,0:T(8,128)(2,1)S(1)} collective-permute-done((bf16[128,512]{1,0:T(8,128)(2,1)S(1)}, bf16[128,512]{1,0:T(8,128)(2,1)S(1)}, u32[]{:S(2)}, u32[]{:S(2)}) %collective-permute-start.20) | collective-permute-done | bytes 131104 | tf_op jit(solution)/shard_map/ppermute | solution.py:30
  (74 shorter events, 21.3 us)
Async XLA Ops:
  1.5 46.0 %collective-permute-start = (bf16[512,1024]{1,0:T(8,128)(2,1)S(1)}, bf16[512,1024]{1,0:T(8,128)(2,1)S(1)}, u32[]{:S(2)}, u32[]{:S(2)}) collective-permute-start(bf16[512,1024]{1,0:T(8,128)(2,1)S(1)} %get-tuple-element.25.own), channel_id=1, source_target_pairs={{0,4},{4,0},{8,12},{12,8},{16,20},{20,16},{24,28},{28,24},{1,5},{5... | collective-permute-start | bytes 3145736 | tf_op jit(solution)/shard_map/ppermute | solution.py:40
  4.6 18.7 %collective-permute-start.1 = (bf16[512,640]{1,0:T(8,128)(2,1)S(1)}, bf16[512,640]{1,0:T(8,128)(2,1)S(1)}, u32[]{:S(2)}, u32[]{:S(2)}) collective-permute-start(bf16[512,640]{1,0:T(8,128)(2,1)S(1)} %get-tuple-element.26), channel_id=1, source_target_pairs={{8,0},{28,4},{16,8},{4,12},{24,16},{12,20},{0,24},{20,28},{9,1},{2... | collective-permute-start | bytes 1966088 | tf_op jit(solution)/shard_map/ppermute | solution.py:36
  8.2 23.4 %collective-permute-start.4 = (bf16[512,256]{1,0:T(8,128)(2,1)S(1)}, bf16[512,256]{1,0:T(8,128)(2,1)S(1)}, u32[]{:S(2)}, u32[]{:S(2)}) collective-permute-start(bf16[512,256]{1,0:T(8,128)(2,1)S(1)} %get-tuple-element.27), channel_id=1, source_target_pairs={{8,0},{28,4},{16,8},{4,12},{24,16},{12,20},{0,24},{20,28},{9,1},{2... | collective-permute-start | bytes 786440 | tf_op jit(solution)/shard_map/ppermute | solution.py:36
  8.6 21.7 %collective-permute-start.7 = (bf16[512,128]{1,0:T(8,128)(2,1)S(1)}, bf16[512,128]{1,0:T(8,128)(2,1)S(1)}, u32[]{:S(2)}, u32[]{:S(2)}) collective-permute-start(bf16[512,128]{1,0:T(8,128)(2,1)S(1)} %get-tuple-element.28), channel_id=1, source_target_pairs={{8,0},{28,4},{16,8},{4,12},{24,16},{12,20},{0,24},{20,28},{9,1},{2... | collective-permute-start | bytes 393224 | tf_op jit(solution)/shard_map/ppermute | solution.py:36
  23.3 39.0 %collective-permute-start.2 = (bf16[512,640]{1,0:T(8,128)(2,1)S(1)}, bf16[512,640]{1,0:T(8,128)(2,1)S(1)}, u32[]{:S(2)}, u32[]{:S(2)}) collective-permute-start(bf16[512,640]{1,0:T(8,128)(2,1)S(1)} %collective-permute-done.1.near.refs_0_), channel_id=1, source_target_pairs={{0,4},{4,0},{8,12},{12,8},{16,20},{20,16},{24,28},{28,24},{1,5},{5... | collective-permute-start | bytes 1966088 | tf_op jit(solution)/shard_map/ppermute | solution.py:40
  30.3 15.1 %collective-permute-start.8 = (bf16[512,128]{1,0:T(8,128)(2,1)S(1)}, bf16[512,128]{1,0:T(8,128)(2,1)S(1)}, u32[]{:S(2)}, u32[]{:S(2)}) collective-permute-start(bf16[512,128]{1,0:T(8,128)(2,1)S(1)} %collective-permute-done.7.near.refs_2_), channel_id=1, source_target_pairs={{0,4},{4,0},{8,12},{12,8},{16,20},{20,16},{24,28},{28,24},{1,5},{5... | collective-permute-start | bytes 393224 | tf_op jit(solution)/shard_map/ppermute | solution.py:40
  31.6 31.7 %collective-permute-start.3 = (bf16[512,640]{1,0:T(8,128)(2,1)S(1)}, bf16[512,640]{1,0:T(8,128)(2,1)S(1)}, u32[]{:S(2)}, u32[]{:S(2)}) collective-permute-start(bf16[512,640]{1,0:T(8,128)(2,1)S(1)} %get-tuple-element.26), channel_id=1, source_target_pairs={{24,0},{12,4},{0,8},{20,12},{8,16},{28,20},{16,24},{4,28},{25,1},{... | collective-permute-start | bytes 1966088 | tf_op jit(solution)/shard_map/ppermute | solution.py:36
  31.6 27.0 %collective-permute-start.5 = (bf16[512,256]{1,0:T(8,128)(2,1)S(1)}, bf16[512,256]{1,0:T(8,128)(2,1)S(1)}, u32[]{:S(2)}, u32[]{:S(2)}) collective-permute-start(bf16[512,256]{1,0:T(8,128)(2,1)S(1)} %collective-permute-done.4.near.refs_1_), channel_id=1, source_target_pairs={{0,4},{4,0},{8,12},{12,8},{16,20},{20,16},{24,28},{28,24},{1,5},{5... | collective-permute-start | bytes 786440 | tf_op jit(solution)/shard_map/ppermute | solution.py:40
  45.4 13.6 %collective-permute-start.6 = (bf16[512,256]{1,0:T(8,128)(2,1)S(1)}, bf16[512,256]{1,0:T(8,128)(2,1)S(1)}, u32[]{:S(2)}, u32[]{:S(2)}) collective-permute-start(bf16[512,256]{1,0:T(8,128)(2,1)S(1)} %get-tuple-element.27), channel_id=1, source_target_pairs={{24,0},{12,4},{0,8},{20,12},{8,16},{28,20},{16,24},{4,28},{25,1},{... | collective-permute-start | bytes 786440 | tf_op jit(solution)/shard_map/ppermute | solution.py:36
  47.5 9.6 %collective-permute-start.9 = (bf16[512,128]{1,0:T(8,128)(2,1)S(1)}, bf16[512,128]{1,0:T(8,128)(2,1)S(1)}, u32[]{:S(2)}, u32[]{:S(2)}) collective-permute-start(bf16[512,128]{1,0:T(8,128)(2,1)S(1)} %get-tuple-element.28), channel_id=1, source_target_pairs={{24,0},{12,4},{0,8},{20,12},{8,16},{28,20},{16,24},{4,28},{25,1},{... | collective-permute-start | bytes 393224 | tf_op jit(solution)/shard_map/ppermute | solution.py:36
  64.6 3.8 %collective-permute-start.10 = (f32[4,1024]{1,0:T(4,128)S(1)}, f32[4,1024]{1,0:T(4,128)S(1)}, u32[]{:S(2)}, u32[]{:S(2)}) collective-permute-start(f32[4,1024]{1,0:T(4,128)S(1)} %pad_maximum_fusion), channel_id=1, source_target_pairs={{0,4},{4,0},{8,12},{12,8},{16,20},{20,16},{24,28},{28,24},{1,5},{5... | collective-permute-start | bytes 49160 | tf_op jit(solution)/shard_map/ppermute | solution.py:40
  65.2 3.7 %collective-permute-start.11 = (f32[4,1024]{1,0:T(4,128)S(1)}, f32[4,1024]{1,0:T(4,128)S(1)}, u32[]{:S(2)}, u32[]{:S(2)}) collective-permute-start(f32[4,1024]{1,0:T(4,128)S(1)} %pad_maximum_fusion), channel_id=1, source_target_pairs={{0,8},{4,12},{8,0},{12,4},{16,24},{20,28},{24,16},{28,20},{1,9},{5... | collective-permute-start | bytes 49160 | tf_op jit(solution)/shard_map/ppermute | solution.py:40
  65.5 4.6 %collective-permute-start.12 = (f32[4,1024]{1,0:T(4,128)S(1)}, f32[4,1024]{1,0:T(4,128)S(1)}, u32[]{:S(2)}, u32[]{:S(2)}) collective-permute-start(f32[4,1024]{1,0:T(4,128)S(1)} %pad_maximum_fusion), channel_id=1, source_target_pairs={{0,12},{4,8},{8,4},{12,0},{16,28},{20,24},{24,20},{28,16},{1,13},{... | collective-permute-start | bytes 49160 | tf_op jit(solution)/shard_map/ppermute | solution.py:40
  70.1 6.3 %collective-permute-start.13 = (f32[4,1024]{1,0:T(4,128)S(1)}, f32[4,1024]{1,0:T(4,128)S(1)}, u32[]{:S(2)}, u32[]{:S(2)}) collective-permute-start(f32[4,1024]{1,0:T(4,128)S(1)} %add_add_fusion), channel_id=1, source_target_pairs={{0,16},{4,20},{8,24},{12,28},{16,0},{20,4},{24,8},{28,12},{1,17},{... | collective-permute-start | bytes 49160 | tf_op jit(solution)/shard_map/ppermute | solution.py:40
  79.7 12.8 %collective-permute-start.16 = (f32[2,2,128,512]{3,2,1,0:T(8,128)S(1)}, f32[2,2,128,512]{3,2,1,0:T(8,128)S(1)}, u32[]{:S(2)}, u32[]{:S(2)}) collective-permute-start(f32[2,2,128,512]{3,2,1,0:T(8,128)S(1)} %shard_map.90), channel_id=1, source_target_pairs={{0,1},{1,0},{2,3},{3,2},{4,5},{5,4},{6,7},{7,6},{8,9},{9,8},{10,11... | collective-permute-start | bytes 3145736 | tf_op jit(solution)/shard_map/ppermute | solution.py:40
  79.8 3.4 %collective-permute-start.21 = (f32[2,128,512]{2,1,0:T(8,128)S(1)}, f32[2,128,512]{2,1,0:T(8,128)S(1)}, u32[]{:S(2)}, u32[]{:S(2)}) collective-permute-start(f32[2,128,512]{2,1,0:T(8,128)S(1)} %get-tuple-element.31.earlier_ref), channel_id=1, source_target_pairs={{0,1},{1,0},{2,3},{3,2},{4,5},{5,4},{6,7},{7,6},{8,9},{9,8},{10,11... | collective-permute-start | bytes 1572872 | tf_op jit(solution)/shard_map/ppermute | solution.py:40
  80.3 4.9 %collective-permute-start.18 = (f32[2,128,512]{2,1,0:T(8,128)S(1)}, f32[2,128,512]{2,1,0:T(8,128)S(1)}, u32[]{:S(2)}, u32[]{:S(2)}) collective-permute-start(f32[2,128,512]{2,1,0:T(8,128)S(1)} %shard_map.87.earlier_ref), channel_id=1, source_target_pairs={{0,1},{1,0},{2,3},{3,2},{4,5},{5,4},{6,7},{7,6},{8,9},{9,8},{10,11... | collective-permute-start | bytes 1572872 | tf_op jit(solution)/shard_map/ppermute | solution.py:40
  80.4 5.9 %collective-permute-start.14 = (f32[2,128,512]{2,1,0:T(8,128)S(1)}, f32[2,128,512]{2,1,0:T(8,128)S(1)}, u32[]{:S(2)}, u32[]{:S(2)}) collective-permute-start(f32[2,128,512]{2,1,0:T(8,128)S(1)} %shard_map.88.earlier_ref), channel_id=1, source_target_pairs={{0,1},{1,0},{2,3},{3,2},{4,5},{5,4},{6,7},{7,6},{8,9},{9,8},{10,11... | collective-permute-start | bytes 1572872 | tf_op jit(solution)/shard_map/ppermute | solution.py:40
  83.7 6.4 %collective-permute-start.22 = (bf16[1,128,512]{2,1,0:T(8,128)(2,1)S(1)}, bf16[1,128,512]{2,1,0:T(8,128)(2,1)S(1)}, u32[]{:S(2)}, u32[]{:S(2)}) collective-permute-start(bf16[1,128,512]{2,1,0:T(8,128)(2,1)S(1)} %get-tuple-element.40), channel_id=1, source_target_pairs={{0,2},{1,3},{2,0},{3,1},{4,6},{5,7},{6,4},{7,5},{8,10},{9,11},{10,... | collective-permute-start | bytes 393224 | tf_op jit(solution)/shard_map/ppermute | solution.py:40
  85.7 9.2 %collective-permute-start.19 = (bf16[1,128,512]{2,1,0:T(8,128)(2,1)S(1)}, bf16[1,128,512]{2,1,0:T(8,128)(2,1)S(1)}, u32[]{:S(2)}, u32[]{:S(2)}) collective-permute-start(bf16[1,128,512]{2,1,0:T(8,128)(2,1)S(1)} %get-tuple-element.38), channel_id=1, source_target_pairs={{0,2},{1,3},{2,0},{3,1},{4,6},{5,7},{6,4},{7,5},{8,10},{9,11},{10,... | collective-permute-start | bytes 393224 | tf_op jit(solution)/shard_map/ppermute | solution.py:40
  87.1 9.4 %collective-permute-start.15 = (bf16[1,144,512]{2,1,0:T(8,128)(2,1)S(1)}, bf16[1,144,512]{2,1,0:T(8,128)(2,1)S(1)}, u32[]{:S(2)}, u32[]{:S(2)}) collective-permute-start(bf16[1,144,512]{2,1,0:T(8,128)(2,1)S(1)} %get-tuple-element.33), channel_id=1, source_target_pairs={{0,2},{1,3},{2,0},{3,1},{4,6},{5,7},{6,4},{7,5},{8,10},{9,11},{10,... | collective-permute-start | bytes 442376 | tf_op jit(solution)/shard_map/ppermute | solution.py:40
  90.1 6.4 %collective-permute-start.23 = (bf16[128,512]{1,0:T(8,128)(2,1)S(1)}, bf16[128,512]{1,0:T(8,128)(2,1)S(1)}, u32[]{:S(2)}, u32[]{:S(2)}) collective-permute-start(bf16[128,512]{1,0:T(8,128)(2,1)S(1)} %fusion.1), channel_id=1, source_target_pairs={{8,0},{12,4},{16,8},{20,12},{24,16},{28,20},{0,24},{4,28},{9,1},{1... | collective-permute-start | bytes 393224 | tf_op jit(solution)/shard_map/ppermute | solution.py:30
  93.3 7.5 %collective-permute-start.17 = (bf16[2,1,128,512]{3,2,1,0:T(8,128)(2,1)S(1)}, bf16[2,1,128,512]{3,2,1,0:T(8,128)(2,1)S(1)}, u32[]{:S(2)}, u32[]{:S(2)}) collective-permute-start(bf16[2,1,128,512]{3,2,1,0:T(8,128)(2,1)S(1)} %get-tuple-element.36), channel_id=1, source_target_pairs={{0,2},{1,3},{2,0},{3,1},{4,6},{5,7},{6,4},{7,5},{8,10},{9,11},{10,... | collective-permute-start | bytes 786440 | tf_op jit(solution)/shard_map/ppermute | solution.py:40
  94.9 5.0 %collective-permute-start.20 = (bf16[128,512]{1,0:T(8,128)(2,1)S(1)}, bf16[128,512]{1,0:T(8,128)(2,1)S(1)}, u32[]{:S(2)}, u32[]{:S(2)}) collective-permute-start(bf16[128,512]{1,0:T(8,128)(2,1)S(1)} %fusion), channel_id=1, source_target_pairs={{4,0},{8,4},{12,8},{16,12},{20,16},{24,20},{28,24},{0,28},{5,1},{9... | collective-permute-start | bytes 393224 | tf_op jit(solution)/shard_map/ppermute | solution.py:30
  (8 other events, 301.4 us)

commit v5 on v4

--- a/solution.py
+++ b/solution.py
@@ -322,24 +322,25 @@
             out_ref[step, :, cols] = keep_ref[k, step] + direct_ref[k, step].astype(F32)
 
 
-def final_kernel(share, central_ref, found_ref, keep_ref, direct_ref, one, two, out_hbm, out_ref, sems):
+def ready_kernel(share, central_ref, found_ref, keep_ref, one, two, out_hbm, rest_ref, block_ref, sem):
     size = keep_ref.shape[-1]
+    central_sum(share, 0, central_ref, found_ref, block_ref)
+    copy = pltpu.make_async_copy(block_ref, out_hbm.at[:, :, :size], sem)
+    copy.start()
+    for k, block in enumerate((one, two)):
+        rest_ref[k] = keep_ref[k, 0] + block[...].astype(F32)
+    copy.wait()
+
+
+def final_kernel(earlier_hbm, rest_ref, direct_ref, out_hbm, block_ref, sems):
+    size = rest_ref.shape[-1]
     copies = []
-
-    def release(k):
-        cols = slice(k * size, (k + 1) * size)
-        copy = pltpu.make_async_copy(out_ref.at[:, :, cols], out_hbm.at[:, :, cols], sems.at[k])
+    for k in range(REACH):
+        block_ref[k] = (rest_ref[k] + direct_ref[k, 0].astype(F32))[None]
+        cols = slice((k + 1) * size, (k + 2) * size)
+        copy = pltpu.make_async_copy(block_ref.at[k], out_hbm.at[:, :, cols], sems.at[k])
         copy.start()
         copies.append(copy)
-
-    for k, block in enumerate((one, two)):
-        cols = slice((k + 1) * size, (k + 2) * size)
-        out_ref[0, :, cols] = (
-            keep_ref[k, 0] + direct_ref[k, 0].astype(F32) + block[...].astype(F32)
-        )
-        release(k + 1)
-    central_sum(share, 0, central_ref, found_ref, out_ref)
-    release(0)
     for copy in copies:
         copy.wait()
 
@@ -510,14 +511,25 @@
         total = scatter(total, 0)[0]
         zero = jnp.zeros((share, row_count), BF16)
         return total + jnp.concatenate([zero, *mirrored], axis=1).astype(F32)
-    return call(
-        functools.partial(final_kernel, share), shape((1, share, 3 * row_count)),
-        [WHOLE] * (4 + REACH), direct_keep.size, 10 * direct_keep.size, out_specs=ANYWHERE,
-        scratch=[
-            pltpu.VMEM((1, share, 3 * row_count), F32),
-            pltpu.SemaphoreType.DMA((3,)),
+    whole = shape((1, share, 3 * row_count))
+    out, rest = call(
+        functools.partial(ready_kernel, share), [whole, shape((REACH, share, row_count))],
+        [WHOLE] * (3 + REACH), direct_keep.size, 8 * direct_keep.size,
+        out_specs=[ANYWHERE, WHOLE],
+        scratch=[pltpu.VMEM((1, share, row_count), F32), pltpu.SemaphoreType.DMA],
+    )(central_keep, central_found, direct_keep, *mirrored)
+    return pl.pallas_call(
+        final_kernel,
+        out_shape=whole,
+        in_specs=[ANYWHERE, WHOLE, WHOLE],
+        out_specs=ANYWHERE,
+        input_output_aliases={0: 0},
+        scratch_shapes=[
+            pltpu.VMEM((REACH, 1, share, row_count), F32),
+            pltpu.SemaphoreType.DMA((REACH,)),
         ],
-    )(*partial, *mirrored)[0]
+        compiler_params=PARAMS,
+    )(out, rest, found)[0]
 
 
 def solution(mesh):

time: 102 us -> 102 us (level)
  transfers between devices with their start and end apart: 24 -> 24, of which waited for: 12 -> 12; matrix products, arithmetic and copies ran while one was open for 0% -> 0% of each run, Pallas kernels for 13% -> 14%
where the time goes in v5:
time: 102 us
  waiting for transfers between devices  43.3 us (42%)
  starting transfers between devices  37.1 us (36%)
  Pallas kernels  20.6 us (20%)
    ppermute x16, starting transfers between devices, swap(): lax.ppermute(block, axis, [(i, i ^ bit) for i in range(lax.axis_size(axis...  24.9 us
    ppermute x6, waiting for transfers between devices, from_side(): return lax.ppermute(block, 'row', route)  24.3 us
    ppermute x16, waiting for transfers between devices, swap(): lax.ppermute(block, axis, [(i, i ^ bit) for i in range(lax.axis_size(axis...  15.6 us
    ppermute x6, starting transfers between devices, from_side(): return lax.ppermute(block, 'row', route)  8.16 us
    pallas_call x3, Pallas kernels, body(): call(functools.partial(early_kernel, first), total, [WHOLE] * 5, 6 * squa...  4.64 us
    ppermute x2, starting transfers between devices, from_ahead(): lax.ppermute(block, 'row', [((i + distance) % size, i) for i in range(siz...  4 us
    ppermute x2, waiting for transfers between devices, from_ahead(): lax.ppermute(block, 'row', [((i + distance) % size, i) for i in range(siz...  3.43 us
    pallas_call x3, Pallas kernels, body(): call(functools.partial(sums_kernel, first), shape((components, width)), [...  2.31 us
  transfers between devices with their start and end apart: 24, of which 12 were waited for; matrix products, arithmetic and copies ran while one was open for 0% of the time, Pallas kernels for 14%

profile of v5, /device:TPU:0, one launch (start us, length us, event | category | flops | bytes accessed | tf_op | source)
XLA Modules:
  0.0 101.8 jit_solution(4661312417704945007)
XLA Ops:
  0.0 1.5 %shard_map.75 = (bf16[512,1024]{1,0:T(8,128)(2,1)S(1)}, bf16[512,640]{1,0:T(8,128)(2,1)S(1)}, bf16[512,256]{1,0:T(8,128)(2,1)S(1)}, bf16[512,128]{1,0:T(8,128)(2,1)S(1)}) custom-call(s32[4,8]{1,0:T(4,128)} %screen_hbm.1, bf16[4,512,1024]{2,1,0:T(8,128)(2,1)} %basis_ref.3), custom_call_target="tpu_custom_call" | custom-call | flops 524288 | bytes 3145728 | tf_op jit(solution)/shard_map/pallas_call | solution.py:363
  1.5 3.1 %collective-permute-start = (bf16[512,1024]{1,0:T(8,128)(2,1)S(1)}, bf16[512,1024]{1,0:T(8,128)(2,1)S(1)}, u32[]{:S(2)}, u32[]{:S(2)}) collective-permute-start(bf16[512,1024]{1,0:T(8,128)(2,1)S(1)} %get-tuple-element.27.own), channel_id=1, source_target_pairs={{0,4},{4,0},{8,12},{12,8},{16,20},{20,16},{24,28},{28,24},{1,5},{5... | collective-permute-start | bytes 3145736 | tf_op jit(solution)/shard_map/ppermute | solution.py:40
  4.6 3.6 %collective-permute-start.1 = (bf16[512,640]{1,0:T(8,128)(2,1)S(1)}, bf16[512,640]{1,0:T(8,128)(2,1)S(1)}, u32[]{:S(2)}, u32[]{:S(2)}) collective-permute-start(bf16[512,640]{1,0:T(8,128)(2,1)S(1)} %get-tuple-element.28), channel_id=1, source_target_pairs={{8,0},{28,4},{16,8},{4,12},{24,16},{12,20},{0,24},{20,28},{9,1},{2... | collective-permute-start | bytes 1966088 | tf_op jit(solution)/shard_map/ppermute | solution.py:36
  9.1 14.2 %collective-permute-done.1.near.refs_0_ = bf16[512,640]{1,0:T(8,128)(2,1)S(1)} collective-permute-done((bf16[512,640]{1,0:T(8,128)(2,1)S(1)}, bf16[512,640]{1,0:T(8,128)(2,1)S(1)}, u32[]{:S(2)}, u32[]{:S(2)}) %collective-permute-start.1) | collective-permute-done | bytes 655392 | tf_op jit(solution)/shard_map/ppermute | solution.py:36
  24.3 6.1 %collective-permute-done.7.near.refs_2_ = bf16[512,128]{1,0:T(8,128)(2,1)S(1)} collective-permute-done((bf16[512,128]{1,0:T(8,128)(2,1)S(1)}, bf16[512,128]{1,0:T(8,128)(2,1)S(1)}, u32[]{:S(2)}, u32[]{:S(2)}) %collective-permute-start.7) | collective-permute-done | bytes 131104 | tf_op jit(solution)/shard_map/ppermute | solution.py:36
  30.3 1.2 %collective-permute-start.8 = (bf16[512,128]{1,0:T(8,128)(2,1)S(1)}, bf16[512,128]{1,0:T(8,128)(2,1)S(1)}, u32[]{:S(2)}, u32[]{:S(2)}) collective-permute-start(bf16[512,128]{1,0:T(8,128)(2,1)S(1)} %collective-permute-done.7.near.refs_2_), channel_id=1, source_target_pairs={{0,4},{4,0},{8,12},{12,8},{16,20},{20,16},{24,28},{28,24},{1,5},{5... | collective-permute-start | bytes 393224 | tf_op jit(solution)/shard_map/ppermute | solution.py:40
  31.6 5.1 %collective-permute-start.5 = (bf16[512,256]{1,0:T(8,128)(2,1)S(1)}, bf16[512,256]{1,0:T(8,128)(2,1)S(1)}, u32[]{:S(2)}, u32[]{:S(2)}) collective-permute-start(bf16[512,256]{1,0:T(8,128)(2,1)S(1)} %collective-permute-done.4.near.refs_1_), channel_id=1, source_target_pairs={{0,4},{4,0},{8,12},{12,8},{16,20},{20,16},{24,28},{28,24},{1,5},{5... | collective-permute-start | bytes 786440 | tf_op jit(solution)/shard_map/ppermute | solution.py:40
  36.7 8.8 %collective-permute-done.8.across.refs_8_ = bf16[512,128]{1,0:T(8,128)(2,1)S(1)} collective-permute-done((bf16[512,128]{1,0:T(8,128)(2,1)S(1)}, bf16[512,128]{1,0:T(8,128)(2,1)S(1)}, u32[]{:S(2)}, u32[]{:S(2)}) %collective-permute-start.8) | collective-permute-done | bytes 131104 | tf_op jit(solution)/shard_map/ppermute | solution.py:40
  45.4 2.1 %collective-permute-start.6 = (bf16[512,256]{1,0:T(8,128)(2,1)S(1)}, bf16[512,256]{1,0:T(8,128)(2,1)S(1)}, u32[]{:S(2)}, u32[]{:S(2)}) collective-permute-start(bf16[512,256]{1,0:T(8,128)(2,1)S(1)} %get-tuple-element.29), channel_id=1, source_target_pairs={{24,0},{12,4},{0,8},{20,12},{8,16},{28,20},{16,24},{4,28},{25,1},{... | collective-permute-start | bytes 786440 | tf_op jit(solution)/shard_map/ppermute | solution.py:36
  47.5 1.6 %collective-permute-start.9 = (bf16[512,128]{1,0:T(8,128)(2,1)S(1)}, bf16[512,128]{1,0:T(8,128)(2,1)S(1)}, u32[]{:S(2)}, u32[]{:S(2)}) collective-permute-start(bf16[512,128]{1,0:T(8,128)(2,1)S(1)} %get-tuple-element.30), channel_id=1, source_target_pairs={{24,0},{12,4},{0,8},{20,12},{8,16},{28,20},{16,24},{4,28},{25,1},{... | collective-permute-start | bytes 393224 | tf_op jit(solution)/shard_map/ppermute | solution.py:36
  49.1 1.8 %shard_map.73.masked_ref = f32[4,512,1024]{2,1,0:T(8,128)S(1)} custom-call(s32[4,8]{1,0:T(4,128)S(1)} %copy-done.2, bf16[4,512,1024]{2,1,0:T(8,128)(2,1)S(1)} %copy-done.1), custom_call_target="tpu_custom_call" | custom-call | flops 2097152 | bytes 12582912 | tf_op jit(solution)/shard_map/pallas_call | solution.py:385
  53.1 4.0 %collective-permute-done.9.far.refs_5_ = bf16[512,128]{1,0:T(8,128)(2,1)S(1)} collective-permute-done((bf16[512,128]{1,0:T(8,128)(2,1)S(1)}, bf16[512,128]{1,0:T(8,128)(2,1)S(1)}, u32[]{:S(2)}, u32[]{:S(2)}) %collective-permute-start.9) | collective-permute-done | bytes 131104 | tf_op jit(solution)/shard_map/ppermute | solution.py:36
  59.6 2.7 %shard_map.76.partial_ref = f32[512,640]{1,0:T(8,128)S(1)} custom-call(bf16[5,512,512]{2,1,0:T(8,128)(2,1)S(1)} %get-tuple-element.25.high_ref, bf16[5,512,512]{2,1,0:T(8,128)(2,1)S(1)} %get-tuple-element.26.low_ref, bf16[512,1024]{1,0:T(8,128)(2,1)S(1)} %get-tuple-element.27.own, bf16[512,1024]{1,0:T(8,128)(2,1)S(1)} %collective-permute-done.beside, ...), custom_call_target="tpu_custom_call" | custom-call | flops 2013265920 | bytes 5242880 | tf_op jit(solution)/shard_map/pallas_call | solution.py:392
  63.3 1.3 %shard_map.78 = f32[4,640]{1,0:T(4,128)S(1)} custom-call(bf16[5,512,512]{2,1,0:T(8,128)(2,1)S(1)} %get-tuple-element.25.high_ref, bf16[5,512,512]{2,1,0:T(8,128)(2,1)S(1)} %get-tuple-element.26.low_ref, f32[512,640]{1,0:T(8,128)S(1)} %shard_map.77.partial_ref, bf16[512,640]{1,0:T(8,128)(2,1)S(1)} %collective-permute-done.3.far.refs_3_, ...), custom_call_target="tpu_custom_call" | custom-call | flops 671088640 | bytes 3145728 | tf_op jit(solution)/shard_map/pallas_call | solution.py:399
  65.5 2.7 %collective-permute-start.12 = (f32[4,1024]{1,0:T(4,128)S(1)}, f32[4,1024]{1,0:T(4,128)S(1)}, u32[]{:S(2)}, u32[]{:S(2)}) collective-permute-start(f32[4,1024]{1,0:T(4,128)S(1)} %pad_maximum_fusion), channel_id=1, source_target_pairs={{0,12},{4,8},{8,4},{12,0},{16,28},{20,24},{24,20},{28,16},{1,13},{... | collective-permute-start | bytes 49160 | tf_op jit(solution)/shard_map/ppermute | solution.py:40
  70.1 4.6 %collective-permute-start.13 = (f32[4,1024]{1,0:T(4,128)S(1)}, f32[4,1024]{1,0:T(4,128)S(1)}, u32[]{:S(2)}, u32[]{:S(2)}) collective-permute-start(f32[4,1024]{1,0:T(4,128)S(1)} %add_add_fusion), channel_id=1, source_target_pairs={{0,16},{4,20},{8,24},{12,28},{16,0},{20,4},{24,8},{28,12},{1,17},{... | collective-permute-start | bytes 49160 | tf_op jit(solution)/shard_map/ppermute | solution.py:40
  80.8 2.4 %collective-permute-done.20.found_ref = f32[2,128,512]{2,1,0:T(8,128)S(1)} collective-permute-done((f32[2,128,512]{2,1,0:T(8,128)S(1)}, f32[2,128,512]{2,1,0:T(8,128)S(1)}, u32[]{:S(2)}, u32[]{:S(2)}) %collective-permute-start.20) | collective-permute-done | bytes 524320 | tf_op jit(solution)/shard_map/ppermute | solution.py:40
  83.7 1.6 %collective-permute-start.21 = (bf16[1,128,512]{2,1,0:T(8,128)(2,1)S(1)}, bf16[1,128,512]{2,1,0:T(8,128)(2,1)S(1)}, u32[]{:S(2)}, u32[]{:S(2)}) collective-permute-start(bf16[1,128,512]{2,1,0:T(8,128)(2,1)S(1)} %get-tuple-element.41), channel_id=1, source_target_pairs={{0,2},{1,3},{2,0},{3,1},{4,6},{5,7},{6,4},{7,5},{8,10},{9,11},{10,... | collective-permute-start | bytes 393224 | tf_op jit(solution)/shard_map/ppermute | solution.py:40
  87.1 1.6 %collective-permute-start.15 = (bf16[1,144,512]{2,1,0:T(8,128)(2,1)S(1)}, bf16[1,144,512]{2,1,0:T(8,128)(2,1)S(1)}, u32[]{:S(2)}, u32[]{:S(2)}) collective-permute-start(bf16[1,144,512]{2,1,0:T(8,128)(2,1)S(1)} %get-tuple-element.35), channel_id=1, source_target_pairs={{0,2},{1,3},{2,0},{3,1},{4,6},{5,7},{6,4},{7,5},{8,10},{9,11},{10,... | collective-permute-start | bytes 442376 | tf_op jit(solution)/shard_map/ppermute | solution.py:40
  88.7 1.4 %collective-permute-done.21 = bf16[1,128,512]{2,1,0:T(8,128)(2,1)S(1)} collective-permute-done((bf16[1,128,512]{2,1,0:T(8,128)(2,1)S(1)}, bf16[1,128,512]{2,1,0:T(8,128)(2,1)S(1)}, u32[]{:S(2)}, u32[]{:S(2)}) %collective-permute-start.21) | collective-permute-done | bytes 131104 | tf_op jit(solution)/shard_map/ppermute | solution.py:40
  90.1 2.4 %collective-permute-start.22 = (bf16[128,512]{1,0:T(8,128)(2,1)S(1)}, bf16[128,512]{1,0:T(8,128)(2,1)S(1)}, u32[]{:S(2)}, u32[]{:S(2)}) collective-permute-start(bf16[128,512]{1,0:T(8,128)(2,1)S(1)} %fusion.1), channel_id=1, source_target_pairs={{8,0},{12,4},{16,8},{20,12},{24,16},{28,20},{0,24},{4,28},{9,1},{1... | collective-permute-start | bytes 393224 | tf_op jit(solution)/shard_map/ppermute | solution.py:30
  93.3 1.6 %collective-permute-start.23 = (bf16[2,1,128,512]{3,2,1,0:T(8,128)(2,1)S(1)}, bf16[2,1,128,512]{3,2,1,0:T(8,128)(2,1)S(1)}, u32[]{:S(2)}, u32[]{:S(2)}) collective-permute-start(bf16[2,1,128,512]{3,2,1,0:T(8,128)(2,1)S(1)} %get-tuple-element.44), channel_id=1, source_target_pairs={{0,2},{1,3},{2,0},{3,1},{4,6},{5,7},{6,4},{7,5},{8,10},{9,11},{10,... | collective-permute-start | bytes 786440 | tf_op jit(solution)/shard_map/ppermute | solution.py:40
  94.9 1.6 %collective-permute-start.19 = (bf16[128,512]{1,0:T(8,128)(2,1)S(1)}, bf16[128,512]{1,0:T(8,128)(2,1)S(1)}, u32[]{:S(2)}, u32[]{:S(2)}) collective-permute-start(bf16[128,512]{1,0:T(8,128)(2,1)S(1)} %fusion), channel_id=1, source_target_pairs={{4,0},{8,4},{12,8},{16,12},{20,16},{24,20},{28,24},{0,28},{5,1},{9... | collective-permute-start | bytes 393224 | tf_op jit(solution)/shard_map/ppermute | solution.py:30
  96.5 3.4 %collective-permute-done.19.one = bf16[128,512]{1,0:T(8,128)(2,1)S(1)} collective-permute-done((bf16[128,512]{1,0:T(8,128)(2,1)S(1)}, bf16[128,512]{1,0:T(8,128)(2,1)S(1)}, u32[]{:S(2)}, u32[]{:S(2)}) %collective-permute-start.19) | collective-permute-done | bytes 131104 | tf_op jit(solution)/shard_map/ppermute | solution.py:30
  (75 shorter events, 21.1 us)
Async XLA Ops:
  1.5 46.0 %collective-permute-start = (bf16[512,1024]{1,0:T(8,128)(2,1)S(1)}, bf16[512,1024]{1,0:T(8,128)(2,1)S(1)}, u32[]{:S(2)}, u32[]{:S(2)}) collective-permute-start(bf16[512,1024]{1,0:T(8,128)(2,1)S(1)} %get-tuple-element.27.own), channel_id=1, source_target_pairs={{0,4},{4,0},{8,12},{12,8},{16,20},{20,16},{24,28},{28,24},{1,5},{5... | collective-permute-start | bytes 3145736 | tf_op jit(solution)/shard_map/ppermute | solution.py:40
  4.6 18.7 %collective-permute-start.1 = (bf16[512,640]{1,0:T(8,128)(2,1)S(1)}, bf16[512,640]{1,0:T(8,128)(2,1)S(1)}, u32[]{:S(2)}, u32[]{:S(2)}) collective-permute-start(bf16[512,640]{1,0:T(8,128)(2,1)S(1)} %get-tuple-element.28), channel_id=1, source_target_pairs={{8,0},{28,4},{16,8},{4,12},{24,16},{12,20},{0,24},{20,28},{9,1},{2... | collective-permute-start | bytes 1966088 | tf_op jit(solution)/shard_map/ppermute | solution.py:36
  8.2 23.4 %collective-permute-start.4 = (bf16[512,256]{1,0:T(8,128)(2,1)S(1)}, bf16[512,256]{1,0:T(8,128)(2,1)S(1)}, u32[]{:S(2)}, u32[]{:S(2)}) collective-permute-start(bf16[512,256]{1,0:T(8,128)(2,1)S(1)} %get-tuple-element.29), channel_id=1, source_target_pairs={{8,0},{28,4},{16,8},{4,12},{24,16},{12,20},{0,24},{20,28},{9,1},{2... | collective-permute-start | bytes 786440 | tf_op jit(solution)/shard_map/ppermute | solution.py:36
  8.6 21.7 %collective-permute-start.7 = (bf16[512,128]{1,0:T(8,128)(2,1)S(1)}, bf16[512,128]{1,0:T(8,128)(2,1)S(1)}, u32[]{:S(2)}, u32[]{:S(2)}) collective-permute-start(bf16[512,128]{1,0:T(8,128)(2,1)S(1)} %get-tuple-element.30), channel_id=1, source_target_pairs={{8,0},{28,4},{16,8},{4,12},{24,16},{12,20},{0,24},{20,28},{9,1},{2... | collective-permute-start | bytes 393224 | tf_op jit(solution)/shard_map/ppermute | solution.py:36
  23.3 39.0 %collective-permute-start.2 = (bf16[512,640]{1,0:T(8,128)(2,1)S(1)}, bf16[512,640]{1,0:T(8,128)(2,1)S(1)}, u32[]{:S(2)}, u32[]{:S(2)}) collective-permute-start(bf16[512,640]{1,0:T(8,128)(2,1)S(1)} %collective-permute-done.1.near.refs_0_), channel_id=1, source_target_pairs={{0,4},{4,0},{8,12},{12,8},{16,20},{20,16},{24,28},{28,24},{1,5},{5... | collective-permute-start | bytes 1966088 | tf_op jit(solution)/shard_map/ppermute | solution.py:40
  30.3 15.1 %collective-permute-start.8 = (bf16[512,128]{1,0:T(8,128)(2,1)S(1)}, bf16[512,128]{1,0:T(8,128)(2,1)S(1)}, u32[]{:S(2)}, u32[]{:S(2)}) collective-permute-start(bf16[512,128]{1,0:T(8,128)(2,1)S(1)} %collective-permute-done.7.near.refs_2_), channel_id=1, source_target_pairs={{0,4},{4,0},{8,12},{12,8},{16,20},{20,16},{24,28},{28,24},{1,5},{5... | collective-permute-start | bytes 393224 | tf_op jit(solution)/shard_map/ppermute | solution.py:40
  31.6 31.7 %collective-permute-start.3 = (bf16[512,640]{1,0:T(8,128)(2,1)S(1)}, bf16[512,640]{1,0:T(8,128)(2,1)S(1)}, u32[]{:S(2)}, u32[]{:S(2)}) collective-permute-start(bf16[512,640]{1,0:T(8,128)(2,1)S(1)} %get-tuple-element.28), channel_id=1, source_target_pairs={{24,0},{12,4},{0,8},{20,12},{8,16},{28,20},{16,24},{4,28},{25,1},{... | collective-permute-start | bytes 1966088 | tf_op jit(solution)/shard_map/ppermute | solution.py:36
  31.6 27.0 %collective-permute-start.5 = (bf16[512,256]{1,0:T(8,128)(2,1)S(1)}, bf16[512,256]{1,0:T(8,128)(2,1)S(1)}, u32[]{:S(2)}, u32[]{:S(2)}) collective-permute-start(bf16[512,256]{1,0:T(8,128)(2,1)S(1)} %collective-permute-done.4.near.refs_1_), channel_id=1, source_target_pairs={{0,4},{4,0},{8,12},{12,8},{16,20},{20,16},{24,28},{28,24},{1,5},{5... | collective-permute-start | bytes 786440 | tf_op jit(solution)/shard_map/ppermute | solution.py:40
  45.4 13.6 %collective-permute-start.6 = (bf16[512,256]{1,0:T(8,128)(2,1)S(1)}, bf16[512,256]{1,0:T(8,128)(2,1)S(1)}, u32[]{:S(2)}, u32[]{:S(2)}) collective-permute-start(bf16[512,256]{1,0:T(8,128)(2,1)S(1)} %get-tuple-element.29), channel_id=1, source_target_pairs={{24,0},{12,4},{0,8},{20,12},{8,16},{28,20},{16,24},{4,28},{25,1},{... | collective-permute-start | bytes 786440 | tf_op jit(solution)/shard_map/ppermute | solution.py:36
  47.5 9.6 %collective-permute-start.9 = (bf16[512,128]{1,0:T(8,128)(2,1)S(1)}, bf16[512,128]{1,0:T(8,128)(2,1)S(1)}, u32[]{:S(2)}, u32[]{:S(2)}) collective-permute-start(bf16[512,128]{1,0:T(8,128)(2,1)S(1)} %get-tuple-element.30), channel_id=1, source_target_pairs={{24,0},{12,4},{0,8},{20,12},{8,16},{28,20},{16,24},{4,28},{25,1},{... | collective-permute-start | bytes 393224 | tf_op jit(solution)/shard_map/ppermute | solution.py:36
  64.6 3.8 %collective-permute-start.10 = (f32[4,1024]{1,0:T(4,128)S(1)}, f32[4,1024]{1,0:T(4,128)S(1)}, u32[]{:S(2)}, u32[]{:S(2)}) collective-permute-start(f32[4,1024]{1,0:T(4,128)S(1)} %pad_maximum_fusion), channel_id=1, source_target_pairs={{0,4},{4,0},{8,12},{12,8},{16,20},{20,16},{24,28},{28,24},{1,5},{5... | collective-permute-start | bytes 49160 | tf_op jit(solution)/shard_map/ppermute | solution.py:40
  65.2 3.7 %collective-permute-start.11 = (f32[4,1024]{1,0:T(4,128)S(1)}, f32[4,1024]{1,0:T(4,128)S(1)}, u32[]{:S(2)}, u32[]{:S(2)}) collective-permute-start(f32[4,1024]{1,0:T(4,128)S(1)} %pad_maximum_fusion), channel_id=1, source_target_pairs={{0,8},{4,12},{8,0},{12,4},{16,24},{20,28},{24,16},{28,20},{1,9},{5... | collective-permute-start | bytes 49160 | tf_op jit(solution)/shard_map/ppermute | solution.py:40
  65.5 4.6 %collective-permute-start.12 = (f32[4,1024]{1,0:T(4,128)S(1)}, f32[4,1024]{1,0:T(4,128)S(1)}, u32[]{:S(2)}, u32[]{:S(2)}) collective-permute-start(f32[4,1024]{1,0:T(4,128)S(1)} %pad_maximum_fusion), channel_id=1, source_target_pairs={{0,12},{4,8},{8,4},{12,0},{16,28},{20,24},{24,20},{28,16},{1,13},{... | collective-permute-start | bytes 49160 | tf_op jit(solution)/shard_map/ppermute | solution.py:40
  70.1 6.3 %collective-permute-start.13 = (f32[4,1024]{1,0:T(4,128)S(1)}, f32[4,1024]{1,0:T(4,128)S(1)}, u32[]{:S(2)}, u32[]{:S(2)}) collective-permute-start(f32[4,1024]{1,0:T(4,128)S(1)} %add_add_fusion), channel_id=1, source_target_pairs={{0,16},{4,20},{8,24},{12,28},{16,0},{20,4},{24,8},{28,12},{1,17},{... | collective-permute-start | bytes 49160 | tf_op jit(solution)/shard_map/ppermute | solution.py:40
  79.7 12.8 %collective-permute-start.16 = (f32[2,2,128,512]{3,2,1,0:T(8,128)S(1)}, f32[2,2,128,512]{3,2,1,0:T(8,128)S(1)}, u32[]{:S(2)}, u32[]{:S(2)}) collective-permute-start(f32[2,2,128,512]{3,2,1,0:T(8,128)S(1)} %shard_map.90), channel_id=1, source_target_pairs={{0,1},{1,0},{2,3},{3,2},{4,5},{5,4},{6,7},{7,6},{8,9},{9,8},{10,11... | collective-permute-start | bytes 3145736 | tf_op jit(solution)/shard_map/ppermute | solution.py:40
  79.8 3.4 %collective-permute-start.20 = (f32[2,128,512]{2,1,0:T(8,128)S(1)}, f32[2,128,512]{2,1,0:T(8,128)S(1)}, u32[]{:S(2)}, u32[]{:S(2)}) collective-permute-start(f32[2,128,512]{2,1,0:T(8,128)S(1)} %get-tuple-element.33.earlier_ref), channel_id=1, source_target_pairs={{0,1},{1,0},{2,3},{3,2},{4,5},{5,4},{6,7},{7,6},{8,9},{9,8},{10,11... | collective-permute-start | bytes 1572872 | tf_op jit(solution)/shard_map/ppermute | solution.py:40
  80.3 4.9 %collective-permute-start.17 = (f32[2,128,512]{2,1,0:T(8,128)S(1)}, f32[2,128,512]{2,1,0:T(8,128)S(1)}, u32[]{:S(2)}, u32[]{:S(2)}) collective-permute-start(f32[2,128,512]{2,1,0:T(8,128)S(1)} %shard_map.87.earlier_ref), channel_id=1, source_target_pairs={{0,1},{1,0},{2,3},{3,2},{4,5},{5,4},{6,7},{7,6},{8,9},{9,8},{10,11... | collective-permute-start | bytes 1572872 | tf_op jit(solution)/shard_map/ppermute | solution.py:40
  80.4 5.9 %collective-permute-start.14 = (f32[2,128,512]{2,1,0:T(8,128)S(1)}, f32[2,128,512]{2,1,0:T(8,128)S(1)}, u32[]{:S(2)}, u32[]{:S(2)}) collective-permute-start(f32[2,128,512]{2,1,0:T(8,128)S(1)} %shard_map.88.earlier_ref), channel_id=1, source_target_pairs={{0,1},{1,0},{2,3},{3,2},{4,5},{5,4},{6,7},{7,6},{8,9},{9,8},{10,11... | collective-permute-start | bytes 1572872 | tf_op jit(solution)/shard_map/ppermute | solution.py:40
  83.7 6.4 %collective-permute-start.21 = (bf16[1,128,512]{2,1,0:T(8,128)(2,1)S(1)}, bf16[1,128,512]{2,1,0:T(8,128)(2,1)S(1)}, u32[]{:S(2)}, u32[]{:S(2)}) collective-permute-start(bf16[1,128,512]{2,1,0:T(8,128)(2,1)S(1)} %get-tuple-element.41), channel_id=1, source_target_pairs={{0,2},{1,3},{2,0},{3,1},{4,6},{5,7},{6,4},{7,5},{8,10},{9,11},{10,... | collective-permute-start | bytes 393224 | tf_op jit(solution)/shard_map/ppermute | solution.py:40
  85.7 9.2 %collective-permute-start.18 = (bf16[1,128,512]{2,1,0:T(8,128)(2,1)S(1)}, bf16[1,128,512]{2,1,0:T(8,128)(2,1)S(1)}, u32[]{:S(2)}, u32[]{:S(2)}) collective-permute-start(bf16[1,128,512]{2,1,0:T(8,128)(2,1)S(1)} %get-tuple-element.39), channel_id=1, source_target_pairs={{0,2},{1,3},{2,0},{3,1},{4,6},{5,7},{6,4},{7,5},{8,10},{9,11},{10,... | collective-permute-start | bytes 393224 | tf_op jit(solution)/shard_map/ppermute | solution.py:40
  87.1 9.4 %collective-permute-start.15 = (bf16[1,144,512]{2,1,0:T(8,128)(2,1)S(1)}, bf16[1,144,512]{2,1,0:T(8,128)(2,1)S(1)}, u32[]{:S(2)}, u32[]{:S(2)}) collective-permute-start(bf16[1,144,512]{2,1,0:T(8,128)(2,1)S(1)} %get-tuple-element.35), channel_id=1, source_target_pairs={{0,2},{1,3},{2,0},{3,1},{4,6},{5,7},{6,4},{7,5},{8,10},{9,11},{10,... | collective-permute-start | bytes 442376 | tf_op jit(solution)/shard_map/ppermute | solution.py:40
  90.1 6.4 %collective-permute-start.22 = (bf16[128,512]{1,0:T(8,128)(2,1)S(1)}, bf16[128,512]{1,0:T(8,128)(2,1)S(1)}, u32[]{:S(2)}, u32[]{:S(2)}) collective-permute-start(bf16[128,512]{1,0:T(8,128)(2,1)S(1)} %fusion.1), channel_id=1, source_target_pairs={{8,0},{12,4},{16,8},{20,12},{24,16},{28,20},{0,24},{4,28},{9,1},{1... | collective-permute-start | bytes 393224 | tf_op jit(solution)/shard_map/ppermute | solution.py:30
  93.3 7.5 %collective-permute-start.23 = (bf16[2,1,128,512]{3,2,1,0:T(8,128)(2,1)S(1)}, bf16[2,1,128,512]{3,2,1,0:T(8,128)(2,1)S(1)}, u32[]{:S(2)}, u32[]{:S(2)}) collective-permute-start(bf16[2,1,128,512]{3,2,1,0:T(8,128)(2,1)S(1)} %get-tuple-element.44), channel_id=1, source_target_pairs={{0,2},{1,3},{2,0},{3,1},{4,6},{5,7},{6,4},{7,5},{8,10},{9,11},{10,... | collective-permute-start | bytes 786440 | tf_op jit(solution)/shard_map/ppermute | solution.py:40
  94.9 5.0 %collective-permute-start.19 = (bf16[128,512]{1,0:T(8,128)(2,1)S(1)}, bf16[128,512]{1,0:T(8,128)(2,1)S(1)}, u32[]{:S(2)}, u32[]{:S(2)}) collective-permute-start(bf16[128,512]{1,0:T(8,128)(2,1)S(1)} %fusion), channel_id=1, source_target_pairs={{4,0},{8,4},{12,8},{16,12},{20,16},{24,20},{28,24},{0,28},{5,1},{9... | collective-permute-start | bytes 393224 | tf_op jit(solution)/shard_map/ppermute | solution.py:30
  (8 other events, 301.4 us)
